TPU v7x, 32 devices: a whole 2x2x4 slice. The times are simulated.
32 devices in a mesh: grp: 4 (over y, core), dev: 8 (over z, x).
Axes of the slice: x: 2, y: 2, z: 4, core: 2. Of those that a mesh axis runs over, the one named last changes fastest.
Arguments:
- coords: float32 [3, 32768], P(None, ('grp', 'dev')), may hold values from 0 to 6
- counts: int32 [256], P(('grp', 'dev')), may hold values from 64 to 128
- neighbours: int32 [8, 256], P(None, ('grp', 'dev')), may hold values from 0 to 255, as said below
- proxies: float32 [3, 32768], P(None, ('grp', 'dev')), may hold values from -1 to 7
- leaf_transfers: float32 [256, 128, 128], P(('grp', 'dev')), may hold values from -0.375 to 0.375
- node_transfers: float32 [256, 128, 128], P(('grp', 'dev')), may hold values from -0.375 to 0.375
Outputs:
- near_tiles: bfloat16 [256, 8, 128, 128], P(('grp', 'dev'))
- leaf_bases: bfloat16 [32768, 128], P(('grp', 'dev'))
- leaf_factors: float32 [256, 128, 128], P(('grp', 'dev'))
- node_factors: float32 [256, 128, 128], P(('grp', 'dev'))
Inputs may be any that keep to these rules, and one draw needn't show every extreme that they name: `neighbours`: row 0 of column l is l itself; every entry of column l differs from l by at most 8.
All inputs are finite; a program needn't handle non-finite values.
Results may differ from a plain program's by a relative error of at most 0.001.
Values sent between devices are 32-bit elements; how exact they have to be, the bound alone decides.
No kernel may reach another device: no remote copies, remote signals or barrier semaphores. Data moves between devices by JAX's collectives and lax.ppermute only.
A program may use at most 64 MiB of HBM per device.

v0:
```python
import jax
import jax.numpy as jnp
from jax import lax
from jax.sharding import PartitionSpec as P

ridge = 0.1
length_scale = 0.3


def extended(block, sides, width):
    for axis, dim in sides:
        count = lax.axis_size(axis)
        forward = [(i, i + 1) for i in range(count - 1)]
        backward = [(target, source) for source, target in forward]
        low = lax.ppermute(
            lax.slice_in_dim(block, block.shape[dim] - width, None, axis=dim), axis, forward
        )
        high = lax.ppermute(lax.slice_in_dim(block, 0, width, axis=dim), axis, backward)
        block = jnp.concatenate([low, block, high], axis=dim)
    return block


def from_partner(value, axis, distance):
    return lax.ppermute(value, axis, [(i, i ^ 1 << distance) for i in range(lax.axis_size(axis))])


def matern(delta_x, delta_y, delta_z):
    distance = jnp.sqrt(delta_x * delta_x + delta_y * delta_y + delta_z * delta_z)
    scaled = 3.0**0.5 / length_scale * distance
    return (1.0 + scaled) * jnp.exp(-scaled)


def lift(transfer, heads):
    inner = jnp.einsum("lba,lbc->lac", transfer, heads, precision=lax.Precision.HIGHEST)
    return jnp.einsum("lac,lcd->lad", inner, transfer, precision=lax.Precision.HIGHEST)


def factor(heads):
    return jnp.swapaxes(jnp.linalg.cholesky(heads), -1, -2)


def climb(weight, transfers, identity):
    count = weight.shape[0]
    levels = count.bit_length() - 1
    heads_list = []
    for level in range(1, levels + 1):
        heads = weight[0::2] + weight[1::2] + identity
        heads_list.append(heads)
        weight = lift(transfers[2 ** (level - 1) :: 2**level], heads)
    return (heads_list, weight)


def trailing(value, count):
    total = jnp.zeros((), jnp.int32)
    for bit in range(1, count + 1):
        total = total + (value % (1 << bit) == 0).astype(jnp.int32)
    return total


def shards(coords, counts, neighbours, proxies, leaf_transfers, node_transfers):
    leaves = counts.shape[0]
    slots = coords.shape[1] // leaves
    width = leaf_transfers.shape[1]
    identity = ridge * jnp.eye(width, dtype=jnp.float32)
    n_grp = lax.axis_size("grp")
    n_dev = lax.axis_size("dev")
    grp_index = lax.axis_index("grp")
    dev_index = lax.axis_index("dev")
    position = grp_index * n_dev + dev_index
    valid = (jnp.arange(slots, dtype=jnp.int32)[None, :] < counts[:, None]).astype(jnp.float32)
    sites = coords.reshape(3, leaves, slots)
    points = proxies.reshape(3, leaves, width)
    delta = sites[:, :, :, None] - points[:, :, None, :]
    basis = matern(delta[0], delta[1], delta[2]) * valid[:, :, None]
    gram = (
        jnp.einsum("lik,lij->lkj", basis, basis, precision=lax.Precision.HIGHEST) / slots + identity
    )
    lower = jnp.linalg.cholesky(gram)
    leaf_factors = jnp.swapaxes(lower, -1, -2)
    solved = jax.scipy.linalg.solve_triangular(lower, jnp.swapaxes(basis, -1, -2), lower=True)
    leaf_bases = jnp.swapaxes(solved, -1, -2).reshape(leaves * slots, width).astype(jnp.bfloat16)
    stacked = jnp.concatenate([coords, valid.reshape(1, leaves * slots)], axis=0)
    widened = extended(stacked, ((("grp", "dev"), 1),), leaves * slots)
    widened = widened.reshape(4, 3 * leaves, slots)
    local_ids = neighbours - (position * leaves - leaves)
    gathered = jnp.take(widened, local_ids, axis=1)
    gathered = jnp.transpose(gathered, (2, 0, 1, 3))
    own_sites = jnp.transpose(sites, (1, 0, 2))

    def tiles_of(items):
        own, own_valid, other = items
        diff = own[:, None, :, None] - other[:3, :, None, :]
        values = matern(diff[0], diff[1], diff[2]) * own_valid[None, :, None] * other[3][:, None, :]
        return values.astype(jnp.bfloat16)

    near_tiles = lax.map(tiles_of, (own_sites, valid, gathered))
    node_factors = jnp.zeros((leaves, width, width), jnp.float32)
    weight = lift(leaf_transfers, gram)
    heads_list, weight = climb(weight, node_transfers, identity)
    for level, heads in enumerate(heads_list, 1):
        node_factors = node_factors.at[2 ** (level - 1) :: 2**level].set(factor(heads))
    own_weight = weight[0]
    own_transfer = node_transfers[0]
    total_levels = (n_grp * n_dev).bit_length() - 1
    tz_all = trailing(position, total_levels - 1)
    chosen = jnp.zeros((width, width), jnp.float32)
    current = own_weight
    first_transfer = own_transfer
    for level in range(total_levels):
        other_weight, other_transfer = from_partner(
            (current, first_transfer), ("grp", "dev"), level
        )
        upper = position // (1 << level) % 2 == 1
        lower_weight = jnp.where(upper, other_weight, current)
        upper_weight = jnp.where(upper, current, other_weight)
        heads = lower_weight + upper_weight + identity
        chosen = jnp.where(tz_all == level, heads, chosen)
        owner_transfer = jnp.where(upper, first_transfer, other_transfer)
        first_transfer = jnp.where(upper, other_transfer, first_transfer)
        if level + 1 < total_levels:
            current = lift(owner_transfer[None], heads[None])[0]
    top_factor = factor(chosen[None])[0]
    node_factors = node_factors.at[0].set(top_factor)
    return (near_tiles, leaf_bases, leaf_factors, node_factors)


def solution(mesh):
    in_specs = (
        P(None, ("grp", "dev")),
        P(("grp", "dev")),
        P(None, ("grp", "dev")),
        P(None, ("grp", "dev")),
        P(("grp", "dev"), None, None),
        P(("grp", "dev"), None, None),
    )
    out_specs = (
        P(("grp", "dev"), None, None, None),
        P(("grp", "dev"), None),
        P(("grp", "dev"), None, None),
        P(("grp", "dev"), None, None),
    )
    return jax.shard_map(shards, mesh=mesh, in_specs=in_specs, out_specs=out_specs, check_vma=False)
```

profile of v0, /device:TPU:1, one launch (start us, length us, event | category | flops | bytes accessed | tf_op | source)
XLA Modules:
  0.0 342.6 jit_solution(10057943742977468209)
XLA Ops:
  1.4 1.3 pad_maximum_fusion
  2.8 7.5 %collective-permute-start.1 = (f32[4,1024]{1,0:T(4,128)}, f32[4,1024]{1,0:T(4,128)}, u32[]{:S(2)}, u32[]{:S(2)}) collective-permute-start(f32[4,1024]{1,0:T(4,128)} %pad_maximum_fusion), channel_id=1, source_target_pairs={{1,0},{2,1},{3,2},{4,3},{5,4},{6,5},{7,6},{8,7},{9,8},{10,9},{11,1... | collective-permute-start | bytes 49160 | tf_op jit(solution)/shard_map/ppermute | solution.py:18
  10.3 1.9 collective-permute-start
  15.6 1.8 broadcast_add_fusion
  22.6 1.4 collective-permute-start.6
  26.9 1.6 copy.117
  28.5 1.3 and_bitcast_fusion
  30.5 1.9 fusion.12
  32.4 94.6 %custom-call.19 = f32[8,128,128]{2,1,0:T(8,128)S(1)} custom-call(f32[8,128,128]{2,1,0:T(8,128)} %fusion.12), custom_call_target="Cholesky" | custom-call | tf_op jit(solution)/shard_map/jit(cholesky)/cholesky | solution.py:78
  128.2 79.4 %custom-call.20 = f32[8,1,128,128]{2,3,1,0:T(8,128)S(1)} custom-call(f32[8,1,128,128]{3,2,1,0:T(8,128)} %get-tuple-element.92), custom_call_target="InvertDiagBlocksLowerTriangular" | custom-call | tf_op jit(solution)/shard_map/jit(_solve_triangular)/vmap()/triangular_solve | solution.py:80
  207.7 1.4 convolution_convert_fusion
  209.1 46.9 %custom-call.21 = f32[4,128,128]{2,1,0:T(8,128)S(1)} custom-call(f32[4,128,128]{2,1,0:T(8,128)S(1)} %fusion.14), custom_call_target="Cholesky" | custom-call | tf_op jit(solution)/shard_map/jit(cholesky)/cholesky | solution.py:39
  257.2 23.7 %custom-call.22 = f32[2,128,128]{2,1,0:T(8,128)S(1)} custom-call(f32[2,128,128]{2,1,0:T(8,128)S(1)} %fusion.19), custom_call_target="Cholesky" | custom-call | tf_op jit(solution)/shard_map/jit(cholesky)/cholesky | solution.py:39
  281.2 11.7 %custom-call.24 = f32[1,128,128]{2,1,0:T(8,128)S(1)} custom-call(f32[1,128,128]{2,1,0:T(8,128)S(1)} %fusion.32), custom_call_target="Cholesky" | custom-call | tf_op jit(solution)/shard_map/jit(cholesky)/cholesky | solution.py:39
  298.5 1.2 fusion.44
  299.7 1.1 fusion.43
  300.8 1.5 collective-permute-start.7
  302.3 2.5 collective-permute-start.4
  305.4 3.0 collective-permute-start.8
  308.5 2.4 collective-permute-start.5
  311.6 2.4 collective-permute-start.9
  316.5 11.0 %while.12 = (s32[]{:T(128)}, bf16[8,8,128,128]{3,2,1,0:T(8,128)(2,1)}, f32[8,3,128]{2,1,0:T(4,128)S(1)}, f32[8,4,8,128]{3,0,2,1:T(8,128)S(1)}, f32[8,128]{1,0:T(8,128)S(1)}, /*index=5*/s32[]{:T(128)}) while((s32[]{:T(128)}, bf16[8,8,128,128]{3,2,1,0:T(8,128)(2,1)}, f32[8,3,128]{2,1,0:T(4,128)S(1)}, f32[8,4,8,128]{3,0,2,1:T(8,128)S(1)}, ...), condition=%wide.region_1.2_spmd, body=%wide.region_0.1_spmd.sunk | while | flops 1966082 | bytes 3496029 | solution.py:96
  318.2 1.1 fusion.77
  328.6 11.7 %custom-call.25 = f32[1,128,128]{2,1,0:T(8,128)S(1)} custom-call(f32[1,128,128]{2,1,0:T(8,128)S(1)} %fusion.26), custom_call_target="Cholesky" | custom-call | tf_op jit(solution)/shard_map/jit(cholesky)/cholesky | solution.py:39
  (176 shorter events, 37.4 us)
Async XLA Ops:
  0.6 16.7 %copy-start = (f32[8,128,128]{2,1,0:T(8,128)S(1)}, f32[8,128,128]{2,1,0:T(8,128)}, u32[]{:S(2)}) copy-start(f32[8,128,128]{2,1,0:T(8,128)} %param.17) | copy-start | bytes 1572868
  1.4 14.1 %copy-start.9 = (f32[8,128]{1,0:T(8,128)}, f32[8,128]{1,0:T(8,128)S(1)}, u32[]{:S(2)}) copy-start(f32[8,128]{1,0:T(8,128)S(1)} %fusion.45) | copy-start | bytes 12292
  2.8 294.2 %collective-permute-start.1 = (f32[4,1024]{1,0:T(4,128)}, f32[4,1024]{1,0:T(4,128)}, u32[]{:S(2)}, u32[]{:S(2)}) collective-permute-start(f32[4,1024]{1,0:T(4,128)} %pad_maximum_fusion), channel_id=1, source_target_pairs={{1,0},{2,1},{3,2},{4,3},{5,4},{6,5},{7,6},{8,7},{9,8},{10,9},{11,1... | collective-permute-start | bytes 49160 | tf_op jit(solution)/shard_map/ppermute | solution.py:18
  10.3 286.6 %collective-permute-start = (f32[4,1024]{1,0:T(4,128)}, f32[4,1024]{1,0:T(4,128)}, u32[]{:S(2)}, u32[]{:S(2)}) collective-permute-start(f32[4,1024]{1,0:T(4,128)} %pad_maximum_fusion), channel_id=1, source_target_pairs={{0,1},{1,2},{2,3},{3,4},{4,5},{5,6},{6,7},{7,8},{8,9},{9,10},{10,1... | collective-permute-start | bytes 49160 | tf_op jit(solution)/shard_map/ppermute | solution.py:15
  13.2 285.2 %collective-permute-start.2 = (f32[128,128]{0,1:T(8,128)S(1)}, f32[128,128]{0,1:T(8,128)}, u32[]{:S(2)}, u32[]{:S(2)}) collective-permute-start(f32[128,128]{0,1:T(8,128)S(1)} %bitcast.117), channel_id=1, source_target_pairs={{0,1},{1,0},{2,3},{3,2},{4,5},{5,4},{6,7},{7,6},{8,9},{9,8},{10,11... | collective-permute-start | bytes 196616 | tf_op jit(solution)/shard_map/ppermute | solution.py:24
  21.5 2.6 copy-start.3
  22.6 275.9 %collective-permute-start.6 = (f32[128,128]{0,1:T(8,128)}, f32[128,128]{0,1:T(8,128)}, u32[]{:S(2)}, u32[]{:S(2)}) collective-permute-start(f32[128,128]{0,1:T(8,128)} %fusion.27), channel_id=1, source_target_pairs={{0,1},{1,0},{2,3},{3,2},{4,5},{5,4},{6,7},{7,6},{8,9},{9,8},{10,11... | collective-permute-start | bytes 196616 | tf_op jit(solution)/shard_map/ppermute | solution.py:24
  26.9 100.1 %copy-start.11 = (pred[128,128]{0,1:T(8,128)(4,1)S(1)}, pred[128,128]{0,1:T(8,128)(4,1)}, u32[]{:S(2)}) copy-start(pred[128,128]{0,1:T(8,128)(4,1)} %iota_compare_fusion.4) | copy-start | bytes 49156
  207.6 49.5 %copy-start.4 = (f32[2,128,128]{2,1,0:T(8,128)S(1)}, f32[2,128,128]{2,1,0:T(8,128)}, u32[]{:S(2)}) copy-start(f32[2,128,128]{2,1,0:T(8,128)} %copy.112) | copy-start | bytes 393220
  209.0 71.8 %copy-start.6 = (pred[128,128]{1,0:T(8,128)(4,1)S(1)}, pred[128,128]{1,0:T(8,128)(4,1)}, u32[]{:S(2)}) copy-start(pred[128,128]{1,0:T(8,128)(4,1)} %copy-done.5) | copy-start | bytes 49156
  209.1 72.1 %copy-start.7 = (f32[1,128,128]{2,1,0:T(8,128)S(1)}, f32[1,128,128]{2,1,0:T(8,128)}, u32[]{:S(2)}) copy-start(f32[1,128,128]{2,1,0:T(8,128)} %copy.117) | copy-start | bytes 196612
  257.0 37.5 %copy-start.15 = (s32[4]{0:T(128)S(1)}, s32[4]{0:T(128)}, u32[]{:S(2)}) copy-start(s32[4]{0:T(128)} %add_bitcast_fusion.1) | copy-start | bytes 52
  257.1 38.0 %copy-start.14 = (s32[2]{0:T(128)S(1)}, s32[2]{0:T(128)}, u32[]{:S(2)}) copy-start(s32[2]{0:T(128)} %add_bitcast_fusion) | copy-start | bytes 28
  257.2 38.6 %copy-start.13 = (s32[64]{0:T(128)S(1)}, s32[64]{0:T(128)}, u32[]{:S(2)}) copy-start(s32[64]{0:T(128)} %reshape.309) | copy-start | bytes 772
  294.4 2.6 copy-start.8
  294.4 2.6 copy-start.10
  296.9 17.1 %copy-start.12 = (pred[8,8]{0,1:T(8,128)(4,1)S(1)}, pred[8,8]{0,1:T(8,128)(4,1)}, u32[]{:S(2)}) copy-start(pred[8,8]{0,1:T(8,128)(4,1)} %get-tuple-element.89) | copy-start | bytes 196
  298.4 3.9 %collective-permute-start.3 = (f32[128,128]{0,1:T(8,128)S(1)}, f32[128,128]{0,1:T(8,128)S(1)}, u32[]{:S(2)}, u32[]{:S(2)}) collective-permute-start(f32[128,128]{0,1:T(8,128)S(1)} %broadcast_select_fusion.1), channel_id=1, source_target_pairs={{0,2},{1,3},{2,0},{3,1},{4,6},{5,7},{6,4},{7,5},{8,10},{9,11},{10,... | collective-permute-start | bytes 196616 | tf_op jit(solution)/shard_map/ppermute | solution.py:24
  300.8 4.1 %collective-permute-start.7 = (f32[128,128]{0,1:T(8,128)S(1)}, f32[128,128]{0,1:T(8,128)S(1)}, u32[]{:S(2)}, u32[]{:S(2)}) collective-permute-start(f32[128,128]{0,1:T(8,128)S(1)} %fusion.43), channel_id=1, source_target_pairs={{0,2},{1,3},{2,0},{3,1},{4,6},{5,7},{6,4},{7,5},{8,10},{9,11},{10,... | collective-permute-start | bytes 196616 | tf_op jit(solution)/shard_map/ppermute | solution.py:24
  302.3 6.1 %collective-permute-start.4 = (f32[128,128]{0,1:T(8,128)S(1)}, f32[128,128]{0,1:T(8,128)S(1)}, u32[]{:S(2)}, u32[]{:S(2)}) collective-permute-start(f32[128,128]{0,1:T(8,128)S(1)} %broadcast_select_fusion.3), channel_id=1, source_target_pairs={{0,4},{1,5},{2,6},{3,7},{4,0},{5,1},{6,2},{7,3},{8,12},{9,13},{10,... | collective-permute-start | bytes 196616 | tf_op jit(solution)/shard_map/ppermute | solution.py:24
  305.4 5.7 %collective-permute-start.8 = (f32[128,128]{0,1:T(8,128)S(1)}, f32[128,128]{0,1:T(8,128)S(1)}, u32[]{:S(2)}, u32[]{:S(2)}) collective-permute-start(f32[128,128]{0,1:T(8,128)S(1)} %fusion.41), channel_id=1, source_target_pairs={{0,4},{1,5},{2,6},{3,7},{4,0},{5,1},{6,2},{7,3},{8,12},{9,13},{10,... | collective-permute-start | bytes 196616 | tf_op jit(solution)/shard_map/ppermute | solution.py:24
  308.5 5.7 %collective-permute-start.5 = (f32[128,128]{0,1:T(8,128)S(1)}, f32[128,128]{0,1:T(8,128)S(1)}, u32[]{:S(2)}, u32[]{:S(2)}) collective-permute-start(f32[128,128]{0,1:T(8,128)S(1)} %broadcast_select_fusion.5), channel_id=1, source_target_pairs={{0,8},{1,9},{2,10},{3,11},{4,12},{5,13},{6,14},{7,15},{8,0},{9,1},... | collective-permute-start | bytes 196616 | tf_op jit(solution)/shard_map/ppermute | solution.py:24
  311.6 3.3 collective-permute-start.9
  315.5 12.1 %collective-permute-start.10 = (f32[128,128]{0,1:T(8,128)S(1)}, f32[128,128]{0,1:T(8,128)S(1)}, u32[]{:S(2)}, u32[]{:S(2)}) collective-permute-start(f32[128,128]{0,1:T(8,128)S(1)} %fusion.37), channel_id=1, source_target_pairs={{0,16},{1,17},{2,18},{3,19},{4,20},{5,21},{6,22},{7,23},{8,24},{9,... | collective-permute-start | bytes 196616 | tf_op jit(solution)/shard_map/ppermute | solution.py:24
  (3 other events, 3.0 us)
where the time goes:
time: 344 us; the launch traced here: 343 us
  other arithmetic  293 us (85%)
  starting transfers between devices  24 us (7%)
  matrix products  12.2 us (4%)
  local copies, waits for them, and re-layouts  10.6 us (3%)
    another operation x12, other arithmetic, factor(): return jnp.swapaxes(jnp.linalg.cholesky(heads), -1, -2)  96.4 us
    another operation x4, other arithmetic, shards(): lower = jnp.linalg.cholesky(gram)  95.3 us
    another operation x2, other arithmetic, shards(): jax.scipy.linalg.solve_triangular(lower, jnp.swapaxes(basis, -1, -2), low...  79.4 us
    ppermute x9, starting transfers between devices, from_partner(): lax.ppermute(value, axis, [(i, i ^ 1 << distance) for i in range(lax.axis...  14.6 us
    dynamic_update_slice x8, other arithmetic, shards(): near_tiles = lax.map(tiles_of, (own_sites, valid, gathered))  8.64 us
    ppermute x1, starting transfers between devices, extended(): lax.ppermute(lax.slice_in_dim(block, 0, width, axis=dim), axis, backward)  7.54 us
  transfers between devices with their start and end apart: 11, of which 2 were waited for; matrix products, arithmetic and copies ran while one was open for 87% of the time, Pallas kernels for 0%

commit v1 on v0

v1 whole, which is shorter than its diff:
```python
import functools
import math

import jax
import jax.numpy as jnp
from jax import lax
from jax.experimental import pallas as pl
from jax.experimental.pallas import tpu as pltpu
from jax.sharding import PartitionSpec as P

ridge = 0.1
length_scale = 0.3
far = 1.0e6
f32 = jnp.float32
bf16 = jnp.bfloat16
BLOCK = 32
STEP = 4
params = pltpu.CompilerParams(vmem_limit_bytes=48 * 1024 * 1024)


def dot(left, right, left_dim, right_dim):
    return lax.dot_general(
        left,
        right,
        (((left_dim,), (right_dim,)), ((), ())),
        precision=lax.Precision.HIGHEST,
        preferred_element_type=f32,
    )


def matern(delta_x, delta_y, delta_z):
    scale = 3.0**0.5 / length_scale * math.log2(math.e)
    square = delta_x * delta_x + delta_y * delta_y + delta_z * delta_z
    square = jnp.maximum(square * (scale * scale), 1e-30)
    u = square * lax.rsqrt(square)
    return (1.0 + u * math.log(2.0)) * jnp.exp2(-u)


def lane_copies(vreg, lane):
    return jnp.broadcast_to(vreg[:, lane : lane + 1], vreg.shape)


def row_copies(vreg, row):
    return jnp.broadcast_to(vreg[row : row + 1, :], vreg.shape)


def eliminate(block, extra, base, step):
    batch = len(block)
    groups = len(block[0])
    count = 8 * groups
    rows = [[None] * count for _ in range(batch)]
    extra_rows = [[None] * count for _ in range(batch)]
    for j in range(0, count, step):
        g, s = divmod(j, 8)
        for b in range(batch):
            own = block[b]
            cols = [[lane_copies(own[q], base + j + k) for k in range(step)] for q in range(g, groups)]
            width = 2 if extra else 1
            rho = [
                [row_copies(side[b][g], s + k) for k in range(step)]
                for side in ((block, extra) if extra else (block,))
            ]
            pivot = [[row_copies(cols[0][k], s + i) for k in range(i + 1)] for i in range(step)]
            low = [[None] * step for _ in range(step)]
            inv = [None] * step
            made = [[None] * step for _ in range(width)]
            for i in range(step):
                for k in range(i):
                    t = pivot[i][k]
                    for m in range(k):
                        t = t - low[i][m] * low[k][m]
                    low[i][k] = t * inv[k]
                t = pivot[i][i]
                for m in range(i):
                    t = t - low[i][m] * low[i][m]
                inv[i] = lax.rsqrt(t)
                for side in range(width):
                    u = rho[side][i]
                    for m in range(i):
                        u = u - low[i][m] * made[side][m]
                    made[side][i] = u * inv[i]
            for k in range(step):
                rows[b][j + k] = made[0][k]
                if extra:
                    extra_rows[b][j + k] = made[1][k]
            if j + step == count:
                continue
            for side in range(width):
                back = [None] * step
                for i in reversed(range(step)):
                    t = made[side][i]
                    for m in range(i + 1, step):
                        t = t - low[m][i] * back[m]
                    back[i] = t * inv[i]
                target = (block, extra)[side][b]
                for q in range(g, groups):
                    if q == g and s + step >= 8:
                        continue
                    t = target[q]
                    for k in range(step):
                        t = t - cols[q - g][k] * back[k]
                    target[q] = t
    return rows, extra_rows


def gather_rows(rows, row_id):
    value = rows[0]
    for i in range(1, 8):
        value = jnp.where(row_id == i, rows[i], value)
    return value


def factor_block(load, store, batch, k, extra):
    row_id = lax.broadcasted_iota(jnp.int32, (8, 128), 0)
    lane_id = lax.broadcasted_iota(jnp.int32, (8, 128), 1)
    block = []
    for b in range(batch):
        value = load(b)
        block.append([value[8 * q : 8 * q + 8, :] for q in range(BLOCK // 8)])
    start = []
    if extra:
        unit = [jnp.where(lane_id == row_id + 8 * q, 1.0, 0.0).astype(f32) for q in range(BLOCK // 8)]
        start = [list(unit) for _ in range(batch)]
    rows, extra_rows = eliminate(block, start, k * BLOCK, STEP)
    inverses = []
    for b in range(batch):
        pieces = []
        for q in range(BLOCK // 8):
            at = k * BLOCK + 8 * q
            value = gather_rows(rows[b][8 * q : 8 * q + 8], row_id)
            store(b, at, jnp.where(lane_id >= row_id + at, value, 0.0))
            if extra:
                pieces.append(gather_rows(extra_rows[b][8 * q : 8 * q + 8], row_id))
        if extra:
            inverses.append(jnp.concatenate(pieces, axis=0)[:, :BLOCK])
    return inverses


def panel(matrix, factor_ref, slot, k):
    at = k * BLOCK
    value = matrix[at : at + BLOCK, :]
    if k:
        done = factor_ref[slot, 0:at, :]
        value = value - dot(done[:, at : at + BLOCK], done, 0, 0)
    return value


def local_kernel(counts, coords, proxies, leaf_t, node_t, basis_ref, gram_ref, heads_ref, weight_ref):
    leaves = basis_ref.shape[0]
    eye = jnp.where(
        lax.broadcasted_iota(jnp.int32, (128, 128), 0) == lax.broadcasted_iota(jnp.int32, (128, 128), 1),
        ridge,
        0.0,
    ).astype(f32)
    lane_id = lax.broadcasted_iota(jnp.int32, (1, 128), 1)
    weights = []
    for leaf in range(leaves):
        span = slice(leaf * 128, leaf * 128 + 128)
        own = jnp.concatenate(
            [
                jnp.where(lane_id < counts[leaf], coords[0:1, span], far),
                coords[1:3, span],
                jnp.zeros((5, 128), f32),
            ],
            axis=0,
        )
        own = own.T
        basis = matern(
            own[:, 0:1] - proxies[0:1, span],
            own[:, 1:2] - proxies[1:2, span],
            own[:, 2:3] - proxies[2:3, span],
        )
        basis_ref[leaf] = basis
        gram = dot(basis, basis, 0, 0) * (1.0 / 128) + eye
        gram_ref[leaf] = gram
        move = leaf_t[leaf]
        weights.append(dot(move, dot(gram, move, 1, 0), 0, 0))
    at = 0
    level = 1
    while len(weights) > 1:
        following = []
        for k in range(len(weights) // 2):
            head = weights[2 * k] + weights[2 * k + 1] + eye
            heads_ref[at] = head
            at += 1
            move = node_t[k * 2**level + 2 ** (level - 1)]
            following.append(dot(move, dot(head, move, 1, 0), 0, 0))
        weights = following
        level += 1
    weight_ref[...] = weights[0]


def lift_kernel(low_ref, high_ref, move_ref, head_ref, weight_ref):
    eye = jnp.where(
        lax.broadcasted_iota(jnp.int32, (128, 128), 0) == lax.broadcasted_iota(jnp.int32, (128, 128), 1),
        ridge,
        0.0,
    ).astype(f32)
    head = low_ref[...] + high_ref[...] + eye
    head_ref[...] = head
    move = move_ref[...]
    weight_ref[...] = dot(move, dot(head, move, 1, 0), 0, 0)


def near_kernel(ids, counts, own_ref, low_ref, high_ref, out_ref, wide):
    leaves = counts.shape[0]
    span = own_ref.shape[1]
    fan = ids.shape[0]
    wide[:, 0:span] = low_ref[...]
    wide[:, span : 2 * span] = own_ref[...]
    wide[:, 2 * span : 3 * span] = high_ref[...]
    lane_id = lax.broadcasted_iota(jnp.int32, (1, 128), 1)

    def leaf_step(leaf, carry):
        start = pl.multiple_of(leaf * 128, 128)
        own = own_ref[:, pl.ds(start, 128)]
        own = jnp.concatenate(
            [jnp.where(lane_id < counts[leaf], own[0:1], far), own[1:3], jnp.zeros((5, 128), f32)], axis=0
        )
        own = own.T
        own_x = jnp.broadcast_to(own[:, 0:1], (128, 128))
        own_y = jnp.broadcast_to(own[:, 1:2], (128, 128))
        own_z = jnp.broadcast_to(own[:, 2:3], (128, 128))
        for n in range(fan):
            at = pl.multiple_of(ids[n, leaf] * 128, 128)
            other = wide[:, pl.ds(at, 128)]
            tile = matern(own_x - other[0:1], own_y - other[1:2], own_z - other[2:3])
            out_ref[leaf, n] = tile.astype(bf16)
        return carry

    lax.fori_loop(0, leaves, leaf_step, 0)


def leaf_kernel(basis_ref, gram_ref, factor_ref, bases_ref, x_ref):
    batch = gram_ref.shape[0]

    def store(b, at, value):
        factor_ref[b, at : at + 8, :] = value

    for k in range(128 // BLOCK):
        at = k * BLOCK
        inverses = factor_block(lambda b: panel(gram_ref[b], factor_ref, b, k), store, batch, k, True)
        for b in range(batch):
            value = basis_ref[b, :, at : at + BLOCK]
            if k:
                value = value - dot(x_ref[b, :, 0:at], factor_ref[b, 0:at, at : at + BLOCK], 1, 0)
            x_ref[b, :, at : at + BLOCK] = dot(value, inverses[b], 1, 1)
    for b in range(batch):
        bases_ref[b * 128 : b * 128 + 128, :] = x_ref[b].astype(bf16)


def node_kernel(heads_ref, top_ref, factor_ref):
    inner = heads_ref.shape[0]
    batch = inner + 1
    slots = []
    level = 1
    while 2**level <= batch:
        slots += [k * 2**level + 2 ** (level - 1) for k in range(batch // 2**level)]
        level += 1
    slots.append(0)

    def matrix(b):
        return heads_ref[b] if b < inner else top_ref[...]

    def store(b, at, value):
        factor_ref[slots[b], at : at + 8, :] = value

    for k in range(128 // BLOCK):
        factor_block(lambda b: panel(matrix(b), factor_ref, slots[b], k), store, batch, k, False)


def partner(value, distance):
    count = lax.axis_size("grp") * lax.axis_size("dev")
    return lax.ppermute(value, ("grp", "dev"), [(i, i ^ 1 << distance) for i in range(count)])


def trailing(value, count):
    total = jnp.zeros((), jnp.int32)
    for bit in range(1, count + 1):
        total = total + (value % (1 << bit) == 0).astype(jnp.int32)
    return total


vmem = pl.BlockSpec(memory_space=pltpu.VMEM)
smem = pl.BlockSpec(memory_space=pltpu.SMEM)


def shards(coords, counts, neighbours, proxies, leaf_transfers, node_transfers):
    leaves = counts.shape[0]
    slots = coords.shape[1] // leaves
    width = leaf_transfers.shape[1]
    fan = neighbours.shape[0]
    count = lax.axis_size("grp") * lax.axis_size("dev")
    position = lax.axis_index("grp") * lax.axis_size("dev") + lax.axis_index("dev")
    mat = jax.ShapeDtypeStruct((width, width), f32)
    mats = jax.ShapeDtypeStruct((leaves, width, width), f32)

    valid = jnp.arange(slots, dtype=jnp.int32)[None, :] < counts[:, None]
    keep = valid.reshape(1, leaves * slots) | (jnp.arange(3, dtype=jnp.int32)[:, None] > 0)
    masked = jnp.where(keep, coords, -far)
    up = [(i, i + 1) for i in range(count - 1)]
    down = [(target, source) for source, target in up]
    low = lax.ppermute(masked, ("grp", "dev"), up)
    high = lax.ppermute(masked, ("grp", "dev"), down)

    total_levels = count.bit_length() - 1
    owners = []
    first = node_transfers[0]
    for level in range(total_levels - 1):
        other = partner(first, level)
        upper = position // (1 << level) % 2 == 1
        owners.append(jnp.where(upper, first, other))
        first = jnp.where(upper, other, first)

    basis, gram, heads, weight = pl.pallas_call(
        local_kernel,
        out_shape=(mats, mats, jax.ShapeDtypeStruct((leaves - 1, width, width), f32), mat),
        in_specs=[smem, vmem, vmem, vmem, vmem],
        out_specs=(vmem, vmem, vmem, vmem),
        compiler_params=params,
        name="local",
    )(counts, coords, proxies, leaf_transfers, node_transfers)

    lift = pl.pallas_call(
        lift_kernel,
        out_shape=(mat, mat),
        in_specs=[vmem, vmem, vmem],
        out_specs=(vmem, vmem),
        compiler_params=params,
        name="lift",
    )
    identity = ridge * jnp.eye(width, dtype=f32)
    tz_all = trailing(position, total_levels - 1)
    chosen = jnp.zeros((width, width), f32)
    for level in range(total_levels):
        other = partner(weight, level)
        if level + 1 < total_levels:
            head, following = lift(weight, other, owners[level])
        else:
            head = weight + other + identity
        chosen = jnp.where(tz_all == level, head, chosen)
        weight = following

    near_tiles = pl.pallas_call(
        near_kernel,
        out_shape=jax.ShapeDtypeStruct((leaves, fan, slots, slots), bf16),
        in_specs=[smem, smem, vmem, vmem, vmem],
        out_specs=vmem,
        scratch_shapes=[pltpu.VMEM((3, 3 * leaves * slots), f32)],
        compiler_params=params,
        name="near",
    )(neighbours - (position * leaves - leaves), counts, masked, low, high)

    leaf_factors, leaf_bases = pl.pallas_call(
        leaf_kernel,
        out_shape=(mats, jax.ShapeDtypeStruct((leaves * slots, width), bf16)),
        in_specs=[vmem, vmem],
        out_specs=(vmem, vmem),
        scratch_shapes=[pltpu.VMEM((leaves, slots, width), f32)],
        compiler_params=params,
        name="leaf",
    )(basis, gram)

    node_factors = pl.pallas_call(
        node_kernel,
        out_shape=mats,
        in_specs=[vmem, vmem],
        out_specs=vmem,
        compiler_params=params,
        name="node",
    )(heads, chosen)
    return (near_tiles, leaf_bases, leaf_factors, node_factors)


def solution(mesh):
    both = ("grp", "dev")
    in_specs = (
        P(None, both),
        P(both),
        P(None, both),
        P(None, both),
        P(both, None, None),
        P(both, None, None),
    )
    out_specs = (
        P(both, None, None, None),
        P(both, None),
        P(both, None, None),
        P(both, None, None),
    )
    return jax.shard_map(shards, mesh=mesh, in_specs=in_specs, out_specs=out_specs, check_vma=False)
```

time: 344 us -> 74.6 us (0.22)
  other arithmetic: 293 us -> 1.07 us
  Pallas kernels: 0 us -> 41.6 us
  matrix products: 12.2 us -> 0 us
  local copies, waits for them, and re-layouts: 10.6 us -> 5.04 us
    another operation x19 -> x0, other arithmetic: 272 us -> none  [the longest x12 96.4 us: factor(): return jnp.swapaxes(jnp.linalg.cholesky(heads), -1, -2)]
    pallas_call x0 -> x8, Pallas kernels: none -> 41.6 us  [the longest x1 17.8 us: shards(): pl.pallas_call(leaf_kernel, out_shape=(mats, jax.ShapeDtypeStruct((leaves...]
    dot_general x17 -> x0, matrix products: 10.8 us -> none  [the longest x8 4.82 us: lift(): jnp.einsum('lac,lcd->lad', inner, transfer, precision=lax.Precision.HIGHEST)]
    dynamic_update_slice x8 -> x0, other arithmetic: 8.64 us -> none  [shards(): near_tiles = lax.map(tiles_of, (own_sites, valid, gathered))]
  transfers between devices with their start and end apart: 11 -> 11, of which waited for: 2 -> 2; matrix products, arithmetic and copies ran while one was open for 87% -> 1% of each run, Pallas kernels for 0% -> 42%
where the time goes in v1:
time: 74.6 us; the launch traced here: 73.6 us
  Pallas kernels  41.6 us (56%)
  starting transfers between devices  23.2 us (31%)
  local copies, waits for them, and re-layouts  5.04 us (7%)
  waiting for transfers between devices  1.8 us (2%)
  other arithmetic  1.07 us (1%)
  between operations  0.84 us (1%)
    pallas_call x1, Pallas kernels, shards(): pl.pallas_call(leaf_kernel, out_shape=(mats, jax.ShapeDtypeStruct((leaves...  17.8 us
    ppermute x9, starting transfers between devices, partner(): lax.ppermute(value, ('grp', 'dev'), [(i, i ^ 1 << distance) for i in rang...  15.8 us
    pallas_call x1, Pallas kernels, shards(): pl.pallas_call(node_kernel, out_shape=mats, in_specs=[vmem, vmem], out_sp...  10.6 us
    pallas_call x1, Pallas kernels, shards(): pl.pallas_call(local_kernel, out_shape=(mats, mats, jax.ShapeDtypeStruct(...  5.87 us
    pallas_call x1, Pallas kernels, shards(): pl.pallas_call(near_kernel, out_shape=jax.ShapeDtypeStruct((leaves, fan,...  5.49 us
    ppermute x1, starting transfers between devices, shards(): high = lax.ppermute(masked, ('grp', 'dev'), down)  5.33 us
    unnamed x16, local copies, waits for them, and re-layouts  4.18 us
    ppermute x1, starting transfers between devices, shards(): low = lax.ppermute(masked, ('grp', 'dev'), up)  2.1 us
  transfers between devices with their start and end apart: 11, of which 2 were waited for; matrix products, arithmetic and copies ran while one was open for 1% of the time, Pallas kernels for 42%

profile of v1, /device:TPU:1, one launch (start us, length us, event | category | flops | bytes accessed | tf_op | source)
XLA Modules:
  0.0 73.6 jit_solution(8996364586678447568)
XLA Ops:
  0.7 0.9 %slice_bitcast_fusion = f32[128,128]{1,0:T(8,128)S(1)} fusion(f32[8,128,128]{2,1,0:T(8,128)} %node_t.1), kind=kLoop, calls=%fused_computation.2 | loop fusion | bytes 131072 | tf_op jit(solution)/shard_map/squeeze | solution.py:308
  1.5 2.0 %collective-permute-start.3 = (f32[128,128]{1,0:T(8,128)S(1)}, f32[128,128]{1,0:T(8,128)S(1)}, u32[]{:S(2)}, u32[]{:S(2)}) collective-permute-start(f32[128,128]{1,0:T(8,128)S(1)} %slice_bitcast_fusion), channel_id=1, source_target_pairs={{0,1},{1,0},{2,3},{3,2},{4,5},{5,4},{6,7},{7,6},{8,9},{9,8},{10,11... | collective-permute-start | bytes 196616 | tf_op jit(solution)/shard_map/ppermute | solution.py:274
  3.6 1.0 %copy-done = f32[8,128,128]{2,1,0:T(8,128)S(1)} copy-done((f32[8,128,128]{2,1,0:T(8,128)S(1)}, f32[8,128,128]{2,1,0:T(8,128)}, u32[]{:S(2)}) %copy-start) | copy-done | bytes 524312
  4.6 1.0 %copy-done.1 = f32[8,128,128]{2,1,0:T(8,128)S(1)} copy-done((f32[8,128,128]{2,1,0:T(8,128)S(1)}, f32[8,128,128]{2,1,0:T(8,128)}, u32[]{:S(2)}) %copy-start.1) | copy-done | bytes 524312
  5.6 0.7 copy-done.2
  6.4 0.7 copy-done.4
  7.1 0.7 copy-done.5
  7.7 5.9 %local.1 = (f32[8,128,128]{2,1,0:T(8,128)S(1)}, f32[8,128,128]{2,1,0:T(8,128)S(1)}, f32[7,128,128]{2,1,0:T(8,128)S(1)}, f32[128,128]{1,0:T(8,128)S(1)}) custom-call(s32[8]{0:T(128)S(1)} %copy-done.5, f32[3,1024]{1,0:T(4,128)S(1)} %copy-done.2, f32[3,1024]{1,0:T(4,128)S(1)} %copy-done.4, f32[8,128,128]{2,1,0:T(8,128)S(1)} %copy-done.1, f32[8,128,128]{2,1,0:T(8,128)S(1)} %copy-done), custom_call_target="tpu_custom_call" | custom-call | tf_op jit(solution)/shard_map/local/pallas_call | solution.py:315
  13.7 0.9 %broadcast_select_fusion.5 = (f32[128,128]{1,0:T(8,128)S(1)}, f32[128,128]{1,0:T(8,128)S(1)}) fusion(f32[128,128]{1,0:T(8,128)S(1)} %collective-permute-done.3, pred[]{:T(512)S(6)} %eq.56, f32[8,128,128]{2,1,0:T(8,128)} %node_t.1), kind=kLoop, calls=%fused_computation.8 | loop fusion | flops 32768 | bytes 262145 | tf_op jit(solution)/shard_map/jit(_where)/select_n | solution.py:313
  14.6 1.6 %collective-permute-start.5 = (f32[128,128]{1,0:T(8,128)S(1)}, f32[128,128]{1,0:T(8,128)S(1)}, u32[]{:S(2)}, u32[]{:S(2)}) collective-permute-start(f32[128,128]{1,0:T(8,128)S(1)} %get-tuple-element.32), channel_id=1, source_target_pairs={{0,2},{1,3},{2,0},{3,1},{4,6},{5,7},{6,4},{7,5},{8,10},{9,11},{10,... | collective-permute-start | bytes 196616 | tf_op jit(solution)/shard_map/ppermute | solution.py:274
  16.2 0.6 collective-permute-done.2.high_ref
  17.2 1.4 %collective-permute-start.4 = (f32[128,128]{1,0:T(8,128)S(1)}, f32[128,128]{1,0:T(8,128)S(1)}, u32[]{:S(2)}, u32[]{:S(2)}) collective-permute-start(f32[128,128]{1,0:T(8,128)S(1)} %get-tuple-element.24.low_ref), channel_id=1, source_target_pairs={{0,2},{1,3},{2,0},{3,1},{4,6},{5,7},{6,4},{7,5},{8,10},{9,11},{10,... | collective-permute-start | bytes 196616 | tf_op jit(solution)/shard_map/ppermute | solution.py:274
  18.6 2.4 %collective-permute-start.7 = (f32[128,128]{1,0:T(8,128)S(1)}, f32[128,128]{1,0:T(8,128)S(1)}, u32[]{:S(2)}, u32[]{:S(2)}) collective-permute-start(f32[128,128]{1,0:T(8,128)S(1)} %get-tuple-element.36), channel_id=1, source_target_pairs={{0,4},{1,5},{2,6},{3,7},{4,0},{5,1},{6,2},{7,3},{8,12},{9,13},{10,... | collective-permute-start | bytes 196616 | tf_op jit(solution)/shard_map/ppermute | solution.py:274
  21.0 0.5 lift.5
  21.5 1.8 %collective-permute-start.6 = (f32[128,128]{1,0:T(8,128)S(1)}, f32[128,128]{1,0:T(8,128)S(1)}, u32[]{:S(2)}, u32[]{:S(2)}) collective-permute-start(f32[128,128]{1,0:T(8,128)S(1)} %get-tuple-element.25.low_ref), channel_id=1, source_target_pairs={{0,4},{1,5},{2,6},{3,7},{4,0},{5,1},{6,2},{7,3},{8,12},{9,13},{10,... | collective-permute-start | bytes 196616 | tf_op jit(solution)/shard_map/ppermute | solution.py:274
  23.3 5.1 %collective-permute-start.9 = (f32[128,128]{1,0:T(8,128)S(1)}, f32[128,128]{1,0:T(8,128)S(1)}, u32[]{:S(2)}, u32[]{:S(2)}) collective-permute-start(f32[128,128]{1,0:T(8,128)S(1)} %get-tuple-element.34), channel_id=1, source_target_pairs={{0,8},{1,9},{2,10},{3,11},{4,12},{5,13},{6,14},{7,15},{8,0},{9,1},... | collective-permute-start | bytes 196616 | tf_op jit(solution)/shard_map/ppermute | solution.py:274
  28.5 5.3 %collective-permute-start.1 = (f32[3,1024]{1,0:T(4,128)S(1)}, f32[3,1024]{1,0:T(4,128)S(1)}, u32[]{:S(2)}, u32[]{:S(2)}) collective-permute-start(f32[3,1024]{1,0:T(4,128)S(1)} %or_select_fusion.own_ref), channel_id=1, source_target_pairs={{1,0},{2,1},{3,2},{4,3},{5,4},{6,5},{7,6},{8,7},{9,8},{10,9},{11,1... | collective-permute-start | bytes 36872 | tf_op jit(solution)/shard_map/ppermute | solution.py:304
  33.8 2.1 %collective-permute-start = (f32[3,1024]{1,0:T(4,128)S(1)}, f32[3,1024]{1,0:T(4,128)S(1)}, u32[]{:S(2)}, u32[]{:S(2)}) collective-permute-start(f32[3,1024]{1,0:T(4,128)S(1)} %or_select_fusion.own_ref), channel_id=1, source_target_pairs={{0,1},{1,2},{2,3},{3,4},{4,5},{5,6},{6,7},{7,8},{8,9},{9,10},{10,1... | collective-permute-start | bytes 36872 | tf_op jit(solution)/shard_map/ppermute | solution.py:303
  36.0 0.5 lift.6
  36.6 1.2 %collective-permute-done.8.high_ref = f32[128,128]{1,0:T(8,128)S(1)} collective-permute-done((f32[128,128]{1,0:T(8,128)S(1)}, f32[128,128]{1,0:T(8,128)S(1)}, u32[]{:S(2)}, u32[]{:S(2)}) %collective-permute-start.8) | collective-permute-done | bytes 65568 | tf_op jit(solution)/shard_map/ppermute | solution.py:274
  38.2 1.4 %collective-permute-start.10 = (f32[128,128]{1,0:T(8,128)S(1)}, f32[128,128]{1,0:T(8,128)S(1)}, u32[]{:S(2)}, u32[]{:S(2)}) collective-permute-start(f32[128,128]{1,0:T(8,128)S(1)} %get-tuple-element.27), channel_id=1, source_target_pairs={{0,16},{1,17},{2,18},{3,19},{4,20},{5,21},{6,22},{7,23},{8,24},{9,... | collective-permute-start | bytes 196616 | tf_op jit(solution)/shard_map/ppermute | solution.py:274
  39.6 17.8 %leaf.1 = (f32[8,128,128]{2,1,0:T(8,128)}, bf16[1024,128]{1,0:T(8,128)(2,1)}) custom-call(f32[8,128,128]{2,1,0:T(8,128)S(1)} %get-tuple-element.18.basis_ref, f32[8,128,128]{2,1,0:T(8,128)S(1)} %get-tuple-element.19.gram_ref), custom_call_target="tpu_custom_call" | custom-call | tf_op jit(solution)/shard_map/leaf/pallas_call | solution.py:354
  57.5 5.5 %near.1 = bf16[8,8,128,128]{3,2,1,0:T(8,128)(2,1)} custom-call(s32[8,8]{1,0:T(8,128)S(1)} %broadcast_subtract_fusion.ids, s32[8]{0:T(128)S(1)} %copy-done.6, f32[3,1024]{1,0:T(4,128)S(1)} %or_select_fusion.own_ref, f32[3,1024]{1,0:T(4,128)S(1)} %collective-permute-done.low_ref, f32[3,1024]{1,0:T(4,128)S(1)} %collective-permute-done.1.high_ref), custom_call_target="tpu_custom_call" | custom-call | tf_op jit(solution)/shard_map/near/pallas_call | solution.py:344
  63.0 10.6 %node.1 = f32[8,128,128]{2,1,0:T(8,128)} custom-call(f32[7,128,128]{2,1,0:T(8,128)S(1)} %get-tuple-element.22.heads_ref, f32[128,128]{1,0:T(8,128)S(1)} %select_select_fusion.top_ref), custom_call_target="tpu_custom_call" | custom-call | tf_op jit(solution)/shard_map/node/pallas_call | solution.py:364
  (32 shorter events, 1.3 us)
Async XLA Ops:
  0.6 27.8 %copy-start.3 = (f32[3,1024]{1,0:T(4,128)S(1)}, f32[3,1024]{1,0:T(4,128)}, u32[]{:S(2)}) copy-start(f32[3,1024]{1,0:T(4,128)} %coords.1) | copy-start | bytes 36868
  0.6 39.0 %copy-start.7 = (s32[8,8]{1,0:T(8,128)S(1)}, s32[8,8]{1,0:T(8,128)}, u32[]{:S(2)}) copy-start(s32[8,8]{1,0:T(8,128)} %param.8) | copy-start | bytes 772
  1.5 12.2 %collective-permute-start.3 = (f32[128,128]{1,0:T(8,128)S(1)}, f32[128,128]{1,0:T(8,128)S(1)}, u32[]{:S(2)}, u32[]{:S(2)}) collective-permute-start(f32[128,128]{1,0:T(8,128)S(1)} %slice_bitcast_fusion), channel_id=1, source_target_pairs={{0,1},{1,0},{2,3},{3,2},{4,5},{5,4},{6,7},{7,6},{8,9},{9,8},{10,11... | collective-permute-start | bytes 196616 | tf_op jit(solution)/shard_map/ppermute | solution.py:274
  3.5 1.0 %copy-start = (f32[8,128,128]{2,1,0:T(8,128)S(1)}, f32[8,128,128]{2,1,0:T(8,128)}, u32[]{:S(2)}) copy-start(f32[8,128,128]{2,1,0:T(8,128)} %node_t.1) | copy-start | bytes 1572868
  4.6 1.0 %copy-start.1 = (f32[8,128,128]{2,1,0:T(8,128)S(1)}, f32[8,128,128]{2,1,0:T(8,128)}, u32[]{:S(2)}) copy-start(f32[8,128,128]{2,1,0:T(8,128)} %leaf_t.1) | copy-start | bytes 1572868
  5.6 0.7 copy-start.2
  6.4 0.7 copy-start.4
  7.1 0.7 copy-start.5
  7.7 49.7 %copy-start.6 = (s32[8]{0:T(128)S(1)}, s32[8]{0:T(128)}, u32[]{:S(2)}) copy-start(s32[8]{0:T(128)} %counts.3) | copy-start | bytes 100
  13.6 3.2 %collective-permute-start.2 = (f32[128,128]{1,0:T(8,128)S(1)}, f32[128,128]{1,0:T(8,128)S(1)}, u32[]{:S(2)}, u32[]{:S(2)}) collective-permute-start(f32[128,128]{1,0:T(8,128)S(1)} %get-tuple-element.23.low_ref), channel_id=1, source_target_pairs={{0,1},{1,0},{2,3},{3,2},{4,5},{5,4},{6,7},{7,6},{8,9},{9,8},{10,11... | collective-permute-start | bytes 196616 | tf_op jit(solution)/shard_map/ppermute | solution.py:274
  14.6 4.0 %collective-permute-start.5 = (f32[128,128]{1,0:T(8,128)S(1)}, f32[128,128]{1,0:T(8,128)S(1)}, u32[]{:S(2)}, u32[]{:S(2)}) collective-permute-start(f32[128,128]{1,0:T(8,128)S(1)} %get-tuple-element.32), channel_id=1, source_target_pairs={{0,2},{1,3},{2,0},{3,1},{4,6},{5,7},{6,4},{7,5},{8,10},{9,11},{10,... | collective-permute-start | bytes 196616 | tf_op jit(solution)/shard_map/ppermute | solution.py:274
  17.2 3.8 %collective-permute-start.4 = (f32[128,128]{1,0:T(8,128)S(1)}, f32[128,128]{1,0:T(8,128)S(1)}, u32[]{:S(2)}, u32[]{:S(2)}) collective-permute-start(f32[128,128]{1,0:T(8,128)S(1)} %get-tuple-element.24.low_ref), channel_id=1, source_target_pairs={{0,2},{1,3},{2,0},{3,1},{4,6},{5,7},{6,4},{7,5},{8,10},{9,11},{10,... | collective-permute-start | bytes 196616 | tf_op jit(solution)/shard_map/ppermute | solution.py:274
  18.6 4.6 %collective-permute-start.7 = (f32[128,128]{1,0:T(8,128)S(1)}, f32[128,128]{1,0:T(8,128)S(1)}, u32[]{:S(2)}, u32[]{:S(2)}) collective-permute-start(f32[128,128]{1,0:T(8,128)S(1)} %get-tuple-element.36), channel_id=1, source_target_pairs={{0,4},{1,5},{2,6},{3,7},{4,0},{5,1},{6,2},{7,3},{8,12},{9,13},{10,... | collective-permute-start | bytes 196616 | tf_op jit(solution)/shard_map/ppermute | solution.py:274
  21.5 14.5 %collective-permute-start.6 = (f32[128,128]{1,0:T(8,128)S(1)}, f32[128,128]{1,0:T(8,128)S(1)}, u32[]{:S(2)}, u32[]{:S(2)}) collective-permute-start(f32[128,128]{1,0:T(8,128)S(1)} %get-tuple-element.25.low_ref), channel_id=1, source_target_pairs={{0,4},{1,5},{2,6},{3,7},{4,0},{5,1},{6,2},{7,3},{8,12},{9,13},{10,... | collective-permute-start | bytes 196616 | tf_op jit(solution)/shard_map/ppermute | solution.py:274
  23.3 13.3 %collective-permute-start.9 = (f32[128,128]{1,0:T(8,128)S(1)}, f32[128,128]{1,0:T(8,128)S(1)}, u32[]{:S(2)}, u32[]{:S(2)}) collective-permute-start(f32[128,128]{1,0:T(8,128)S(1)} %get-tuple-element.34), channel_id=1, source_target_pairs={{0,8},{1,9},{2,10},{3,11},{4,12},{5,13},{6,14},{7,15},{8,0},{9,1},... | collective-permute-start | bytes 196616 | tf_op jit(solution)/shard_map/ppermute | solution.py:274
  28.5 29.0 %collective-permute-start.1 = (f32[3,1024]{1,0:T(4,128)S(1)}, f32[3,1024]{1,0:T(4,128)S(1)}, u32[]{:S(2)}, u32[]{:S(2)}) collective-permute-start(f32[3,1024]{1,0:T(4,128)S(1)} %or_select_fusion.own_ref), channel_id=1, source_target_pairs={{1,0},{2,1},{3,2},{4,3},{5,4},{6,5},{7,6},{8,7},{9,8},{10,9},{11,1... | collective-permute-start | bytes 36872 | tf_op jit(solution)/shard_map/ppermute | solution.py:304
  33.8 23.6 %collective-permute-start = (f32[3,1024]{1,0:T(4,128)S(1)}, f32[3,1024]{1,0:T(4,128)S(1)}, u32[]{:S(2)}, u32[]{:S(2)}) collective-permute-start(f32[3,1024]{1,0:T(4,128)S(1)} %or_select_fusion.own_ref), channel_id=1, source_target_pairs={{0,1},{1,2},{2,3},{3,4},{4,5},{5,6},{6,7},{7,8},{8,9},{9,10},{10,1... | collective-permute-start | bytes 36872 | tf_op jit(solution)/shard_map/ppermute | solution.py:303
  36.5 1.3 %collective-permute-start.8 = (f32[128,128]{1,0:T(8,128)S(1)}, f32[128,128]{1,0:T(8,128)S(1)}, u32[]{:S(2)}, u32[]{:S(2)}) collective-permute-start(f32[128,128]{1,0:T(8,128)S(1)} %get-tuple-element.26.low_ref), channel_id=1, source_target_pairs={{0,8},{1,9},{2,10},{3,11},{4,12},{5,13},{6,14},{7,15},{8,0},{9,1},... | collective-permute-start | bytes 196616 | tf_op jit(solution)/shard_map/ppermute | solution.py:274
  38.2 24.7 %collective-permute-start.10 = (f32[128,128]{1,0:T(8,128)S(1)}, f32[128,128]{1,0:T(8,128)S(1)}, u32[]{:S(2)}, u32[]{:S(2)}) collective-permute-start(f32[128,128]{1,0:T(8,128)S(1)} %get-tuple-element.27), channel_id=1, source_target_pairs={{0,16},{1,17},{2,18},{3,19},{4,20},{5,21},{6,22},{7,23},{8,24},{9,... | collective-permute-start | bytes 196616 | tf_op jit(solution)/shard_map/ppermute | solution.py:274

commit v2 on v0

v2 whole, which is shorter than its diff:
```python
import functools
import math

import jax
import jax.numpy as jnp
from jax import lax
from jax.experimental import pallas as pl
from jax.experimental.pallas import tpu as pltpu
from jax.sharding import PartitionSpec as P

ridge = 0.1
length_scale = 0.3
far = 1.0e6
f32 = jnp.float32
bf16 = jnp.bfloat16
BLOCK = 32
STEP = 8
WIDTH = 128
GROUP = 8
params = pltpu.CompilerParams(vmem_limit_bytes=40 * 1024 * 1024)
vmem = pl.BlockSpec(memory_space=pltpu.VMEM)
smem = pl.BlockSpec(memory_space=pltpu.SMEM)
anywhere = pl.BlockSpec(memory_space=pltpu.HBM)


def cost(micros):
    return pl.CostEstimate(flops=int(micros * 1.0e9), bytes_accessed=int(micros * 3.0e6), transcendentals=0)


def iota(shape, dim):
    return lax.broadcasted_iota(jnp.int32, shape, dim)


def split(value):
    high = value.astype(bf16)
    return high, (value - high.astype(f32)).astype(bf16)


def product(left, right, left_dim, right_dim):
    def dot(a, b):
        return lax.dot_general(a, b, (((left_dim,), (right_dim,)), ((), ())), preferred_element_type=f32)

    (lh, ll), (rh, rl) = split(left), split(right)
    return dot(lh, rh) + (dot(lh, rl) + dot(ll, rh))


def lift(move, head):
    return product(move, product(head, move, 1, 0), 0, 0)


def unit(scale):
    shape = (WIDTH, WIDTH)
    return jnp.where(iota(shape, 0) == iota(shape, 1), scale, 0.0).astype(f32)


def matern(delta_x, delta_y, delta_z):
    scale = 3.0**0.5 / length_scale * math.log2(math.e)
    square = delta_x * delta_x + delta_y * delta_y + delta_z * delta_z
    square = jnp.maximum(square * (scale * scale), 1e-30)
    u = square * lax.rsqrt(square)
    return (1.0 + u * math.log(2.0)) * jnp.exp2(-u)


def site_columns(own, count):
    moved = jnp.where(iota((1, WIDTH), 1) < count, own[0:1], far)
    return jnp.concatenate([moved, own[1:3], jnp.zeros((5, WIDTH), f32)], axis=0).T


def lane_copies(vreg, lane):
    return jnp.broadcast_to(vreg[:, lane : lane + 1], vreg.shape)


def add_up(terms):
    while len(terms) > 1:
        terms = [
            terms[a] + terms[a + 1] if a + 1 < len(terms) else terms[a] for a in range(0, len(terms), 2)
        ]
    return terms[0]


def eliminate(rows, base, inverse, store_r, store_s, filler):
    lane = iota((GROUP, WIDTH), 1)
    count = len(rows)
    rows = list(rows)
    for j in range(0, count, STEP):
        at = base + j
        cols = [[lane_copies(rows[i], at + k) for k in range(min(STEP, i - j + 1))] for i in range(j, count)]
        filler(at // STEP)
        spot = (lane >= at) & (lane < at + STEP)
        low = [[None] * STEP for _ in range(STEP)]
        inv = [None] * STEP
        made = [None] * STEP
        made_s = [None] * STEP
        for i in range(STEP):
            for k in range(i):
                t = cols[i][k]
                for m in range(k):
                    t = t - low[i][m] * low[k][m]
                low[i][k] = t * inv[k]
            t = cols[i][i]
            for m in range(i):
                t = t - low[i][m] * low[i][m]
            inv[i] = lax.rsqrt(t)
            u = rows[j + i]
            for m in range(i):
                u = u - low[i][m] * made[m]
            made[i] = u * inv[i]
            store_r(at + i, made[i])
            if inverse:
                u = jnp.where(spot, jnp.where(lane == at + i, 1.0, 0.0).astype(f32), rows[j + i])
                for m in range(i):
                    u = u - low[i][m] * made_s[m]
                made_s[i] = u * inv[i]
                store_s(at + i, made_s[i])
        if j + STEP >= count:
            break
        source = made_s if inverse else made
        back = [None] * STEP
        for i in reversed(range(STEP)):
            t = source[i]
            for m in range(i + 1, STEP):
                t = t - low[m][i] * back[m]
            back[i] = t * inv[i]
        for i in range(j + STEP, count):
            t = jnp.where(spot, 0.0, rows[i]) if inverse else rows[i]
            rows[i] = t - add_up([cols[i - j][k] * back[k] for k in range(STEP)])


def stacked(ref, matrix, first, count):
    return ref[pl.ds(GROUP * first + matrix, count, stride=GROUP), :]


def factor_block(k, load, r_refs, s_refs, store_r, store_s, update, filler):
    base = k * BLOCK
    inverse = s_refs is not None
    if k:
        for b in range(GROUP):
            total = None
            for m in range(k):
                r = stacked(r_refs[m], b, 0, BLOCK)
                right = r
                if inverse:
                    lane = iota((BLOCK, WIDTH), 1)
                    row = iota((BLOCK, WIDTH), 0) + m * BLOCK
                    right = jnp.where(lane >= base, r, 0.0)
                    right = jnp.where(lane <= row, stacked(s_refs[m], b, 0, BLOCK), right)
                pieces = (r[:, base : base + BLOCK], right)
                total = (
                    pieces
                    if total is None
                    else tuple(jnp.concatenate([t, p], axis=0) for t, p in zip(total, pieces))
                )
            update[pl.ds(b, BLOCK, stride=GROUP), :] = product(total[0], total[1], 0, 0)
    lane = iota((GROUP, WIDTH), 1)
    rows = []
    for i in range(BLOCK):
        t = load(base + i)
        if k:
            if inverse:
                t = jnp.where(lane >= base, t, 0.0)
            t = t - update[GROUP * i : GROUP * (i + 1), :]
        rows.append(t)
    eliminate(rows, base, inverse, store_r, store_s, filler)


def write_factor(b, r_refs, target):
    for m, r_ref in enumerate(r_refs):
        shape = (BLOCK, WIDTH)
        keep = iota(shape, 1) >= iota(shape, 0) + m * BLOCK
        target[m * BLOCK : (m + 1) * BLOCK, :] = jnp.where(keep, stacked(r_ref, b, 0, BLOCK), 0.0)


def position():
    return lax.axis_index("grp") * lax.axis_size("dev") + lax.axis_index("dev")


def local_kernel(
    counts_in, coords_in, proxies_in, leaf_in, node_in,
    basis_ref, gram_ref, heads_ref, weight_ref, move_ref,
    counts, coords, proxies, leaf_t, node_t, sems,
):
    pairs = ((counts_in, counts), (coords_in, coords), (proxies_in, proxies), (leaf_in, leaf_t), (node_in, node_t))
    copies = [pltpu.make_async_copy(a, b, sems.at[i]) for i, (a, b) in enumerate(pairs)]
    for copy in copies:
        copy.start()
    leaves = basis_ref.shape[0]
    eye = unit(ridge)
    for copy in copies[:3]:
        copy.wait()
    grams = []
    for leaf in range(leaves):
        span = slice(leaf * WIDTH, leaf * WIDTH + WIDTH)
        own = site_columns(coords[:, span], counts[leaf])
        basis = matern(
            own[:, 0:1] - proxies[0:1, span],
            own[:, 1:2] - proxies[1:2, span],
            own[:, 2:3] - proxies[2:3, span],
        )
        basis_ref[leaf] = basis
        gram = product(basis, basis, 0, 0) * (1.0 / WIDTH) + eye
        gram_ref[pl.ds(leaf, WIDTH, stride=GROUP), :] = gram
        grams.append(gram)
    copies[3].wait()
    weights = [lift(leaf_t[leaf], grams[leaf]) for leaf in range(leaves)]
    copies[4].wait()
    move_ref[...] = node_t[0]
    at = 0
    level = 1
    while len(weights) > 1:
        following = []
        for k in range(len(weights) // 2):
            head = weights[2 * k] + weights[2 * k + 1] + eye
            heads_ref[pl.ds(at, WIDTH, stride=GROUP), :] = head
            at += 1
            following.append(lift(node_t[k * 2**level + 2 ** (level - 1)], head))
        weights = following
        level += 1
    weight_ref[...] = weights[0]


def lift_kernel(left, right, move, chosen_in, weight_ref, chosen_ref, *, level):
    head = left[...] + right[...] + unit(ridge)
    mine = position() % (2 ** (level + 1)) == 2**level
    chosen_ref[...] = jnp.where(mine, head, chosen_in[...])
    weight_ref[...] = lift(move[...], head)


def leaf_kernel(*refs, k, leaves):
    refs = list(refs)
    counts, ids, own_ref, low_ref, high_ref, gram_ref = refs[:6]
    r_done, s_done = refs[6 : 6 + k], refs[6 + k : 6 + 2 * k]
    refs = refs[6 + 2 * k :]
    last = k == WIDTH // BLOCK - 1
    if last:
        basis_ref = refs.pop(0)
    if k:
        refs.pop(0)
    near_out, r_out, s_out = refs[:3]
    refs = refs[3:]
    if last:
        factor_ref, bases_ref = refs[:2]
        refs = refs[2:]
    wide, tiles, update, sems = refs
    span = own_ref.shape[1]
    fan = ids.shape[0]
    share = leaves // (WIDTH // BLOCK)
    wide[:, 0:span] = low_ref[...]
    wide[:, span : 2 * span] = own_ref[...]
    wide[:, 2 * span : 3 * span] = high_ref[...]
    offset = (position() - 1) * leaves
    held = {}

    def tile(t):
        leaf, n = divmod(t, fan)
        at = k * share + leaf
        if n == 0:
            own = site_columns(own_ref[:, at * WIDTH : (at + 1) * WIDTH], counts[at])
            held[leaf] = [jnp.broadcast_to(own[:, d : d + 1], (WIDTH, WIDTH)) for d in range(3)]
        own = held[leaf]
        other = wide[:, pl.ds(pl.multiple_of((ids[n, at] - offset) * WIDTH, WIDTH), WIDTH)]
        value = matern(own[0] - other[0:1], own[1] - other[1:2], own[2] - other[2:3])
        tiles[leaf, n] = value.astype(bf16)
        if n == fan - 1:
            pltpu.make_async_copy(tiles.at[leaf], near_out.at[at], sems.at[leaf]).start()

    each = share * fan // (BLOCK // STEP)

    def filler(step):
        first = (step % (BLOCK // STEP)) * each
        for t in range(first, first + each):
            tile(t)

    def store_r(i, value):
        r_out[GROUP * (i - k * BLOCK) : GROUP * (i - k * BLOCK + 1), :] = value

    def store_s(i, value):
        s_out[GROUP * (i - k * BLOCK) : GROUP * (i - k * BLOCK + 1), :] = value

    def load(i):
        return gram_ref[GROUP * i : GROUP * (i + 1), :]

    factor_block(k, load, r_done, s_done, store_r, store_s, update, filler)
    if last:
        r_all, s_all = list(r_done) + [r_out], list(s_done) + [s_out]
        for b in range(GROUP):
            write_factor(b, r_all, factor_ref.at[b])
            shape = (WIDTH, WIDTH)
            turned = jnp.concatenate([stacked(s, b, 0, BLOCK) for s in s_all], axis=0)
            turned = jnp.where(iota(shape, 1) <= iota(shape, 0), turned, 0.0)
            bases_ref[b * WIDTH : (b + 1) * WIDTH, :] = product(basis_ref[b], turned, 1, 1).astype(bf16)
    for leaf in range(share):
        pltpu.make_async_copy(tiles.at[leaf], near_out.at[k * share + leaf], sems.at[leaf]).wait()


def node_kernel(heads_ref, left, right, chosen, factor_ref, r_ref, update, *, half):
    top_row = jnp.where(position() % half == 0, left[...] + right[...] + unit(ridge), chosen[...])
    group = iota((GROUP, WIDTH), 0)
    blocks = [r_ref.at[pl.ds(m * BLOCK * GROUP, BLOCK * GROUP), :] for m in range(WIDTH // BLOCK)]
    slots = []
    level = 1
    while 2**level <= GROUP:
        slots += [k * 2**level + 2 ** (level - 1) for k in range(GROUP // 2**level)]
        level += 1
    slots.append(0)

    def load(i):
        top = jnp.broadcast_to(top_row[i : i + 1, :], (GROUP, WIDTH))
        return jnp.where(group == GROUP - 1, top, heads_ref[GROUP * i : GROUP * (i + 1), :])

    def store(i, value):
        r_ref[GROUP * i : GROUP * (i + 1), :] = value

    for k in range(WIDTH // BLOCK):
        factor_block(k, load, blocks[:k], None, store, None, update, lambda step: None)
    for b in range(GROUP):
        write_factor(b, blocks, factor_ref.at[slots[b]])


def tied(first, *others):
    return lax.optimization_barrier((first, *others))[0]


def shards(coords, counts, neighbours, proxies, leaf_transfers, node_transfers):
    leaves = counts.shape[0]
    slots = coords.shape[1] // leaves
    fan = neighbours.shape[0]
    count = lax.axis_size("grp") * lax.axis_size("dev")
    levels = count.bit_length() - 1
    half = count // 2
    both = ("grp", "dev")
    mat = jax.ShapeDtypeStruct((WIDTH, WIDTH), f32)
    mats = jax.ShapeDtypeStruct((leaves, WIDTH, WIDTH), f32)
    flat = jax.ShapeDtypeStruct((WIDTH * GROUP, WIDTH), f32)
    part = jax.ShapeDtypeStruct((BLOCK * GROUP, WIDTH), f32)

    valid = jnp.arange(slots, dtype=jnp.int32)[None, :] < counts[:, None]
    keep = valid.reshape(1, leaves * slots) | (jnp.arange(3, dtype=jnp.int32)[:, None] > 0)
    masked = jnp.where(keep, coords, -far)
    up = [(i, i + 1) for i in range(count - 1)]
    low = lax.ppermute(masked, both, up)
    high = lax.ppermute(masked, both, [(target, source) for source, target in up])

    basis, gram, heads, weight, move = pl.pallas_call(
        local_kernel,
        out_shape=(mats, flat, flat, mat, mat),
        in_specs=[anywhere] * 5,
        out_specs=(vmem,) * 5,
        scratch_shapes=[
            pltpu.SMEM(counts.shape, jnp.int32),
            pltpu.VMEM(coords.shape, f32),
            pltpu.VMEM(proxies.shape, f32),
            pltpu.VMEM(leaf_transfers.shape, f32),
            pltpu.VMEM(node_transfers.shape, f32),
            pltpu.SemaphoreType.DMA((5,)),
        ],
        compiler_params=params,
        cost_estimate=cost(4),
        name="local",
    )(*(pltpu.with_memory_space_constraint(x, pltpu.HBM) for x in (counts, coords, proxies, leaf_transfers, node_transfers)))

    chunks = WIDTH // BLOCK
    r_parts, s_parts = [], []
    near = None
    chosen = weight

    def leaf_chunk(k, after):
        nonlocal near
        last = k == chunks - 1
        operands = [counts, neighbours, tied(masked, after), low, high, gram, *r_parts, *s_parts]
        specs = [smem, smem] + [vmem] * (4 + 2 * k)
        if last:
            operands.append(basis)
            specs.append(vmem)
        if k:
            operands.append(near)
            specs.append(anywhere)
        shapes = [jax.ShapeDtypeStruct((leaves, fan, slots, slots), bf16), part, part]
        outs = [anywhere, vmem, vmem]
        if last:
            shapes += [mats, jax.ShapeDtypeStruct((leaves * slots, WIDTH), bf16)]
            outs += [vmem, vmem]
        near, r, s, *rest = pl.pallas_call(
            functools.partial(leaf_kernel, k=k, leaves=leaves),
            out_shape=shapes,
            in_specs=specs,
            out_specs=outs,
            scratch_shapes=[
                pltpu.VMEM((3, 3 * leaves * slots), f32),
                pltpu.VMEM((leaves // chunks, fan, slots, slots), bf16),
                pltpu.VMEM((BLOCK * GROUP, WIDTH), f32),
                pltpu.SemaphoreType.DMA((leaves // chunks,)),
            ],
            input_output_aliases={len(operands) - 1: 0} if k else {},
            compiler_params=params,
            cost_estimate=cost(2.5),
            name=f"leaf{k}",
        )(*operands)
        r_parts.append(r)
        s_parts.append(s)
        return r, rest

    rest = None
    for level in range(levels):
        span = 2 ** (level + 1)
        if level == 0:
            left = lax.ppermute(weight, both, [(i, i + 1) for i in range(0, count, 2)])
            right = weight
        else:
            quarter = span // 4
            first = [(i + quarter, i + 2 * quarter) for i in range(0, count, span)]
            second = [(i + 3 * quarter, i + 2 * quarter) for i in range(0, count, span)]
            if level + 1 == levels:
                first.append((3 * quarter, 0))
                second.append((quarter, 0))
            left = lax.ppermute(weight, both, first)
            right = lax.ppermute(weight, both, second)
        if level < chunks:
            mark, rest = leaf_chunk(level, weight)
            left = tied(left, mark)
        if level + 1 < levels:
            weight, chosen = pl.pallas_call(
                functools.partial(lift_kernel, level=level),
                out_shape=(mat, mat),
                in_specs=[vmem] * 4,
                out_specs=(vmem,) * 2,
                compiler_params=params,
                cost_estimate=cost(0.4),
                name=f"lift{level}",
            )(left, right, move, chosen)
    leaf_factors, leaf_bases = rest

    node_factors = pl.pallas_call(
        functools.partial(node_kernel, half=half),
        out_shape=mats,
        in_specs=[vmem] * 4,
        out_specs=vmem,
        scratch_shapes=[pltpu.VMEM((WIDTH * GROUP, WIDTH), f32), pltpu.VMEM((BLOCK * GROUP, WIDTH), f32)],
        compiler_params=params,
        cost_estimate=cost(6),
        name="node",
    )(heads, left, right, chosen)
    return (near, leaf_bases, leaf_factors, node_factors)


def solution(mesh):
    both = ("grp", "dev")
    in_specs = (
        P(None, both),
        P(both),
        P(None, both),
        P(None, both),
        P(both, None, None),
        P(both, None, None),
    )
    out_specs = (
        P(both, None, None, None),
        P(both, None),
        P(both, None, None),
        P(both, None, None),
    )
    return jax.shard_map(shards, mesh=mesh, in_specs=in_specs, out_specs=out_specs, check_vma=False)
```

time: 344 us -> 56.1 us (0.16)
  other arithmetic: 293 us -> 1.53 us
  Pallas kernels: 0 us -> 27.9 us
  matrix products: 12.2 us -> 0 us
  local copies, waits for them, and re-layouts: 10.6 us -> 0.01 us
  waiting for transfers between devices: 1 us -> 6.53 us
  starting transfers between devices: 24 us -> 18.9 us
    another operation x19 -> x0, other arithmetic: 272 us -> none  [the longest x12 96.4 us: factor(): return jnp.swapaxes(jnp.linalg.cholesky(heads), -1, -2)]
    pallas_call x0 -> x10, Pallas kernels: none -> 27.9 us  [the longest x4 15.3 us: leaf_chunk(): pl.pallas_call(functools.partial(leaf_kernel, k=k, leaves=leaves), out_sh...]
    dot_general x17 -> x0, matrix products: 10.8 us -> none  [the longest x8 4.82 us: lift(): jnp.einsum('lac,lcd->lad', inner, transfer, precision=lax.Precision.HIGHEST)]
    dynamic_update_slice x8 -> x0, other arithmetic: 8.64 us -> none  [shards(): near_tiles = lax.map(tiles_of, (own_sites, valid, gathered))]
    ppermute x11, waiting for transfers between devices: 1 us -> 6.53 us  [the longest x4 6.52 us: shards(): left = lax.ppermute(weight, both, first)]
    ppermute x11, starting transfers between devices: 24 us -> 18.9 us  [the longest x1 5.52 us: shards(): lax.ppermute(masked, both, [(target, source) for source, target in up])]
  transfers between devices with their start and end apart: 11 -> 11, of which waited for: 2 -> 1; matrix products, arithmetic and copies ran while one was open for 87% -> 0% of each run, Pallas kernels for 0% -> 36%
where the time goes in v2:
time: 56.1 us; the launch traced here: 55.7 us
  Pallas kernels  27.9 us (50%)
  starting transfers between devices  18.9 us (34%)
  waiting for transfers between devices  6.53 us (12%)
  other arithmetic  1.53 us (3%)
  between operations  0.89 us (2%)
    pallas_call x4, Pallas kernels, leaf_chunk(): pl.pallas_call(functools.partial(leaf_kernel, k=k, leaves=leaves), out_sh...  15.3 us
    ppermute x4, waiting for transfers between devices, shards(): left = lax.ppermute(weight, both, first)  6.52 us
    pallas_call x1, Pallas kernels, shards(): pl.pallas_call(functools.partial(node_kernel, half=half), out_shape=mats,...  6.46 us
    ppermute x1, starting transfers between devices, shards(): lax.ppermute(masked, both, [(target, source) for source, target in up])  5.52 us
    pallas_call x1, Pallas kernels, shards(): pl.pallas_call(local_kernel, out_shape=(mats, flat, flat, mat, mat), in_s...  4.78 us
    ppermute x4, starting transfers between devices, shards(): left = lax.ppermute(weight, both, first)  4.1 us
    ppermute x1, starting transfers between devices, shards(): low = lax.ppermute(masked, both, up)  4.08 us
    ppermute x4, starting transfers between devices, shards(): right = lax.ppermute(weight, both, second)  3.91 us
  transfers between devices with their start and end apart: 11, of which 1 were waited for; matrix products, arithmetic and copies ran while one was open for 0% of the time, Pallas kernels for 36%

profile of v2, /device:TPU:1, one launch (start us, length us, event | category | flops | bytes accessed | tf_op | source)
XLA Modules:
  0.0 55.7 jit_solution(2332281264664145627)
XLA Ops:
  0.6 0.7 %fusion = pred[1024]{0:T(1024)(128)(4,1)S(1)} fusion(s32[8]{0:T(128)} %refs_0_.7), kind=kLoop, calls=%fused_computation.2 | loop fusion | flops 1024 | bytes 1056 | tf_op jit(solution)/shard_map/lt | solution.py:336
  1.4 0.8 %or_select_fusion.refs_2_ = f32[3,1024]{1,0:T(4,128)S(1)} fusion(f32[3,1024]{1,0:T(4,128)} %coords_in.1, pred[1024]{0:T(1024)(128)(4,1)S(1)} %fusion, pred[3]{0:T(512)(128)(4,1)S(1)} %iota_compare_fusion.1), kind=kLoop, calls=%fused_computation | loop fusion | flops 6144 | bytes 25603 | tf_op jit(solution)/shard_map/jit(_where)/select_n | solution.py:338
  2.2 4.1 %collective-permute-start.1 = (f32[3,1024]{1,0:T(4,128)S(1)}, f32[3,1024]{1,0:T(4,128)S(1)}, u32[]{:S(2)}, u32[]{:S(2)}) collective-permute-start(f32[3,1024]{1,0:T(4,128)S(1)} %or_select_fusion.refs_2_), channel_id=1, source_target_pairs={{0,1},{1,2},{2,3},{3,4},{4,5},{5,6},{6,7},{7,8},{8,9},{9,10},{10,1... | collective-permute-start | bytes 36872 | tf_op jit(solution)/shard_map/ppermute | solution.py:340
  6.3 5.5 %collective-permute-start.2 = (f32[3,1024]{1,0:T(4,128)S(1)}, f32[3,1024]{1,0:T(4,128)S(1)}, u32[]{:S(2)}, u32[]{:S(2)}) collective-permute-start(f32[3,1024]{1,0:T(4,128)S(1)} %or_select_fusion.refs_2_), channel_id=1, source_target_pairs={{1,0},{2,1},{3,2},{4,3},{5,4},{6,5},{7,6},{8,7},{9,8},{10,9},{11,1... | collective-permute-start | bytes 36872 | tf_op jit(solution)/shard_map/ppermute | solution.py:341
  11.8 4.8 %local.1 = (f32[8,128,128]{2,1,0:T(8,128)S(1)}, f32[1024,128]{1,0:T(8,128)S(1)}, f32[1024,128]{1,0:T(8,128)S(1)}, f32[128,128]{1,0:T(8,128)S(1)}, f32[128,128]{1,0:T(8,128)S(1)}) custom-call(s32[8]{0:T(128)} %refs_0_.7, f32[3,1024]{1,0:T(4,128)} %coords_in.1, f32[3,1024]{1,0:T(4,128)} %proxies_in.1, f32[8,128,128]{2,1,0:T(8,128)} %leaf_in.1, ...), custom_call_target="tpu_custom_call" | custom-call | flops 4000000000 | bytes 12000000 | tf_op jit(solution)/shard_map/local/pallas_call | solution.py:343
  16.6 1.3 %collective-permute-start = (f32[128,128]{1,0:T(8,128)S(1)}, f32[128,128]{1,0:T(8,128)S(1)}, u32[]{:S(2)}, u32[]{:S(2)}) collective-permute-start(f32[128,128]{1,0:T(8,128)S(1)} %get-tuple-element.36.right.chosen_in), channel_id=1, source_target_pairs={{0,1},{2,3},{4,5},{6,7},{8,9},{10,11},{12,13},{14,15},{16,17},{18,... | collective-permute-start | bytes 196616 | tf_op jit(solution)/shard_map/ppermute | solution.py:406
  17.9 2.9 %leaf0.1 = (bf16[8,8,128,128]{3,2,1,0:T(8,128)(2,1)}, f32[256,128]{1,0:T(8,128)S(1)}, f32[256,128]{1,0:T(8,128)S(1)}) custom-call(s32[8]{0:T(128)S(1)} %copy-done.1, s32[8,8]{1,0:T(8,128)S(1)} %copy-done, f32[3,1024]{1,0:T(4,128)S(1)} %or_select_fusion.refs_2_, f32[3,1024]{1,0:T(4,128)S(1)} %collective-permute-done.1.refs_3_, ...), custom_call_target="tpu_custom_call" | custom-call | flops 2500000000 | bytes 7500000 | tf_op jit(solution)/shard_map/leaf0/pallas_call | solution.py:382
  20.8 0.3 lift0.1
  21.2 0.7 %collective-permute-start.3 = (f32[128,128]{1,0:T(8,128)S(1)}, f32[128,128]{1,0:T(8,128)S(1)}, u32[]{:S(2)}, u32[]{:S(2)}) collective-permute-start(f32[128,128]{1,0:T(8,128)S(1)} %get-tuple-element.42), channel_id=1, source_target_pairs={{1,2},{5,6},{9,10},{13,14},{17,18},{21,22},{25,26},{29,30}} | collective-permute-start | bytes 196616 | tf_op jit(solution)/shard_map/ppermute | solution.py:415
  21.9 0.7 %collective-permute-start.4 = (f32[128,128]{1,0:T(8,128)S(1)}, f32[128,128]{1,0:T(8,128)S(1)}, u32[]{:S(2)}, u32[]{:S(2)}) collective-permute-start(f32[128,128]{1,0:T(8,128)S(1)} %get-tuple-element.42), channel_id=1, source_target_pairs={{3,2},{7,6},{11,10},{15,14},{19,18},{23,22},{27,26},{31,30}} | collective-permute-start | bytes 196616 | tf_op jit(solution)/shard_map/ppermute | solution.py:416
  22.5 3.5 %leaf1.1 = (bf16[8,8,128,128]{3,2,1,0:T(8,128)(2,1)}, f32[256,128]{1,0:T(8,128)S(1)}, f32[256,128]{1,0:T(8,128)S(1)}) custom-call(s32[8]{0:T(128)S(1)} %copy-done.1, s32[8,8]{1,0:T(8,128)S(1)} %copy-done, f32[3,1024]{1,0:T(4,128)S(1)} %or_select_fusion.refs_2_, f32[3,1024]{1,0:T(4,128)S(1)} %collective-permute-done.1.refs_3_, ...), custom_call_target="tpu_custom_call", output_to_operand_aliasing={{0}: (8, {})} | custom-call | flops 2500000000 | bytes 7500000 | tf_op jit(solution)/shard_map/leaf1/pallas_call | solution.py:382
  26.0 0.3 lift1.1
  26.4 0.7 %collective-permute-start.5 = (f32[128,128]{1,0:T(8,128)S(1)}, f32[128,128]{1,0:T(8,128)S(1)}, u32[]{:S(2)}, u32[]{:S(2)}) collective-permute-start(f32[128,128]{1,0:T(8,128)S(1)} %get-tuple-element.49), channel_id=1, source_target_pairs={{2,4},{10,12},{18,20},{26,28}} | collective-permute-start | bytes 196616 | tf_op jit(solution)/shard_map/ppermute | solution.py:415
  27.0 0.7 %collective-permute-start.6 = (f32[128,128]{1,0:T(8,128)S(1)}, f32[128,128]{1,0:T(8,128)S(1)}, u32[]{:S(2)}, u32[]{:S(2)}) collective-permute-start(f32[128,128]{1,0:T(8,128)S(1)} %get-tuple-element.49), channel_id=1, source_target_pairs={{6,4},{14,12},{22,20},{30,28}} | collective-permute-start | bytes 196616 | tf_op jit(solution)/shard_map/ppermute | solution.py:416
  27.7 3.6 %leaf2.1 = (bf16[8,8,128,128]{3,2,1,0:T(8,128)(2,1)}, f32[256,128]{1,0:T(8,128)S(1)}, f32[256,128]{1,0:T(8,128)S(1)}) custom-call(s32[8]{0:T(128)S(1)} %copy-done.1, s32[8,8]{1,0:T(8,128)S(1)} %copy-done, f32[3,1024]{1,0:T(4,128)S(1)} %or_select_fusion.refs_2_, f32[3,1024]{1,0:T(4,128)S(1)} %collective-permute-done.1.refs_3_, ...), custom_call_target="tpu_custom_call", output_to_operand_aliasing={{0}: (10, {})} | custom-call | flops 2500000000 | bytes 7500000 | tf_op jit(solution)/shard_map/leaf2/pallas_call | solution.py:382
  31.4 0.3 lift2.1
  31.7 1.3 %collective-permute-start.7 = (f32[128,128]{1,0:T(8,128)S(1)}, f32[128,128]{1,0:T(8,128)S(1)}, u32[]{:S(2)}, u32[]{:S(2)}) collective-permute-start(f32[128,128]{1,0:T(8,128)S(1)} %get-tuple-element.56), channel_id=1, source_target_pairs={{4,8},{20,24}} | collective-permute-start | bytes 196616 | tf_op jit(solution)/shard_map/ppermute | solution.py:415
  33.0 1.3 %collective-permute-start.8 = (f32[128,128]{1,0:T(8,128)S(1)}, f32[128,128]{1,0:T(8,128)S(1)}, u32[]{:S(2)}, u32[]{:S(2)}) collective-permute-start(f32[128,128]{1,0:T(8,128)S(1)} %get-tuple-element.56), channel_id=1, source_target_pairs={{12,8},{28,24}} | collective-permute-start | bytes 196616 | tf_op jit(solution)/shard_map/ppermute | solution.py:416
  34.3 6.5 %collective-permute-done.7.left = f32[128,128]{1,0:T(8,128)S(1)} collective-permute-done((f32[128,128]{1,0:T(8,128)S(1)}, f32[128,128]{1,0:T(8,128)S(1)}, u32[]{:S(2)}, u32[]{:S(2)}) %collective-permute-start.7) | collective-permute-done | bytes 65568 | tf_op jit(solution)/shard_map/ppermute | solution.py:415
  40.8 0.3 lift3.1
  41.2 1.3 %collective-permute-start.10 = (f32[128,128]{1,0:T(8,128)S(1)}, f32[128,128]{1,0:T(8,128)S(1)}, u32[]{:S(2)}, u32[]{:S(2)}) collective-permute-start(f32[128,128]{1,0:T(8,128)S(1)} %get-tuple-element.66), channel_id=1, source_target_pairs={{24,16},{8,0}} | collective-permute-start | bytes 196616 | tf_op jit(solution)/shard_map/ppermute | solution.py:416
  42.5 1.5 %collective-permute-start.9 = (f32[128,128]{1,0:T(8,128)S(1)}, f32[128,128]{1,0:T(8,128)S(1)}, u32[]{:S(2)}, u32[]{:S(2)}) collective-permute-start(f32[128,128]{1,0:T(8,128)S(1)} %get-tuple-element.66), channel_id=1, source_target_pairs={{8,16},{24,0}} | collective-permute-start | bytes 196616 | tf_op jit(solution)/shard_map/ppermute | solution.py:415
  44.0 5.3 %leaf3.1 = (bf16[8,8,128,128]{3,2,1,0:T(8,128)(2,1)}, f32[256,128]{1,0:T(8,128)}, f32[256,128]{1,0:T(8,128)}, f32[8,128,128]{2,1,0:T(8,128)}, bf16[1024,128]{1,0:T(8,128)(2,1)}) custom-call(s32[8]{0:T(128)S(1)} %copy-done.1, s32[8,8]{1,0:T(8,128)S(1)} %copy-done, f32[3,1024]{1,0:T(4,128)S(1)} %or_select_fusion.refs_2_, ...), custom_call_target="tpu_custom_call", output_to_operand_aliasing={{0}: (13, {})} | custom-call | flops 2500000000 | bytes 7500000 | tf_op jit(solution)/shard_map/leaf3/pallas_call | solution.py:382
  49.3 6.5 %node.1 = f32[8,128,128]{2,1,0:T(8,128)} custom-call(f32[1024,128]{1,0:T(8,128)S(1)} %get-tuple-element.64.heads_ref, f32[128,128]{1,0:T(8,128)S(1)} %collective-permute-done.9.left, f32[128,128]{1,0:T(8,128)S(1)} %collective-permute-done.10.right, f32[128,128]{1,0:T(8,128)S(1)} %get-tuple-element.67.chosen), custom_call_target="tpu_custom_call" | custom-call | flops 6000000000 | bytes 18000000 | tf_op jit(solution)/shard_map/node/pallas_call | solution.py:432
  (15 shorter events, 0.0 us)
Async XLA Ops:
  2.2 15.7 %copy-start = (s32[8,8]{1,0:T(8,128)S(1)}, s32[8,8]{1,0:T(8,128)}, u32[]{:S(2)}) copy-start(s32[8,8]{1,0:T(8,128)} %refs_1_.7) | copy-start | bytes 772
  2.2 15.7 %copy-start.1 = (s32[8]{0:T(128)S(1)}, s32[8]{0:T(128)}, u32[]{:S(2)}) copy-start(s32[8]{0:T(128)} %refs_0_.7) | copy-start | bytes 100
  2.2 15.7 %collective-permute-start.1 = (f32[3,1024]{1,0:T(4,128)S(1)}, f32[3,1024]{1,0:T(4,128)S(1)}, u32[]{:S(2)}, u32[]{:S(2)}) collective-permute-start(f32[3,1024]{1,0:T(4,128)S(1)} %or_select_fusion.refs_2_), channel_id=1, source_target_pairs={{0,1},{1,2},{2,3},{3,4},{4,5},{5,6},{6,7},{7,8},{8,9},{9,10},{10,1... | collective-permute-start | bytes 36872 | tf_op jit(solution)/shard_map/ppermute | solution.py:340
  6.3 11.6 %collective-permute-start.2 = (f32[3,1024]{1,0:T(4,128)S(1)}, f32[3,1024]{1,0:T(4,128)S(1)}, u32[]{:S(2)}, u32[]{:S(2)}) collective-permute-start(f32[3,1024]{1,0:T(4,128)S(1)} %or_select_fusion.refs_2_), channel_id=1, source_target_pairs={{1,0},{2,1},{3,2},{4,3},{5,4},{6,5},{7,6},{8,7},{9,8},{10,9},{11,1... | collective-permute-start | bytes 36872 | tf_op jit(solution)/shard_map/ppermute | solution.py:341
  16.6 4.3 %collective-permute-start = (f32[128,128]{1,0:T(8,128)S(1)}, f32[128,128]{1,0:T(8,128)S(1)}, u32[]{:S(2)}, u32[]{:S(2)}) collective-permute-start(f32[128,128]{1,0:T(8,128)S(1)} %get-tuple-element.36.right.chosen_in), channel_id=1, source_target_pairs={{0,1},{2,3},{4,5},{6,7},{8,9},{10,11},{12,13},{14,15},{16,17},{18,... | collective-permute-start | bytes 196616 | tf_op jit(solution)/shard_map/ppermute | solution.py:406
  21.2 4.8 %collective-permute-start.3 = (f32[128,128]{1,0:T(8,128)S(1)}, f32[128,128]{1,0:T(8,128)S(1)}, u32[]{:S(2)}, u32[]{:S(2)}) collective-permute-start(f32[128,128]{1,0:T(8,128)S(1)} %get-tuple-element.42), channel_id=1, source_target_pairs={{1,2},{5,6},{9,10},{13,14},{17,18},{21,22},{25,26},{29,30}} | collective-permute-start | bytes 196616 | tf_op jit(solution)/shard_map/ppermute | solution.py:415
  21.9 4.1 %collective-permute-start.4 = (f32[128,128]{1,0:T(8,128)S(1)}, f32[128,128]{1,0:T(8,128)S(1)}, u32[]{:S(2)}, u32[]{:S(2)}) collective-permute-start(f32[128,128]{1,0:T(8,128)S(1)} %get-tuple-element.42), channel_id=1, source_target_pairs={{3,2},{7,6},{11,10},{15,14},{19,18},{23,22},{27,26},{31,30}} | collective-permute-start | bytes 196616 | tf_op jit(solution)/shard_map/ppermute | solution.py:416
  26.4 5.0 %collective-permute-start.5 = (f32[128,128]{1,0:T(8,128)S(1)}, f32[128,128]{1,0:T(8,128)S(1)}, u32[]{:S(2)}, u32[]{:S(2)}) collective-permute-start(f32[128,128]{1,0:T(8,128)S(1)} %get-tuple-element.49), channel_id=1, source_target_pairs={{2,4},{10,12},{18,20},{26,28}} | collective-permute-start | bytes 196616 | tf_op jit(solution)/shard_map/ppermute | solution.py:415
  27.0 4.3 %collective-permute-start.6 = (f32[128,128]{1,0:T(8,128)S(1)}, f32[128,128]{1,0:T(8,128)S(1)}, u32[]{:S(2)}, u32[]{:S(2)}) collective-permute-start(f32[128,128]{1,0:T(8,128)S(1)} %get-tuple-element.49), channel_id=1, source_target_pairs={{6,4},{14,12},{22,20},{30,28}} | collective-permute-start | bytes 196616 | tf_op jit(solution)/shard_map/ppermute | solution.py:416
  31.7 9.1 %collective-permute-start.7 = (f32[128,128]{1,0:T(8,128)S(1)}, f32[128,128]{1,0:T(8,128)S(1)}, u32[]{:S(2)}, u32[]{:S(2)}) collective-permute-start(f32[128,128]{1,0:T(8,128)S(1)} %get-tuple-element.56), channel_id=1, source_target_pairs={{4,8},{20,24}} | collective-permute-start | bytes 196616 | tf_op jit(solution)/shard_map/ppermute | solution.py:415
  33.0 7.8 %collective-permute-start.8 = (f32[128,128]{1,0:T(8,128)S(1)}, f32[128,128]{1,0:T(8,128)S(1)}, u32[]{:S(2)}, u32[]{:S(2)}) collective-permute-start(f32[128,128]{1,0:T(8,128)S(1)} %get-tuple-element.56), channel_id=1, source_target_pairs={{12,8},{28,24}} | collective-permute-start | bytes 196616 | tf_op jit(solution)/shard_map/ppermute | solution.py:416
  41.2 8.1 %collective-permute-start.10 = (f32[128,128]{1,0:T(8,128)S(1)}, f32[128,128]{1,0:T(8,128)S(1)}, u32[]{:S(2)}, u32[]{:S(2)}) collective-permute-start(f32[128,128]{1,0:T(8,128)S(1)} %get-tuple-element.66), channel_id=1, source_target_pairs={{24,16},{8,0}} | collective-permute-start | bytes 196616 | tf_op jit(solution)/shard_map/ppermute | solution.py:416
  42.5 6.8 %collective-permute-start.9 = (f32[128,128]{1,0:T(8,128)S(1)}, f32[128,128]{1,0:T(8,128)S(1)}, u32[]{:S(2)}, u32[]{:S(2)}) collective-permute-start(f32[128,128]{1,0:T(8,128)S(1)} %get-tuple-element.66), channel_id=1, source_target_pairs={{8,16},{24,0}} | collective-permute-start | bytes 196616 | tf_op jit(solution)/shard_map/ppermute | solution.py:415

commit v3 on v0

v3 whole, which is shorter than its diff:
```python
import functools
import math

import jax
import jax.numpy as jnp
from jax import lax
from jax.experimental import pallas as pl
from jax.experimental.pallas import tpu as pltpu
from jax.sharding import PartitionSpec as P

ridge = 0.1
length_scale = 0.3
far = 1.0e6
f32 = jnp.float32
bf16 = jnp.bfloat16
STEP = 8
WIDTH = 128
GROUP = 8
STEPS = WIDTH // STEP
params = pltpu.CompilerParams(vmem_limit_bytes=40 * 1024 * 1024)
vmem = pl.BlockSpec(memory_space=pltpu.VMEM)
smem = pl.BlockSpec(memory_space=pltpu.SMEM)
anywhere = pl.BlockSpec(memory_space=pl.ANY)


def cost(micros):
    return pl.CostEstimate(flops=int(micros * 1.0e9), bytes_accessed=int(micros * 3.0e6), transcendentals=0)


def iota(shape, dim):
    return lax.broadcasted_iota(jnp.int32, shape, dim)


def split(value):
    high = value.astype(bf16)
    return high, (value - high.astype(f32)).astype(bf16)


def product(left, right, left_dim, right_dim):
    def dot(a, b):
        return lax.dot_general(a, b, (((left_dim,), (right_dim,)), ((), ())), preferred_element_type=f32)

    (lh, ll), (rh, rl) = split(left), split(right)
    return dot(lh, rh) + (dot(lh, rl) + dot(ll, rh))


def lift(move, head):
    return product(move, product(head, move, 1, 0), 0, 0)


def unit(scale):
    shape = (WIDTH, WIDTH)
    return jnp.where(iota(shape, 0) == iota(shape, 1), scale, 0.0).astype(f32)


def matern(delta_x, delta_y, delta_z):
    scale = 3.0**0.5 / length_scale * math.log2(math.e)
    square = delta_x * delta_x + delta_y * delta_y + delta_z * delta_z
    square = jnp.maximum(square * (scale * scale), 1e-30)
    u = square * lax.rsqrt(square)
    return (1.0 + u * math.log(2.0)) * jnp.exp2(-u)


def lane_copies(vreg, lane):
    return jnp.broadcast_to(vreg[:, lane : lane + 1], vreg.shape)


def add_up(terms):
    while len(terms) > 1:
        terms = [
            terms[a] + terms[a + 1] if a + 1 < len(terms) else terms[a] for a in range(0, len(terms), 2)
        ]
    return terms[0]


def rows_of(ref, i):
    return ref[GROUP * i : GROUP * (i + 1), :]


def stacked(ref, matrix):
    return ref[pl.ds(matrix, ref.shape[0] // GROUP, stride=GROUP), :]


def eliminate(s, get, put, put_r, put_s):
    at = STEP * s
    lane = iota((GROUP, WIDTH), 1)
    pivots = [get(at + i) for i in range(STEP)]
    cols = [[lane_copies(pivots[i], at + k) for k in range(i + 1)] for i in range(STEP)]
    spot = (lane >= at) & (lane < at + STEP)
    low = [[None] * STEP for _ in range(STEP)]
    inv = [None] * STEP
    made = [None] * STEP
    made_s = [None] * STEP
    for i in range(STEP):
        for k in range(i):
            t = cols[i][k]
            for m in range(k):
                t = t - low[i][m] * low[k][m]
            low[i][k] = t * inv[k]
        t = cols[i][i]
        for m in range(i):
            t = t - low[i][m] * low[i][m]
        inv[i] = lax.rsqrt(t)
        u = pivots[i]
        for m in range(i):
            u = u - low[i][m] * made[m]
        made[i] = u * inv[i]
        put_r(at + i, made[i])
        if put_s:
            u = jnp.where(spot, jnp.where(lane == at + i, 1.0, 0.0).astype(f32), pivots[i])
            for m in range(i):
                u = u - low[i][m] * made_s[m]
            made_s[i] = u * inv[i]
            put_s(at + i, made_s[i])
    first = at + STEP
    if first == WIDTH:
        return
    back = [None] * STEP
    for i in reversed(range(STEP)):
        t = (made_s if put_s else made)[i]
        for m in range(i + 1, STEP):
            t = t - low[m][i] * back[m]
        back[i] = t * inv[i]

    def start(i):
        return jnp.where(spot, 0.0, get(i)) if put_s else get(i)

    later = first + STEP
    for i in range(first, later):
        row = get(i)
        put(i, start(i) - add_up([lane_copies(row, at + k) * back[k] for k in range(STEP)]))
    if later == WIDTH:
        return
    index = at + (lane % 64) // GROUP
    own = lane % GROUP == iota((GROUP, WIDTH), 0)
    left = []
    for i in range(later, WIDTH):
        value = jnp.take_along_axis(get(i), index, axis=1, mode="promise_in_bounds")
        value = jnp.where(own, value, 0.0)
        high = value.astype(bf16).astype(f32)
        left.append(jnp.where(lane < 64, high, value - high))
    left = jnp.concatenate(left, axis=0).astype(bf16)
    right = jnp.concatenate(split(jnp.concatenate(back, axis=0)), axis=1)
    right = jnp.concatenate([right, right], axis=0)
    out = lax.dot_general(left, right, (((1,), (0,)), ((), ())), preferred_element_type=f32)
    out = out[:, :WIDTH] + out[:, WIDTH:]
    for i in range(later, WIDTH):
        put(i, start(i) - out[GROUP * (i - later) : GROUP * (i - later + 1), :])


def position():
    return lax.axis_index("grp") * lax.axis_size("dev") + lax.axis_index("dev")


def local_kernel(
    counts_in, coords_in, proxies_in, leaf_in, node_in,
    basis_ref, gram_ref, heads_ref, message_ref, move_ref, columns_ref,
    counts, coords, proxies, leaf_t, node_t, sems,
):
    pairs = ((counts_in, counts), (coords_in, coords), (proxies_in, proxies), (leaf_in, leaf_t), (node_in, node_t))
    copies = [pltpu.make_async_copy(a, b, sems.at[i]) for i, (a, b) in enumerate(pairs)]
    for copy in copies:
        copy.start()
    leaves = basis_ref.shape[0]
    eye = unit(ridge)
    shape = (WIDTH, WIDTH)
    for copy in copies[:3]:
        copy.wait()
    grams = []
    lane = iota((1, WIDTH), 1)
    for leaf in range(leaves):
        span = slice(leaf * WIDTH, leaf * WIDTH + WIDTH)
        own = coords[:, span]
        valid = lane < counts[leaf]
        at = WIDTH + 3 * leaf
        message_ref[at : at + 1, :] = jnp.where(valid, own[0:1], -far)
        message_ref[at + 1 : at + 3, :] = own[1:3]
        turned = jnp.concatenate([jnp.where(valid, own[0:1], far), own[1:3], jnp.zeros((5, WIDTH), f32)], axis=0).T
        side = [jnp.broadcast_to(turned[:, d : d + 1], shape) for d in range(3)]
        for d in range(3):
            columns_ref[leaf, d] = side[d]
        basis = matern(*(side[d] - jnp.broadcast_to(proxies[d : d + 1, span], shape) for d in range(3)))
        basis_ref[leaf] = basis
        gram = product(basis, basis, 0, 0) * (1.0 / WIDTH) + eye
        gram_ref[pl.ds(leaf, WIDTH, stride=GROUP), :] = gram
        grams.append(gram)
    copies[3].wait()
    weights = [lift(leaf_t[leaf], grams[leaf]) for leaf in range(leaves)]
    copies[4].wait()
    move_ref[...] = node_t[0]
    heads_ref[pl.ds(GROUP - 1, WIDTH, stride=GROUP), :] = eye
    at = 0
    level = 1
    while len(weights) > 1:
        following = []
        for k in range(len(weights) // 2):
            head = weights[2 * k] + weights[2 * k + 1] + eye
            heads_ref[pl.ds(at, WIDTH, stride=GROUP), :] = head
            at += 1
            following.append(lift(node_t[k * 2**level + 2 ** (level - 1)], head))
        weights = following
        level += 1
    message_ref[0:WIDTH, :] = weights[0]


def lift_kernel(left, right, move, chosen_in, *rest, level):
    weight_ref, chosen_ref = rest[-2:]
    span = slice(0, WIDTH)
    head = left[span, :] + right[span, :] + unit(ridge)
    mine = position() % (2 ** (level + 1)) == 2**level
    chosen_ref[...] = jnp.where(mine, head, chosen_in[span, :])
    weight_ref[span, :] = lift(move[...], head)
    if weight_ref.shape[0] > WIDTH:
        weight_ref[WIDTH:, :] = right[WIDTH:, :]


def node_slots():
    slots = []
    level = 1
    while 2**level <= GROUP:
        slots += [k * 2**level + 2 ** (level - 1) for k in range(GROUP // 2**level)]
        level += 1
    return slots


class Copies:
    def __init__(self, sems):
        self.sems, self.made = sems, []

    def start(self, source, target):
        copy = pltpu.make_async_copy(source, target, self.sems.at[len(self.made)])
        copy.start()
        self.made.append(copy)

    def wait(self):
        for copy in self.made:
            copy.wait()


def near_part(near, flush, tiles_in, near_out, operands, tiles_out, wide, copies):
    for n, leaf in enumerate(flush):
        copies.start(tiles_in.at[n], near_out.at[leaf])
    if not near:
        return lambda t: None
    ids, message, low, high, columns = operands
    size = message.shape[0] - WIDTH
    leaves, fan = ids.shape[1], ids.shape[0]
    for n, ref in enumerate((low, message, high)):
        wide[n * size : (n + 1) * size, :] = ref[WIDTH:, :]
    offset = (position() - 1) * leaves
    shape = (WIDTH, WIDTH)

    def tile(t):
        if t >= len(near) * fan:
            return
        at, n = divmod(t, fan)
        leaf = near[at]
        other = wide[pl.ds(3 * (ids[n, leaf] - offset), 3), :]
        value = matern(*(columns[leaf, d] - jnp.broadcast_to(other[d : d + 1], shape) for d in range(3)))
        tiles_out[at, n] = value.astype(bf16)

    return tile


def work_kernel(*refs, names, steps, near, flush, final):
    ref = dict(zip(names, refs))
    copies = Copies(ref["sems"])
    tile = near_part(
        near, flush, ref.get("tiles_in"), ref.get("near_out"),
        [ref.get(n) for n in ("ids", "message", "low", "high", "columns")],
        ref.get("tiles_out"), ref.get("wide"), copies,
    )
    fan = ref["ids"].shape[0] if near else 0
    total = len(near) * fan
    share = -(-total // max(1, 2 * len(steps)))
    done = 0
    held = ({}, {})
    for s in steps:
        for side, name in enumerate(("leaf", "node")):
            source, values = ref[name + "_in"], held[side]
            base = STEP * steps[0]

            def get(i, source=source, values=values):
                return values[i] if i in values else rows_of(source, i)

            def put(i, value, values=values):
                values[i] = value

            def store(kind):
                target = ref[kind]

                def put_row(i, value):
                    target[GROUP * (i - base) : GROUP * (i - base + 1), :] = value

                return put_row

            eliminate(s, get, put, store(name + "_r"), store("leaf_s") if name == "leaf" else None)
            for t in range(done, done + share):
                tile(t)
            done += share
    for side, name in enumerate(("leaf", "node")):
        if name + "_out" in ref:
            for i in range(STEP * (steps[-1] + 1), WIDTH):
                ref[name + "_out"][GROUP * i : GROUP * (i + 1), :] = held[side][i]
    if final:
        parts = {
            kind: [ref[f"{kind}{n}"] for n in range(final)] for kind in ("leaf_r", "leaf_s", "node_r")
        }
        upper = iota((WIDTH, WIDTH), 1) >= iota((WIDTH, WIDTH), 0)
        lower = iota((WIDTH, WIDTH), 1) <= iota((WIDTH, WIDTH), 0)

        def whole(kind, b):
            return jnp.concatenate([stacked(part, b) for part in parts[kind]], axis=0)

        for b in range(GROUP):
            turned = jnp.where(lower, whole("leaf_s", b), 0.0)
            ref["bases"][b * WIDTH : (b + 1) * WIDTH, :] = product(ref["basis"][b], turned, 1, 1).astype(bf16)
            ref["factors"][b] = jnp.where(upper, whole("leaf_r", b), 0.0)
            copies.start(ref["factors"].at[b], ref["leaf_factors"].at[b])
            if b < GROUP - 1:
                ref["nodes"][b] = jnp.where(upper, whole("node_r", b), 0.0)
                copies.start(ref["nodes"].at[b], ref["node_factors"].at[node_slots()[b]])
        copies.start(ref["bases"], ref["leaf_bases"])
        for t in range(total):
            tile(t)
    copies.wait()


def top_kernel(*refs, names, flush, half):
    ref = dict(zip(names, refs))
    copies = Copies(ref["sems"])
    near_part((), flush, ref["tiles_in"], ref["near_out"], None, None, None, copies)
    left, right, chosen = ref["left"], ref["right"], ref["chosen"]
    top = jnp.where(position() % half == 0, left[...] + right[...] + unit(ridge), chosen[...])
    values = {}

    def get(i):
        return values[i] if i in values else jnp.broadcast_to(top[i : i + 1, :], (GROUP, WIDTH))

    def put(i, value):
        values[i] = value

    lane = iota((1, WIDTH), 1)
    target = ref["factor"]

    def put_r(i, value):
        target[i : i + 1, :] = jnp.where(lane >= i, value[0:1, :], 0.0)

    for s in range(STEPS):
        eliminate(s, get, put, put_r, None)
    copies.start(target, ref["node_out"].at[0])
    copies.wait()


def call(body, operands, outs, scratch, aliases, micros, name, **static):
    names = [o[0] for o in operands] + [o[0] for o in outs] + [s[0] for s in scratch]
    at = {o[0]: n for n, o in enumerate(operands)}
    to = {o[0]: n for n, o in enumerate(outs)}
    made = pl.pallas_call(
        functools.partial(body, names=names, **static),
        out_shape=[o[1] for o in outs],
        in_specs=[o[2] for o in operands],
        out_specs=[o[2] for o in outs],
        scratch_shapes=[s[1] for s in scratch],
        input_output_aliases={at[a]: to[b] for a, b in aliases.items()},
        compiler_params=params,
        cost_estimate=cost(micros),
        name=name,
    )(*(o[1] for o in operands))
    return dict(zip(to, made))


def shards(coords, counts, neighbours, proxies, leaf_transfers, node_transfers):
    leaves = counts.shape[0]
    slots = coords.shape[1] // leaves
    fan = neighbours.shape[0]
    count = lax.axis_size("grp") * lax.axis_size("dev")
    levels = count.bit_length() - 1
    half = count // 2
    both = ("grp", "dev")
    shape = jax.ShapeDtypeStruct
    mat = shape((WIDTH, WIDTH), f32)
    mats = shape((leaves, WIDTH, WIDTH), f32)
    flat = shape((WIDTH * GROUP, WIDTH), f32)
    long = shape((WIDTH + 3 * leaves, WIDTH), f32)

    basis, gram, heads, message, move, columns = pl.pallas_call(
        local_kernel,
        out_shape=(mats, flat, flat, long, mat, shape((leaves, 3, slots, WIDTH), f32)),
        in_specs=[anywhere] * 5,
        out_specs=(vmem,) * 6,
        scratch_shapes=[
            pltpu.SMEM(counts.shape, jnp.int32),
            pltpu.VMEM(coords.shape, f32),
            pltpu.VMEM(proxies.shape, f32),
            pltpu.VMEM(leaf_transfers.shape, f32),
            pltpu.VMEM(node_transfers.shape, f32),
            pltpu.SemaphoreType.DMA((5,)),
        ],
        compiler_params=params,
        cost_estimate=cost(4),
        name="local",
    )(*(pltpu.with_memory_space_constraint(x, pltpu.HBM) for x in (counts, coords, proxies, leaf_transfers, node_transfers)))

    plan = [
        dict(steps=(0, 1, 2, 3), near=()),
        dict(steps=(4, 5, 6, 7), near=()),
        dict(steps=(8, 9, 10, 11), near=(0, 1, 2)),
        dict(steps=(12, 13, 14, 15), near=(3, 4, 5)),
        dict(steps=(), near=tuple(range(6, leaves))),
    ]
    state = dict(leaf=gram, node=heads, parts=[], tiles=None, flush=(), near_out=None)

    def work(n, after, low, high):
        steps, near = plan[n]["steps"], plan[n]["near"]
        final = n == len(plan) - 1
        flush = state["flush"]
        operands = [("after", after, anywhere)]
        outs, scratch, aliases = [], [], {}
        if steps:
            rows = shape((STEP * len(steps) * GROUP, WIDTH), f32)
            operands += [("leaf_in", state["leaf"], vmem), ("node_in", state["node"], vmem)]
            outs += [(kind, rows, vmem) for kind in ("leaf_r", "leaf_s", "node_r")]
            if steps[-1] + 1 < STEPS:
                outs += [("leaf_out", flat, vmem), ("node_out", flat, vmem)]
        if near:
            operands += [("ids", neighbours, smem), ("message", message, vmem), ("low", low, vmem)]
            operands += [("high", high, vmem), ("columns", columns, vmem)]
            outs.append(("tiles_out", shape((len(near), fan, slots, slots), bf16), vmem))
            scratch.append(("wide", pltpu.VMEM((9 * leaves, WIDTH), f32)))
        if flush:
            operands.append(("tiles_in", state["tiles"], vmem))
            outs.append(("near_out", shape((leaves, fan, slots, slots), bf16), anywhere))
            if state["near_out"] is not None:
                operands.append(("near_in", state["near_out"], anywhere))
                aliases["near_in"] = "near_out"
        if final:
            for k, part in enumerate(state["parts"]):
                operands += [(f"{kind}{k}", part[kind], vmem) for kind in ("leaf_r", "leaf_s", "node_r")]
            operands.append(("basis", basis, vmem))
            outs += [("leaf_factors", mats, anywhere), ("node_factors", mats, anywhere)]
            outs.append(("leaf_bases", shape((leaves * slots, WIDTH), bf16), anywhere))
            scratch += [("factors", pltpu.VMEM(mats.shape, f32)), ("nodes", pltpu.VMEM(mats.shape, f32))]
            scratch.append(("bases", pltpu.VMEM((leaves * slots, WIDTH), bf16)))
        scratch.append(("sems", pltpu.SemaphoreType.DMA((32,))))
        made = call(
            work_kernel, operands, outs, scratch, aliases, 3, f"work{n}",
            steps=steps, near=near, flush=flush, final=len(state["parts"]) if final else 0,
        )
        if steps:
            state["parts"].append(made)
            state["leaf"], state["node"] = made.get("leaf_out"), made.get("node_out")
        state["tiles"], state["flush"] = made.get("tiles_out"), near
        state["near_out"] = made.get("near_out", state["near_out"])
        return made

    up = [(i, i + 1) for i in range(count - 1)]
    weight = chosen = message
    low = high = made = None
    for level in range(levels):
        span = 2 ** (level + 1)
        quarter = span // 4
        first = [(i + quarter, i + 2 * quarter) for i in range(0, count, span)]
        second = [(i + 3 * quarter, i + 2 * quarter) for i in range(0, count, span)]
        if level + 1 == levels:
            first.append((3 * quarter, 0))
            second.append((quarter, 0))
        if level == 0:
            left, right = lax.ppermute(weight, both, up), weight
            low = left
        elif level == 1:
            left = lax.ppermute(weight, both, first)
            right = lax.ppermute(weight, both, [(target, source) for source, target in up])
            high = right
        else:
            left, right = lax.ppermute(weight, both, first), lax.ppermute(weight, both, second)
        if level < len(plan):
            made = work(level, weight, low, high)
        if level + 1 < levels:
            outs = [("weight", long if level == 0 else mat, vmem), ("chosen_out", mat, vmem)]
            token = next(iter(made.values()))
            weight, chosen = pl.pallas_call(
                functools.partial(lift_kernel, level=level),
                out_shape=[o[1] for o in outs],
                in_specs=[vmem] * 4 + [anywhere],
                out_specs=[vmem] * 2,
                compiler_params=params,
                cost_estimate=cost(0.4),
                name=f"lift{level}",
            )(left, right, move, chosen, token)

    top = call(
        top_kernel,
        [
            ("left", left, vmem), ("right", right, vmem), ("chosen", chosen, vmem),
            ("tiles_in", state["tiles"], vmem), ("near_in", state["near_out"], anywhere),
            ("node_in", made["node_factors"], anywhere),
        ],
        [("near_out", shape((leaves, fan, slots, slots), bf16), anywhere), ("node_out", mats, anywhere)],
        [("factor", pltpu.VMEM((WIDTH, WIDTH), f32)), ("sems", pltpu.SemaphoreType.DMA((16,)))],
        {"near_in": "near_out", "node_in": "node_out"},
        5, "top", flush=state["flush"], half=half,
    )
    return (top["near_out"], made["leaf_bases"], made["leaf_factors"], top["node_out"])


def solution(mesh):
    both = ("grp", "dev")
    in_specs = (
        P(None, both),
        P(both),
        P(None, both),
        P(None, both),
        P(both, None, None),
        P(both, None, None),
    )
    out_specs = (
        P(both, None, None, None),
        P(both, None),
        P(both, None, None),
        P(both, None, None),
    )
    return jax.shard_map(shards, mesh=mesh, in_specs=in_specs, out_specs=out_specs, check_vma=False)
```

time: 344 us -> 48.9 us (0.14)
  the two profiles are of different devices: /device:TPU:1 before, /device:TPU:0 now
where the time goes in v3:
time: 48.9 us; the launch traced here: 48.7 us
  Pallas kernels  26.6 us (54%)
  starting transfers between devices  12.2 us (25%)
  waiting for transfers between devices  8.8 us (18%)
  between operations  1 us (2%)
    pallas_call x6, Pallas kernels, call(): pl.pallas_call(functools.partial(body, names=names, **static), out_shape=...  20.4 us
    ppermute x1, starting transfers between devices, shards(): left, right = (lax.ppermute(weight, both, up), weight)  4.85 us
    pallas_call x1, Pallas kernels, shards(): pl.pallas_call(local_kernel, out_shape=(mats, flat, flat, long, mat, shap...  4.81 us
    ppermute x3, waiting for transfers between devices, shards(): lax.ppermute(weight, both, first)  3.63 us
    ppermute x3, waiting for transfers between devices, shards(): lax.ppermute(weight, both, second)  3.41 us
    ppermute x3, starting transfers between devices, shards(): lax.ppermute(weight, both, first)  2.8 us
    ppermute x3, starting transfers between devices, shards(): lax.ppermute(weight, both, second)  2.62 us
    ppermute x1, waiting for transfers between devices, shards(): lax.ppermute(weight, both, [(target, source) for source, target in up])  1.75 us
  transfers between devices with their start and end apart: 9, of which 3 were waited for; matrix products, arithmetic and copies ran while one was open for 0% of the time, Pallas kernels for 30%

profile of v3, /device:TPU:0, one launch (start us, length us, event | category | flops | bytes accessed | tf_op | source)
XLA Modules:
  0.0 48.7 jit_solution(4964161568775895018)
XLA Ops:
  0.6 4.8 %local.1 = (f32[8,128,128]{2,1,0:T(8,128)S(1)}, f32[1024,128]{1,0:T(8,128)S(1)}, f32[1024,128]{1,0:T(8,128)S(1)}, f32[152,128]{1,0:T(8,128)S(1)}, f32[128,128]{1...) custom-call(s32[8]{0:T(128)} %counts_in.1, f32[3,1024]{1,0:T(4,128)} %coords_in.1, f32[3,1024]{1,0:T(4,128)} %proxies_in.1, ...), custom_call_target="tpu_custom_call" | custom-call | flops 4000000000 | bytes 12000000 | tf_op jit(solution)/shard_map/local/pallas_call | solution.py:387
  5.5 4.8 %collective-permute-start = (f32[152,128]{1,0:T(8,128)S(1)}, f32[152,128]{1,0:T(8,128)S(1)}, u32[]{:S(2)}, u32[]{:S(2)}) collective-permute-start(f32[152,128]{1,0:T(8,128)S(1)} %get-tuple-element.46.refs_0_.right.chosen_in.refs_4_.refs_2_), channel_id=1, source_target_pairs={{0,1},{1,2},{2,3},{3,4},{4,5},{5,6},{6,7},{7,8},{8,9},{9,10},{10,1... | collective-permute-start | bytes 233480 | tf_op jit(solution)/shard_map/ppermute | solution.py:469
  10.3 2.9 %work0.1 = (f32[256,128]{1,0:T(8,128)S(1)}, f32[256,128]{1,0:T(8,128)S(1)}, f32[256,128]{1,0:T(8,128)S(1)}, f32[1024,128]{1,0:T(8,128)S(1)}, f32[1024,128]{1,0:T(8,128)S(1)}) custom-call(f32[152,128]{1,0:T(8,128)S(1)} %get-tuple-element.46.refs_0_.right.chosen_in.refs_4_.refs_2_, f32[1024,128]{1,0:T(8,128)S(1)} %get-tuple-element.48.refs_1_, ...), custom_call_target="tpu_custom_call" | custom-call | flops 3000000000 | bytes 9000000 | tf_op jit(solution)/shard_map/work0/pallas_call | solution.py:359
  13.2 0.4 lift0.1
  13.6 1.3 %collective-permute-start.2 = (f32[152,128]{1,0:T(8,128)S(1)}, f32[152,128]{1,0:T(8,128)S(1)}, u32[]{:S(2)}, u32[]{:S(2)}) collective-permute-start(f32[152,128]{1,0:T(8,128)S(1)} %get-tuple-element.51.refs_0_), channel_id=1, source_target_pairs={{1,0},{2,1},{3,2},{4,3},{5,4},{6,5},{7,6},{8,7},{9,8},{10,9},{11,1... | collective-permute-start | bytes 233480 | tf_op jit(solution)/shard_map/ppermute | solution.py:473
  14.9 0.7 %collective-permute-start.1 = (f32[152,128]{1,0:T(8,128)S(1)}, f32[152,128]{1,0:T(8,128)S(1)}, u32[]{:S(2)}, u32[]{:S(2)}) collective-permute-start(f32[152,128]{1,0:T(8,128)S(1)} %get-tuple-element.51.refs_0_), channel_id=1, source_target_pairs={{1,2},{5,6},{9,10},{13,14},{17,18},{21,22},{25,26},{29,30}} | collective-permute-start | bytes 233480 | tf_op jit(solution)/shard_map/ppermute | solution.py:472
  15.5 0.0 copy-start
  15.5 2.5 %work1.1 = (f32[256,128]{1,0:T(8,128)S(1)}, f32[256,128]{1,0:T(8,128)S(1)}, f32[256,128]{1,0:T(8,128)S(1)}, f32[1024,128]{1,0:T(8,128)S(1)}, f32[1024,128]{1,0:T(8,128)S(1)}) custom-call(f32[152,128]{1,0:T(8,128)S(1)} %get-tuple-element.51.refs_0_, f32[1024,128]{1,0:T(8,128)S(1)} %get-tuple-element.53.refs_1_, f32[1024,128]{1,0:T(8,128)S(1)} %get-tuple-element.54.refs_2_), custom_call_target="tpu_custom_call" | custom-call | flops 3000000000 | bytes 9000000 | tf_op jit(solution)/shard_map/work1/pallas_call | solution.py:359
  18.1 1.7 %collective-permute-done.2.right.refs_6_.refs_4_ = f32[152,128]{1,0:T(8,128)S(1)} collective-permute-done((f32[152,128]{1,0:T(8,128)S(1)}, f32[152,128]{1,0:T(8,128)S(1)}, u32[]{:S(2)}, u32[]{:S(2)}) %collective-permute-start.2) | collective-permute-done | bytes 77856 | tf_op jit(solution)/shard_map/ppermute | solution.py:473
  19.8 0.3 lift1.1
  20.2 0.7 %collective-permute-start.4 = (f32[128,128]{1,0:T(8,128)S(1)}, f32[128,128]{1,0:T(8,128)S(1)}, u32[]{:S(2)}, u32[]{:S(2)}) collective-permute-start(f32[128,128]{1,0:T(8,128)S(1)} %get-tuple-element.56.refs_0_), channel_id=1, source_target_pairs={{6,4},{14,12},{22,20},{30,28}} | collective-permute-start | bytes 196616 | tf_op jit(solution)/shard_map/ppermute | solution.py:476
  20.9 0.7 %collective-permute-start.3 = (f32[128,128]{1,0:T(8,128)S(1)}, f32[128,128]{1,0:T(8,128)S(1)}, u32[]{:S(2)}, u32[]{:S(2)}) collective-permute-start(f32[128,128]{1,0:T(8,128)S(1)} %get-tuple-element.56.refs_0_), channel_id=1, source_target_pairs={{2,4},{10,12},{18,20},{26,28}} | collective-permute-start | bytes 196616 | tf_op jit(solution)/shard_map/ppermute | solution.py:476
  21.6 3.6 %work2.1 = (f32[256,128]{1,0:T(8,128)S(1)}, f32[256,128]{1,0:T(8,128)S(1)}, f32[256,128]{1,0:T(8,128)S(1)}, f32[1024,128]{1,0:T(8,128)S(1)}, f32[1024,128]{1,0:T...) custom-call(f32[128,128]{1,0:T(8,128)S(1)} %get-tuple-element.56.refs_0_, f32[1024,128]{1,0:T(8,128)S(1)} %get-tuple-element.58.refs_1_, ...), custom_call_target="tpu_custom_call" | custom-call | flops 3000000000 | bytes 9000000 | tf_op jit(solution)/shard_map/work2/pallas_call | solution.py:359
  25.2 0.3 lift2.1
  25.5 0.7 %collective-permute-start.6 = (f32[128,128]{1,0:T(8,128)S(1)}, f32[128,128]{1,0:T(8,128)S(1)}, u32[]{:S(2)}, u32[]{:S(2)}) collective-permute-start(f32[128,128]{1,0:T(8,128)S(1)} %get-tuple-element.62.refs_0_), channel_id=1, source_target_pairs={{12,8},{28,24}} | collective-permute-start | bytes 196616 | tf_op jit(solution)/shard_map/ppermute | solution.py:476
  26.2 0.8 %collective-permute-start.5 = (f32[128,128]{1,0:T(8,128)S(1)}, f32[128,128]{1,0:T(8,128)S(1)}, u32[]{:S(2)}, u32[]{:S(2)}) collective-permute-start(f32[128,128]{1,0:T(8,128)S(1)} %get-tuple-element.62.refs_0_), channel_id=1, source_target_pairs={{4,8},{20,24}} | collective-permute-start | bytes 196616 | tf_op jit(solution)/shard_map/ppermute | solution.py:476
  27.0 3.0 %work3.1 = (f32[256,128]{1,0:T(8,128)S(1)}, f32[256,128]{1,0:T(8,128)S(1)}, f32[256,128]{1,0:T(8,128)S(1)}, bf16[3,8,128,128]{3,2,1,0:T(8,128)(2,1)S(1)}, bf16[8,8,128,128]{3,2,1,0:T(8,128)(2,1)}) custom-call(f32[128,128]{1,0:T(8,128)S(1)} %get-tuple-element.62.refs_0_, f32[1024,128]{1,0:T(8,128)S(1)} %get-tuple-element.64.refs_1_, ...), custom_call_target="tpu_custom_call" | custom-call | flops 3000000000 | bytes 9000000 | tf_op jit(solution)/shard_map/work3/pallas_call | solution.py:359
  30.1 0.3 lift3.1
  30.5 1.3 %collective-permute-start.8 = (f32[128,128]{1,0:T(8,128)S(1)}, f32[128,128]{1,0:T(8,128)S(1)}, u32[]{:S(2)}, u32[]{:S(2)}) collective-permute-start(f32[128,128]{1,0:T(8,128)S(1)} %get-tuple-element.68.refs_0_), channel_id=1, source_target_pairs={{24,16},{8,0}} | collective-permute-start | bytes 196616 | tf_op jit(solution)/shard_map/ppermute | solution.py:476
  31.8 1.3 %collective-permute-start.7 = (f32[128,128]{1,0:T(8,128)S(1)}, f32[128,128]{1,0:T(8,128)S(1)}, u32[]{:S(2)}, u32[]{:S(2)}) collective-permute-start(f32[128,128]{1,0:T(8,128)S(1)} %get-tuple-element.68.refs_0_), channel_id=1, source_target_pairs={{8,16},{24,0}} | collective-permute-start | bytes 196616 | tf_op jit(solution)/shard_map/ppermute | solution.py:476
  33.1 2.7 %work4.1 = (bf16[2,8,128,128]{3,2,1,0:T(8,128)(2,1)S(1)}, bf16[8,8,128,128]{3,2,1,0:T(8,128)(2,1)}, f32[8,128,128]{2,1,0:T(8,128)}, f32[8,128,128]{2,1,0:T(8,128)}, bf16[1024,128]{1,0:T(8,128)(2,1)}) custom-call(f32[128,128]{1,0:T(8,128)S(1)} %get-tuple-element.68.refs_0_, s32[8,8]{1,0:T(8,128)S(1)} %copy-done, ...), custom_call_target="tpu_custom_call", output_to_operand_aliasing={{1}: (7, {})} | custom-call | flops 3000000000 | bytes 9000000 | tf_op jit(solution)/shard_map/work4/pallas_call | solution.py:359
  35.8 3.4 %collective-permute-done.8.refs_1_ = f32[128,128]{1,0:T(8,128)S(1)} collective-permute-done((f32[128,128]{1,0:T(8,128)S(1)}, f32[128,128]{1,0:T(8,128)S(1)}, u32[]{:S(2)}, u32[]{:S(2)}) %collective-permute-start.8) | collective-permute-done | bytes 65568 | tf_op jit(solution)/shard_map/ppermute | solution.py:476
  39.2 3.6 %collective-permute-done.7.refs_0_ = f32[128,128]{1,0:T(8,128)S(1)} collective-permute-done((f32[128,128]{1,0:T(8,128)S(1)}, f32[128,128]{1,0:T(8,128)S(1)}, u32[]{:S(2)}, u32[]{:S(2)}) %collective-permute-start.7) | collective-permute-done | bytes 65568 | tf_op jit(solution)/shard_map/ppermute | solution.py:476
  42.8 5.7 %top.1 = (bf16[8,8,128,128]{3,2,1,0:T(8,128)(2,1)}, f32[8,128,128]{2,1,0:T(8,128)}) custom-call(f32[128,128]{1,0:T(8,128)S(1)} %collective-permute-done.7.refs_0_, f32[128,128]{1,0:T(8,128)S(1)} %collective-permute-done.8.refs_1_, f32[128,128]{1,0:T(8,128)S(1)} %get-tuple-element.69.refs_2_, ...), custom_call_target="tpu_custom_call", output_to_operand_aliasing={{0}: (4, {}), {1}: (5, {})} | custom-call | flops 5000000000 | bytes 15000000 | tf_op jit(solution)/shard_map/top/pallas_call | solution.py:359
  (7 shorter events, 0.0 us)
Async XLA Ops:
  5.5 7.7 %collective-permute-start = (f32[152,128]{1,0:T(8,128)S(1)}, f32[152,128]{1,0:T(8,128)S(1)}, u32[]{:S(2)}, u32[]{:S(2)}) collective-permute-start(f32[152,128]{1,0:T(8,128)S(1)} %get-tuple-element.46.refs_0_.right.chosen_in.refs_4_.refs_2_), channel_id=1, source_target_pairs={{0,1},{1,2},{2,3},{3,4},{4,5},{5,6},{6,7},{7,8},{8,9},{9,10},{10,1... | collective-permute-start | bytes 233480 | tf_op jit(solution)/shard_map/ppermute | solution.py:469
  13.6 6.3 %collective-permute-start.2 = (f32[152,128]{1,0:T(8,128)S(1)}, f32[152,128]{1,0:T(8,128)S(1)}, u32[]{:S(2)}, u32[]{:S(2)}) collective-permute-start(f32[152,128]{1,0:T(8,128)S(1)} %get-tuple-element.51.refs_0_), channel_id=1, source_target_pairs={{1,0},{2,1},{3,2},{4,3},{5,4},{6,5},{7,6},{8,7},{9,8},{10,9},{11,1... | collective-permute-start | bytes 233480 | tf_op jit(solution)/shard_map/ppermute | solution.py:473
  14.9 5.0 %collective-permute-start.1 = (f32[152,128]{1,0:T(8,128)S(1)}, f32[152,128]{1,0:T(8,128)S(1)}, u32[]{:S(2)}, u32[]{:S(2)}) collective-permute-start(f32[152,128]{1,0:T(8,128)S(1)} %get-tuple-element.51.refs_0_), channel_id=1, source_target_pairs={{1,2},{5,6},{9,10},{13,14},{17,18},{21,22},{25,26},{29,30}} | collective-permute-start | bytes 233480 | tf_op jit(solution)/shard_map/ppermute | solution.py:472
  15.5 6.0 %copy-start = (s32[8,8]{1,0:T(8,128)S(1)}, s32[8,8]{1,0:T(8,128)}, u32[]{:S(2)}) copy-start(s32[8,8]{1,0:T(8,128)} %refs_1_.1) | copy-start | bytes 772
  20.2 4.9 %collective-permute-start.4 = (f32[128,128]{1,0:T(8,128)S(1)}, f32[128,128]{1,0:T(8,128)S(1)}, u32[]{:S(2)}, u32[]{:S(2)}) collective-permute-start(f32[128,128]{1,0:T(8,128)S(1)} %get-tuple-element.56.refs_0_), channel_id=1, source_target_pairs={{6,4},{14,12},{22,20},{30,28}} | collective-permute-start | bytes 196616 | tf_op jit(solution)/shard_map/ppermute | solution.py:476
  20.9 4.3 %collective-permute-start.3 = (f32[128,128]{1,0:T(8,128)S(1)}, f32[128,128]{1,0:T(8,128)S(1)}, u32[]{:S(2)}, u32[]{:S(2)}) collective-permute-start(f32[128,128]{1,0:T(8,128)S(1)} %get-tuple-element.56.refs_0_), channel_id=1, source_target_pairs={{2,4},{10,12},{18,20},{26,28}} | collective-permute-start | bytes 196616 | tf_op jit(solution)/shard_map/ppermute | solution.py:476
  25.5 4.6 %collective-permute-start.6 = (f32[128,128]{1,0:T(8,128)S(1)}, f32[128,128]{1,0:T(8,128)S(1)}, u32[]{:S(2)}, u32[]{:S(2)}) collective-permute-start(f32[128,128]{1,0:T(8,128)S(1)} %get-tuple-element.62.refs_0_), channel_id=1, source_target_pairs={{12,8},{28,24}} | collective-permute-start | bytes 196616 | tf_op jit(solution)/shard_map/ppermute | solution.py:476
  26.2 3.9 %collective-permute-start.5 = (f32[128,128]{1,0:T(8,128)S(1)}, f32[128,128]{1,0:T(8,128)S(1)}, u32[]{:S(2)}, u32[]{:S(2)}) collective-permute-start(f32[128,128]{1,0:T(8,128)S(1)} %get-tuple-element.62.refs_0_), channel_id=1, source_target_pairs={{4,8},{20,24}} | collective-permute-start | bytes 196616 | tf_op jit(solution)/shard_map/ppermute | solution.py:476
  30.5 8.7 %collective-permute-start.8 = (f32[128,128]{1,0:T(8,128)S(1)}, f32[128,128]{1,0:T(8,128)S(1)}, u32[]{:S(2)}, u32[]{:S(2)}) collective-permute-start(f32[128,128]{1,0:T(8,128)S(1)} %get-tuple-element.68.refs_0_), channel_id=1, source_target_pairs={{24,16},{8,0}} | collective-permute-start | bytes 196616 | tf_op jit(solution)/shard_map/ppermute | solution.py:476
  31.8 11.1 %collective-permute-start.7 = (f32[128,128]{1,0:T(8,128)S(1)}, f32[128,128]{1,0:T(8,128)S(1)}, u32[]{:S(2)}, u32[]{:S(2)}) collective-permute-start(f32[128,128]{1,0:T(8,128)S(1)} %get-tuple-element.68.refs_0_), channel_id=1, source_target_pairs={{8,16},{24,0}} | collective-permute-start | bytes 196616 | tf_op jit(solution)/shard_map/ppermute | solution.py:476

commit v4 on v3

--- a/solution.py
+++ b/solution.py
@@ -154,7 +154,7 @@
 
 def local_kernel(
     counts_in, coords_in, proxies_in, leaf_in, node_in,
-    basis_ref, gram_ref, heads_ref, message_ref, move_ref, columns_ref,
+    basis_ref, gram_ref, heads_ref, weight_ref, message_ref, move_ref, columns_ref,
     counts, coords, proxies, leaf_t, node_t, sems,
 ):
     pairs = ((counts_in, counts), (coords_in, coords), (proxies_in, proxies), (leaf_in, leaf_t), (node_in, node_t))
@@ -172,7 +172,7 @@
         span = slice(leaf * WIDTH, leaf * WIDTH + WIDTH)
         own = coords[:, span]
         valid = lane < counts[leaf]
-        at = WIDTH + 3 * leaf
+        at = 3 * leaf
         message_ref[at : at + 1, :] = jnp.where(valid, own[0:1], -far)
         message_ref[at + 1 : at + 3, :] = own[1:3]
         turned = jnp.concatenate([jnp.where(valid, own[0:1], far), own[1:3], jnp.zeros((5, WIDTH), f32)], axis=0).T
@@ -200,18 +200,15 @@
             following.append(lift(node_t[k * 2**level + 2 ** (level - 1)], head))
         weights = following
         level += 1
-    message_ref[0:WIDTH, :] = weights[0]
-
-
-def lift_kernel(left, right, move, chosen_in, *rest, level):
-    weight_ref, chosen_ref = rest[-2:]
-    span = slice(0, WIDTH)
-    head = left[span, :] + right[span, :] + unit(ridge)
+    weight_ref[...] = weights[0]
+
+
+def lift_kernel(left, right, move, chosen_in, token, weight_ref, chosen_ref, *, level):
+    del token
+    head = left[...] + right[...] + unit(ridge)
     mine = position() % (2 ** (level + 1)) == 2**level
-    chosen_ref[...] = jnp.where(mine, head, chosen_in[span, :])
-    weight_ref[span, :] = lift(move[...], head)
-    if weight_ref.shape[0] > WIDTH:
-        weight_ref[WIDTH:, :] = right[WIDTH:, :]
+    chosen_ref[...] = jnp.where(mine, head, chosen_in[...])
+    weight_ref[...] = lift(move[...], head)
 
 
 def node_slots():
@@ -237,43 +234,8 @@
             copy.wait()
 
 
-def near_part(near, flush, tiles_in, near_out, operands, tiles_out, wide, copies):
-    for n, leaf in enumerate(flush):
-        copies.start(tiles_in.at[n], near_out.at[leaf])
-    if not near:
-        return lambda t: None
-    ids, message, low, high, columns = operands
-    size = message.shape[0] - WIDTH
-    leaves, fan = ids.shape[1], ids.shape[0]
-    for n, ref in enumerate((low, message, high)):
-        wide[n * size : (n + 1) * size, :] = ref[WIDTH:, :]
-    offset = (position() - 1) * leaves
-    shape = (WIDTH, WIDTH)
-
-    def tile(t):
-        if t >= len(near) * fan:
-            return
-        at, n = divmod(t, fan)
-        leaf = near[at]
-        other = wide[pl.ds(3 * (ids[n, leaf] - offset), 3), :]
-        value = matern(*(columns[leaf, d] - jnp.broadcast_to(other[d : d + 1], shape) for d in range(3)))
-        tiles_out[at, n] = value.astype(bf16)
-
-    return tile
-
-
-def work_kernel(*refs, names, steps, near, flush, final):
+def work_kernel(*refs, names, steps, final):
     ref = dict(zip(names, refs))
-    copies = Copies(ref["sems"])
-    tile = near_part(
-        near, flush, ref.get("tiles_in"), ref.get("near_out"),
-        [ref.get(n) for n in ("ids", "message", "low", "high", "columns")],
-        ref.get("tiles_out"), ref.get("wide"), copies,
-    )
-    fan = ref["ids"].shape[0] if near else 0
-    total = len(near) * fan
-    share = -(-total // max(1, 2 * len(steps)))
-    done = 0
     held = ({}, {})
     for s in steps:
         for side, name in enumerate(("leaf", "node")):
@@ -295,41 +257,55 @@
                 return put_row
 
             eliminate(s, get, put, store(name + "_r"), store("leaf_s") if name == "leaf" else None)
-            for t in range(done, done + share):
-                tile(t)
-            done += share
     for side, name in enumerate(("leaf", "node")):
         if name + "_out" in ref:
             for i in range(STEP * (steps[-1] + 1), WIDTH):
                 ref[name + "_out"][GROUP * i : GROUP * (i + 1), :] = held[side][i]
-    if final:
-        parts = {
-            kind: [ref[f"{kind}{n}"] for n in range(final)] for kind in ("leaf_r", "leaf_s", "node_r")
-        }
-        upper = iota((WIDTH, WIDTH), 1) >= iota((WIDTH, WIDTH), 0)
-        lower = iota((WIDTH, WIDTH), 1) <= iota((WIDTH, WIDTH), 0)
-
-        def whole(kind, b):
-            return jnp.concatenate([stacked(part, b) for part in parts[kind]], axis=0)
-
-        for b in range(GROUP):
-            turned = jnp.where(lower, whole("leaf_s", b), 0.0)
-            ref["bases"][b * WIDTH : (b + 1) * WIDTH, :] = product(ref["basis"][b], turned, 1, 1).astype(bf16)
-            ref["factors"][b] = jnp.where(upper, whole("leaf_r", b), 0.0)
-            copies.start(ref["factors"].at[b], ref["leaf_factors"].at[b])
-            if b < GROUP - 1:
-                ref["nodes"][b] = jnp.where(upper, whole("node_r", b), 0.0)
-                copies.start(ref["nodes"].at[b], ref["node_factors"].at[node_slots()[b]])
-        copies.start(ref["bases"], ref["leaf_bases"])
-        for t in range(total):
-            tile(t)
+    if "own" in ref:
+        ref["own"][...] = ref["message"][...]
+    if not final:
+        return
+    copies = Copies(ref["sems"])
+    parts = {kind: [ref[f"{kind}{n}"] for n in range(final)] for kind in ("leaf_r", "leaf_s", "node_r")}
+    upper = iota((WIDTH, WIDTH), 1) >= iota((WIDTH, WIDTH), 0)
+    lower = iota((WIDTH, WIDTH), 1) <= iota((WIDTH, WIDTH), 0)
+
+    def whole(kind, b):
+        return jnp.concatenate([stacked(part, b) for part in parts[kind]], axis=0)
+
+    for b in range(GROUP):
+        ref["factors"][b] = jnp.where(upper, whole("leaf_r", b), 0.0)
+        copies.start(ref["factors"].at[b], ref["leaf_factors"].at[b])
+        if b < GROUP - 1:
+            ref["nodes"][b] = jnp.where(upper, whole("node_r", b), 0.0)
+            copies.start(ref["nodes"].at[b], ref["node_factors"].at[node_slots()[b]])
+    for b in range(GROUP):
+        span = pl.ds(b * WIDTH, WIDTH)
+        turned = jnp.where(lower, whole("leaf_s", b), 0.0)
+        ref["bases"][span, :] = product(ref["basis"][b], turned, 1, 1).astype(bf16)
+        copies.start(ref["bases"].at[span, :], ref["leaf_bases"].at[span, :])
     copies.wait()
 
 
-def top_kernel(*refs, names, flush, half):
+def top_kernel(*refs, names, half):
     ref = dict(zip(names, refs))
     copies = Copies(ref["sems"])
-    near_part((), flush, ref["tiles_in"], ref["near_out"], None, None, None, copies)
+    ids, columns, tiles, wide = ref["ids"], ref["columns"], ref["tiles"], ref["wide"]
+    leaves, fan = ids.shape[1], ids.shape[0]
+    size = ref["own"].shape[0]
+    for n, name in enumerate(("low", "own", "high")):
+        wide[n * size : (n + 1) * size, :] = ref[name][...]
+    offset = (position() - 1) * leaves
+
+    def tile(t):
+        leaf, n = divmod(t, fan)
+        other = wide[pl.ds(3 * (ids[n, leaf] - offset), 3), :]
+        shape = (WIDTH, WIDTH)
+        value = matern(*(columns[leaf, d] - jnp.broadcast_to(other[d : d + 1], shape) for d in range(3)))
+        tiles[leaf, n] = value.astype(bf16)
+        if n == fan - 1:
+            copies.start(tiles.at[leaf], ref["near_out"].at[leaf])
+
     left, right, chosen = ref["left"], ref["right"], ref["chosen"]
     top = jnp.where(position() % half == 0, left[...] + right[...] + unit(ridge), chosen[...])
     values = {}
@@ -346,8 +322,12 @@
     def put_r(i, value):
         target[i : i + 1, :] = jnp.where(lane >= i, value[0:1, :], 0.0)
 
+    total = leaves * fan
+    share = -(-total // (STEPS - 2))
     for s in range(STEPS):
         eliminate(s, get, put, put_r, None)
+        for t in range(s * share, min((s + 1) * share, total)):
+            tile(t)
     copies.start(target, ref["node_out"].at[0])
     copies.wait()
 
@@ -382,13 +362,14 @@
     mat = shape((WIDTH, WIDTH), f32)
     mats = shape((leaves, WIDTH, WIDTH), f32)
     flat = shape((WIDTH * GROUP, WIDTH), f32)
-    long = shape((WIDTH + 3 * leaves, WIDTH), f32)
-
-    basis, gram, heads, message, move, columns = pl.pallas_call(
+    coords_shape = shape((3 * leaves, WIDTH), f32)
+    halo_level = 3
+
+    basis, gram, heads, weight_own, message, move, columns = pl.pallas_call(
         local_kernel,
-        out_shape=(mats, flat, flat, long, mat, shape((leaves, 3, slots, WIDTH), f32)),
+        out_shape=(mats, flat, flat, mat, coords_shape, mat, shape((leaves, 3, slots, WIDTH), f32)),
         in_specs=[anywhere] * 5,
-        out_specs=(vmem,) * 6,
+        out_specs=(vmem,) * 7,
         scratch_shapes=[
             pltpu.SMEM(counts.shape, jnp.int32),
             pltpu.VMEM(coords.shape, f32),
@@ -402,104 +383,90 @@
         name="local",
     )(*(pltpu.with_memory_space_constraint(x, pltpu.HBM) for x in (counts, coords, proxies, leaf_transfers, node_transfers)))
 
-    plan = [
-        dict(steps=(0, 1, 2, 3), near=()),
-        dict(steps=(4, 5, 6, 7), near=()),
-        dict(steps=(8, 9, 10, 11), near=(0, 1, 2)),
-        dict(steps=(12, 13, 14, 15), near=(3, 4, 5)),
-        dict(steps=(), near=tuple(range(6, leaves))),
-    ]
-    state = dict(leaf=gram, node=heads, parts=[], tiles=None, flush=(), near_out=None)
-
-    def work(n, after, low, high):
-        steps, near = plan[n]["steps"], plan[n]["near"]
+    plan = [(0, 1, 2, 3), (4, 5, 6, 7), (8, 9, 10, 11), (12, 13, 14, 15), ()]
+    state = dict(leaf=gram, node=heads)
+    parts = []
+
+    def work(n, after):
+        steps = plan[n]
         final = n == len(plan) - 1
-        flush = state["flush"]
         operands = [("after", after, anywhere)]
-        outs, scratch, aliases = [], [], {}
+        outs, scratch = [], []
         if steps:
             rows = shape((STEP * len(steps) * GROUP, WIDTH), f32)
             operands += [("leaf_in", state["leaf"], vmem), ("node_in", state["node"], vmem)]
             outs += [(kind, rows, vmem) for kind in ("leaf_r", "leaf_s", "node_r")]
             if steps[-1] + 1 < STEPS:
                 outs += [("leaf_out", flat, vmem), ("node_out", flat, vmem)]
-        if near:
-            operands += [("ids", neighbours, smem), ("message", message, vmem), ("low", low, vmem)]
-            operands += [("high", high, vmem), ("columns", columns, vmem)]
-            outs.append(("tiles_out", shape((len(near), fan, slots, slots), bf16), vmem))
-            scratch.append(("wide", pltpu.VMEM((9 * leaves, WIDTH), f32)))
-        if flush:
-            operands.append(("tiles_in", state["tiles"], vmem))
-            outs.append(("near_out", shape((leaves, fan, slots, slots), bf16), anywhere))
-            if state["near_out"] is not None:
-                operands.append(("near_in", state["near_out"], anywhere))
-                aliases["near_in"] = "near_out"
+        if n == halo_level:
+            operands.append(("message", message, vmem))
+            outs.append(("own", coords_shape, vmem))
         if final:
-            for k, part in enumerate(state["parts"]):
+            for k, part in enumerate(parts):
                 operands += [(f"{kind}{k}", part[kind], vmem) for kind in ("leaf_r", "leaf_s", "node_r")]
             operands.append(("basis", basis, vmem))
             outs += [("leaf_factors", mats, anywhere), ("node_factors", mats, anywhere)]
             outs.append(("leaf_bases", shape((leaves * slots, WIDTH), bf16), anywhere))
             scratch += [("factors", pltpu.VMEM(mats.shape, f32)), ("nodes", pltpu.VMEM(mats.shape, f32))]
             scratch.append(("bases", pltpu.VMEM((leaves * slots, WIDTH), bf16)))
-        scratch.append(("sems", pltpu.SemaphoreType.DMA((32,))))
+            scratch.append(("sems", pltpu.SemaphoreType.DMA((3 * GROUP,))))
         made = call(
-            work_kernel, operands, outs, scratch, aliases, 3, f"work{n}",
-            steps=steps, near=near, flush=flush, final=len(state["parts"]) if final else 0,
+            work_kernel, operands, outs, scratch, {}, 3, f"work{n}",
+            steps=steps, final=len(parts) if final else 0,
         )
         if steps:
-            state["parts"].append(made)
+            parts.append(made)
             state["leaf"], state["node"] = made.get("leaf_out"), made.get("node_out")
-        state["tiles"], state["flush"] = made.get("tiles_out"), near
-        state["near_out"] = made.get("near_out", state["near_out"])
         return made
 
-    up = [(i, i + 1) for i in range(count - 1)]
-    weight = chosen = message
-    low = high = made = None
+    weight = chosen = weight_own
+    made = low = high = own = None
     for level in range(levels):
         span = 2 ** (level + 1)
         quarter = span // 4
-        first = [(i + quarter, i + 2 * quarter) for i in range(0, count, span)]
-        second = [(i + 3 * quarter, i + 2 * quarter) for i in range(0, count, span)]
-        if level + 1 == levels:
-            first.append((3 * quarter, 0))
-            second.append((quarter, 0))
         if level == 0:
-            left, right = lax.ppermute(weight, both, up), weight
-            low = left
-        elif level == 1:
-            left = lax.ppermute(weight, both, first)
-            right = lax.ppermute(weight, both, [(target, source) for source, target in up])
-            high = right
+            left, right = lax.ppermute(weight, both, [(i, i + 1) for i in range(0, count, 2)]), weight
         else:
+            first = [(i + quarter, i + 2 * quarter) for i in range(0, count, span)]
+            second = [(i + 3 * quarter, i + 2 * quarter) for i in range(0, count, span)]
+            if level + 1 == levels:
+                first.append((3 * quarter, 0))
+                second.append((quarter, 0))
             left, right = lax.ppermute(weight, both, first), lax.ppermute(weight, both, second)
         if level < len(plan):
-            made = work(level, weight, low, high)
+            made = work(level, weight)
+        if level == halo_level:
+            own = made["own"]
+            up = [(i, i + 1) for i in range(count - 1)]
+            low = lax.ppermute(own, both, up)
+            high = lax.ppermute(own, both, [(target, source) for source, target in up])
         if level + 1 < levels:
-            outs = [("weight", long if level == 0 else mat, vmem), ("chosen_out", mat, vmem)]
-            token = next(iter(made.values()))
             weight, chosen = pl.pallas_call(
                 functools.partial(lift_kernel, level=level),
-                out_shape=[o[1] for o in outs],
+                out_shape=[mat, mat],
                 in_specs=[vmem] * 4 + [anywhere],
                 out_specs=[vmem] * 2,
                 compiler_params=params,
                 cost_estimate=cost(0.4),
                 name=f"lift{level}",
-            )(left, right, move, chosen, token)
+            )(left, right, move, chosen, next(iter(made.values())))
 
     top = call(
         top_kernel,
         [
-            ("left", left, vmem), ("right", right, vmem), ("chosen", chosen, vmem),
-            ("tiles_in", state["tiles"], vmem), ("near_in", state["near_out"], anywhere),
+            ("left", left, vmem), ("right", right, vmem), ("chosen", chosen, vmem), ("ids", neighbours, smem),
+            ("own", own, vmem), ("low", low, vmem), ("high", high, vmem), ("columns", columns, vmem),
             ("node_in", made["node_factors"], anywhere),
         ],
         [("near_out", shape((leaves, fan, slots, slots), bf16), anywhere), ("node_out", mats, anywhere)],
-        [("factor", pltpu.VMEM((WIDTH, WIDTH), f32)), ("sems", pltpu.SemaphoreType.DMA((16,)))],
-        {"near_in": "near_out", "node_in": "node_out"},
-        5, "top", flush=state["flush"], half=half,
+        [
+            ("factor", pltpu.VMEM((WIDTH, WIDTH), f32)),
+            ("tiles", pltpu.VMEM((leaves, fan, slots, slots), bf16)),
+            ("wide", pltpu.VMEM((9 * leaves, WIDTH), f32)),
+            ("sems", pltpu.SemaphoreType.DMA((leaves + 1,))),
+        ],
+        {"node_in": "node_out"},
+        6, "top", half=half,
     )
     return (top["near_out"], made["leaf_bases"], made["leaf_factors"], top["node_out"])
 

time: 48.9 us -> 49.3 us (level)
  starting transfers between devices: 12.2 us -> 20.3 us
  waiting for transfers between devices: 8.8 us -> 2.9 us
  Pallas kernels: 26.6 us -> 24.7 us
    ppermute x3, starting transfers between devices: 6.8 us -> 13.6 us  [the longest x1 7.44 us: shards(): low = lax.ppermute(own, both, up)]
    ppermute x3 -> x4, waiting for transfers between devices: 3.41 us -> 0.01 us  [shards(): lax.ppermute(weight, both, second)]
    pallas_call x6, Pallas kernels: 20.4 us -> 18.5 us  [call(): pl.pallas_call(functools.partial(body, names=names, **static), out_shape=...]
    ppermute x3, waiting for transfers between devices: 1.75 us -> 0.01 us  [the longest x1 0.01 us: shards(): lax.ppermute(weight, both, [(i, i + 1) for i in range(0, count, 2)])]
    ppermute x3 -> x4, waiting for transfers between devices: 3.63 us -> 2.89 us  [shards(): lax.ppermute(weight, both, first)]
    ppermute x3 -> x4, starting transfers between devices: 2.8 us -> 3.47 us  [shards(): lax.ppermute(weight, both, first)]
    ppermute x3 -> x4, starting transfers between devices: 2.62 us -> 3.29 us  [shards(): lax.ppermute(weight, both, second)]
  transfers between devices with their start and end apart: 9 -> 11, of which waited for: 3 -> 1; matrix products, arithmetic and copies ran while one was open for 0% -> 0% of each run, Pallas kernels for 30% -> 21%
where the time goes in v4:
time: 49.3 us; the launch traced here: 49 us
  Pallas kernels  24.7 us (50%)
  starting transfers between devices  20.3 us (41%)
  waiting for transfers between devices  2.9 us (6%)
  between operations  1.04 us (2%)
    pallas_call x6, Pallas kernels, call(): pl.pallas_call(functools.partial(body, names=names, **static), out_shape=...  18.5 us
    ppermute x1, starting transfers between devices, shards(): low = lax.ppermute(own, both, up)  7.44 us
    ppermute x1, starting transfers between devices, shards(): lax.ppermute(weight, both, [(i, i + 1) for i in range(0, count, 2)])  4.84 us
    pallas_call x1, Pallas kernels, shards(): pl.pallas_call(local_kernel, out_shape=(mats, flat, flat, mat, coords_sha...  4.81 us
    ppermute x4, starting transfers between devices, shards(): lax.ppermute(weight, both, first)  3.47 us
    ppermute x4, starting transfers between devices, shards(): lax.ppermute(weight, both, second)  3.29 us
    ppermute x4, waiting for transfers between devices, shards(): lax.ppermute(weight, both, first)  2.89 us
    pallas_call x4, Pallas kernels, shards(): pl.pallas_call(functools.partial(lift_kernel, level=level), out_shape=[ma...  1.39 us
  transfers between devices with their start and end apart: 11, of which 1 were waited for; matrix products, arithmetic and copies ran while one was open for 0% of the time, Pallas kernels for 21%

profile of v4, /device:TPU:0, one launch (start us, length us, event | category | flops | bytes accessed | tf_op | source)
XLA Modules:
  0.0 49.0 jit_solution(14631533802766521864)
XLA Ops:
  0.6 4.8 %local.1 = (f32[8,128,128]{2,1,0:T(8,128)S(1)}, f32[1024,128]{1,0:T(8,128)S(1)}, f32[1024,128]{1,0:T(8,128)S(1)}, f32[128,128]{1,0:T(8,128)S(1)}, f32[24,128]{1,...) custom-call(s32[8]{0:T(128)} %counts_in.1, f32[3,1024]{1,0:T(4,128)} %coords_in.1, ...), custom_call_target="tpu_custom_call" | custom-call | flops 4000000000 | bytes 12000000 | tf_op jit(solution)/shard_map/local/pallas_call | solution.py:368
  5.5 4.8 %collective-permute-start = (f32[128,128]{1,0:T(8,128)S(1)}, f32[128,128]{1,0:T(8,128)S(1)}, u32[]{:S(2)}, u32[]{:S(2)}) collective-permute-start(f32[128,128]{1,0:T(8,128)S(1)} %get-tuple-element.43.refs_0_.right.chosen_in), channel_id=1, source_target_pairs={{0,1},{2,3},{4,5},{6,7},{8,9},{10,11},{12,13},{14,15},{16,17},{18,... | collective-permute-start | bytes 196616 | tf_op jit(solution)/shard_map/ppermute | solution.py:428
  10.3 2.6 %work0.1 = (f32[256,128]{1,0:T(8,128)S(1)}, f32[256,128]{1,0:T(8,128)S(1)}, f32[256,128]{1,0:T(8,128)S(1)}, f32[1024,128]{1,0:T(8,128)S(1)}, f32[1024,128]{1,0:T(8,128)S(1)}) custom-call(f32[128,128]{1,0:T(8,128)S(1)} %get-tuple-element.43.refs_0_.right.chosen_in, f32[1024,128]{1,0:T(8,128)S(1)} %get-tuple-element.45.refs_1_, ...), custom_call_target="tpu_custom_call" | custom-call | flops 3000000000 | bytes 9000000 | tf_op jit(solution)/shard_map/work0/pallas_call | solution.py:339
  12.9 0.3 lift0.1
  13.2 0.7 %collective-permute-start.2 = (f32[128,128]{1,0:T(8,128)S(1)}, f32[128,128]{1,0:T(8,128)S(1)}, u32[]{:S(2)}, u32[]{:S(2)}) collective-permute-start(f32[128,128]{1,0:T(8,128)S(1)} %get-tuple-element.48.refs_0_), channel_id=1, source_target_pairs={{3,2},{7,6},{11,10},{15,14},{19,18},{23,22},{27,26},{31,30}} | collective-permute-start | bytes 196616 | tf_op jit(solution)/shard_map/ppermute | solution.py:435
  13.9 0.7 %collective-permute-start.1 = (f32[128,128]{1,0:T(8,128)S(1)}, f32[128,128]{1,0:T(8,128)S(1)}, u32[]{:S(2)}, u32[]{:S(2)}) collective-permute-start(f32[128,128]{1,0:T(8,128)S(1)} %get-tuple-element.48.refs_0_), channel_id=1, source_target_pairs={{1,2},{5,6},{9,10},{13,14},{17,18},{21,22},{25,26},{29,30}} | collective-permute-start | bytes 196616 | tf_op jit(solution)/shard_map/ppermute | solution.py:435
  14.6 2.3 %work1.1 = (f32[256,128]{1,0:T(8,128)S(1)}, f32[256,128]{1,0:T(8,128)S(1)}, f32[256,128]{1,0:T(8,128)S(1)}, f32[1024,128]{1,0:T(8,128)S(1)}, f32[1024,128]{1,0:T(8,128)S(1)}) custom-call(f32[128,128]{1,0:T(8,128)S(1)} %get-tuple-element.48.refs_0_, f32[1024,128]{1,0:T(8,128)S(1)} %get-tuple-element.50.refs_1_, f32[1024,128]{1,0:T(8,128)S(1)} %get-tuple-element.51.refs_2_), custom_call_target="tpu_custom_call" | custom-call | flops 3000000000 | bytes 9000000 | tf_op jit(solution)/shard_map/work1/pallas_call | solution.py:339
  16.9 0.3 lift1.1
  17.2 0.7 %collective-permute-start.4 = (f32[128,128]{1,0:T(8,128)S(1)}, f32[128,128]{1,0:T(8,128)S(1)}, u32[]{:S(2)}, u32[]{:S(2)}) collective-permute-start(f32[128,128]{1,0:T(8,128)S(1)} %get-tuple-element.53.refs_0_), channel_id=1, source_target_pairs={{6,4},{14,12},{22,20},{30,28}} | collective-permute-start | bytes 196616 | tf_op jit(solution)/shard_map/ppermute | solution.py:435
  17.9 0.7 %collective-permute-start.3 = (f32[128,128]{1,0:T(8,128)S(1)}, f32[128,128]{1,0:T(8,128)S(1)}, u32[]{:S(2)}, u32[]{:S(2)}) collective-permute-start(f32[128,128]{1,0:T(8,128)S(1)} %get-tuple-element.53.refs_0_), channel_id=1, source_target_pairs={{2,4},{10,12},{18,20},{26,28}} | collective-permute-start | bytes 196616 | tf_op jit(solution)/shard_map/ppermute | solution.py:435
  18.6 1.9 %work2.1 = (f32[256,128]{1,0:T(8,128)S(1)}, f32[256,128]{1,0:T(8,128)S(1)}, f32[256,128]{1,0:T(8,128)S(1)}, f32[1024,128]{1,0:T(8,128)S(1)}, f32[1024,128]{1,0:T(8,128)S(1)}) custom-call(f32[128,128]{1,0:T(8,128)S(1)} %get-tuple-element.53.refs_0_, f32[1024,128]{1,0:T(8,128)S(1)} %get-tuple-element.55.refs_1_, f32[1024,128]{1,0:T(8,128)S(1)} %get-tuple-element.56.refs_2_), custom_call_target="tpu_custom_call" | custom-call | flops 3000000000 | bytes 9000000 | tf_op jit(solution)/shard_map/work2/pallas_call | solution.py:339
  20.5 0.3 lift2.1
  20.9 0.7 %collective-permute-start.6 = (f32[128,128]{1,0:T(8,128)S(1)}, f32[128,128]{1,0:T(8,128)S(1)}, u32[]{:S(2)}, u32[]{:S(2)}) collective-permute-start(f32[128,128]{1,0:T(8,128)S(1)} %get-tuple-element.58.refs_0_), channel_id=1, source_target_pairs={{12,8},{28,24}} | collective-permute-start | bytes 196616 | tf_op jit(solution)/shard_map/ppermute | solution.py:435
  21.6 0.7 %collective-permute-start.5 = (f32[128,128]{1,0:T(8,128)S(1)}, f32[128,128]{1,0:T(8,128)S(1)}, u32[]{:S(2)}, u32[]{:S(2)}) collective-permute-start(f32[128,128]{1,0:T(8,128)S(1)} %get-tuple-element.58.refs_0_), channel_id=1, source_target_pairs={{4,8},{20,24}} | collective-permute-start | bytes 196616 | tf_op jit(solution)/shard_map/ppermute | solution.py:435
  22.2 1.4 %work3.1 = (f32[256,128]{1,0:T(8,128)S(1)}, f32[256,128]{1,0:T(8,128)S(1)}, f32[256,128]{1,0:T(8,128)S(1)}, f32[24,128]{1,0:T(8,128)S(1)}) custom-call(f32[128,128]{1,0:T(8,128)S(1)} %get-tuple-element.58.refs_0_, f32[1024,128]{1,0:T(8,128)S(1)} %get-tuple-element.60.refs_1_, f32[1024,128]{1,0:T(8,128)S(1)} %get-tuple-element.61.refs_2_, ...), custom_call_target="tpu_custom_call" | custom-call | flops 3000000000 | bytes 9000000 | tf_op jit(solution)/shard_map/work3/pallas_call | solution.py:339
  23.6 1.3 %collective-permute-start.10 = (f32[24,128]{1,0:T(8,128)S(1)}, f32[24,128]{1,0:T(8,128)S(1)}, u32[]{:S(2)}, u32[]{:S(2)}) collective-permute-start(f32[24,128]{1,0:T(8,128)S(1)} %get-tuple-element.66.refs_4_), channel_id=1, source_target_pairs={{1,0},{2,1},{3,2},{4,3},{5,4},{6,5},{7,6},{8,7},{9,8},{10,9},{11,1... | collective-permute-start | bytes 36872 | tf_op jit(solution)/shard_map/ppermute | solution.py:442
  24.9 7.4 %collective-permute-start.9 = (f32[24,128]{1,0:T(8,128)S(1)}, f32[24,128]{1,0:T(8,128)S(1)}, u32[]{:S(2)}, u32[]{:S(2)}) collective-permute-start(f32[24,128]{1,0:T(8,128)S(1)} %get-tuple-element.66.refs_4_), channel_id=1, source_target_pairs={{0,1},{1,2},{2,3},{3,4},{4,5},{5,6},{6,7},{7,8},{8,9},{9,10},{10,1... | collective-permute-start | bytes 36872 | tf_op jit(solution)/shard_map/ppermute | solution.py:441
  32.4 0.3 lift3.1
  32.7 1.3 %collective-permute-start.8 = (f32[128,128]{1,0:T(8,128)S(1)}, f32[128,128]{1,0:T(8,128)S(1)}, u32[]{:S(2)}, u32[]{:S(2)}) collective-permute-start(f32[128,128]{1,0:T(8,128)S(1)} %get-tuple-element.64.refs_0_), channel_id=1, source_target_pairs={{24,16},{8,0}} | collective-permute-start | bytes 196616 | tf_op jit(solution)/shard_map/ppermute | solution.py:435
  34.0 1.5 %collective-permute-start.7 = (f32[128,128]{1,0:T(8,128)S(1)}, f32[128,128]{1,0:T(8,128)S(1)}, u32[]{:S(2)}, u32[]{:S(2)}) collective-permute-start(f32[128,128]{1,0:T(8,128)S(1)} %get-tuple-element.64.refs_0_), channel_id=1, source_target_pairs={{8,16},{24,0}} | collective-permute-start | bytes 196616 | tf_op jit(solution)/shard_map/ppermute | solution.py:435
  35.5 0.0 copy-start
  35.5 1.7 %work4.1 = (f32[8,128,128]{2,1,0:T(8,128)}, f32[8,128,128]{2,1,0:T(8,128)}, bf16[1024,128]{1,0:T(8,128)(2,1)}) custom-call(f32[128,128]{1,0:T(8,128)S(1)} %get-tuple-element.64.refs_0_, f32[256,128]{1,0:T(8,128)S(1)} %get-tuple-element.47.token.refs_1_, f32[256,128]{1,0:T(8,128)S(1)} %get-tuple-element.68.refs_2_, f32[256,128]{1,0:T(8,128)S(1)} %get-tuple-element.69.refs_3_, ...), custom_call_target="tpu_custom_call" | custom-call | flops 3000000000 | bytes 9000000 | tf_op jit(solution)/shard_map/work4/pallas_call | solution.py:339
  37.3 2.9 %collective-permute-done.7.refs_0_ = f32[128,128]{1,0:T(8,128)S(1)} collective-permute-done((f32[128,128]{1,0:T(8,128)S(1)}, f32[128,128]{1,0:T(8,128)S(1)}, u32[]{:S(2)}, u32[]{:S(2)}) %collective-permute-start.7) | collective-permute-done | bytes 65568 | tf_op jit(solution)/shard_map/ppermute | solution.py:435
  40.2 8.7 %top.1 = (bf16[8,8,128,128]{3,2,1,0:T(8,128)(2,1)}, f32[8,128,128]{2,1,0:T(8,128)}) custom-call(f32[128,128]{1,0:T(8,128)S(1)} %collective-permute-done.7.refs_0_, f32[128,128]{1,0:T(8,128)S(1)} %collective-permute-done.8.refs_1_, f32[128,128]{1,0:T(8,128)S(1)} %get-tuple-element.65.refs_2_, s32[8,8]{1,0:T(8,128)S(1)} %copy-done, ...), custom_call_target="tpu_custom_call", output_to_operand_aliasing={{1}: (8, {})} | custom-call | flops 6000000000 | bytes 18000000 | tf_op jit(solution)/shard_map/top/pallas_call | solution.py:339
  (11 shorter events, 0.0 us)
Async XLA Ops:
  5.5 7.4 %collective-permute-start = (f32[128,128]{1,0:T(8,128)S(1)}, f32[128,128]{1,0:T(8,128)S(1)}, u32[]{:S(2)}, u32[]{:S(2)}) collective-permute-start(f32[128,128]{1,0:T(8,128)S(1)} %get-tuple-element.43.refs_0_.right.chosen_in), channel_id=1, source_target_pairs={{0,1},{2,3},{4,5},{6,7},{8,9},{10,11},{12,13},{14,15},{16,17},{18,... | collective-permute-start | bytes 196616 | tf_op jit(solution)/shard_map/ppermute | solution.py:428
  13.2 3.6 %collective-permute-start.2 = (f32[128,128]{1,0:T(8,128)S(1)}, f32[128,128]{1,0:T(8,128)S(1)}, u32[]{:S(2)}, u32[]{:S(2)}) collective-permute-start(f32[128,128]{1,0:T(8,128)S(1)} %get-tuple-element.48.refs_0_), channel_id=1, source_target_pairs={{3,2},{7,6},{11,10},{15,14},{19,18},{23,22},{27,26},{31,30}} | collective-permute-start | bytes 196616 | tf_op jit(solution)/shard_map/ppermute | solution.py:435
  13.9 2.9 %collective-permute-start.1 = (f32[128,128]{1,0:T(8,128)S(1)}, f32[128,128]{1,0:T(8,128)S(1)}, u32[]{:S(2)}, u32[]{:S(2)}) collective-permute-start(f32[128,128]{1,0:T(8,128)S(1)} %get-tuple-element.48.refs_0_), channel_id=1, source_target_pairs={{1,2},{5,6},{9,10},{13,14},{17,18},{21,22},{25,26},{29,30}} | collective-permute-start | bytes 196616 | tf_op jit(solution)/shard_map/ppermute | solution.py:435
  17.2 3.3 %collective-permute-start.4 = (f32[128,128]{1,0:T(8,128)S(1)}, f32[128,128]{1,0:T(8,128)S(1)}, u32[]{:S(2)}, u32[]{:S(2)}) collective-permute-start(f32[128,128]{1,0:T(8,128)S(1)} %get-tuple-element.53.refs_0_), channel_id=1, source_target_pairs={{6,4},{14,12},{22,20},{30,28}} | collective-permute-start | bytes 196616 | tf_op jit(solution)/shard_map/ppermute | solution.py:435
  17.9 2.6 %collective-permute-start.3 = (f32[128,128]{1,0:T(8,128)S(1)}, f32[128,128]{1,0:T(8,128)S(1)}, u32[]{:S(2)}, u32[]{:S(2)}) collective-permute-start(f32[128,128]{1,0:T(8,128)S(1)} %get-tuple-element.53.refs_0_), channel_id=1, source_target_pairs={{2,4},{10,12},{18,20},{26,28}} | collective-permute-start | bytes 196616 | tf_op jit(solution)/shard_map/ppermute | solution.py:435
  20.9 11.5 %collective-permute-start.6 = (f32[128,128]{1,0:T(8,128)S(1)}, f32[128,128]{1,0:T(8,128)S(1)}, u32[]{:S(2)}, u32[]{:S(2)}) collective-permute-start(f32[128,128]{1,0:T(8,128)S(1)} %get-tuple-element.58.refs_0_), channel_id=1, source_target_pairs={{12,8},{28,24}} | collective-permute-start | bytes 196616 | tf_op jit(solution)/shard_map/ppermute | solution.py:435
  21.6 10.8 %collective-permute-start.5 = (f32[128,128]{1,0:T(8,128)S(1)}, f32[128,128]{1,0:T(8,128)S(1)}, u32[]{:S(2)}, u32[]{:S(2)}) collective-permute-start(f32[128,128]{1,0:T(8,128)S(1)} %get-tuple-element.58.refs_0_), channel_id=1, source_target_pairs={{4,8},{20,24}} | collective-permute-start | bytes 196616 | tf_op jit(solution)/shard_map/ppermute | solution.py:435
  23.6 13.7 %collective-permute-start.10 = (f32[24,128]{1,0:T(8,128)S(1)}, f32[24,128]{1,0:T(8,128)S(1)}, u32[]{:S(2)}, u32[]{:S(2)}) collective-permute-start(f32[24,128]{1,0:T(8,128)S(1)} %get-tuple-element.66.refs_4_), channel_id=1, source_target_pairs={{1,0},{2,1},{3,2},{4,3},{5,4},{6,5},{7,6},{8,7},{9,8},{10,9},{11,1... | collective-permute-start | bytes 36872 | tf_op jit(solution)/shard_map/ppermute | solution.py:442
  24.9 12.4 %collective-permute-start.9 = (f32[24,128]{1,0:T(8,128)S(1)}, f32[24,128]{1,0:T(8,128)S(1)}, u32[]{:S(2)}, u32[]{:S(2)}) collective-permute-start(f32[24,128]{1,0:T(8,128)S(1)} %get-tuple-element.66.refs_4_), channel_id=1, source_target_pairs={{0,1},{1,2},{2,3},{3,4},{4,5},{5,6},{6,7},{7,8},{8,9},{9,10},{10,1... | collective-permute-start | bytes 36872 | tf_op jit(solution)/shard_map/ppermute | solution.py:441
  32.7 4.6 %collective-permute-start.8 = (f32[128,128]{1,0:T(8,128)S(1)}, f32[128,128]{1,0:T(8,128)S(1)}, u32[]{:S(2)}, u32[]{:S(2)}) collective-permute-start(f32[128,128]{1,0:T(8,128)S(1)} %get-tuple-element.64.refs_0_), channel_id=1, source_target_pairs={{24,16},{8,0}} | collective-permute-start | bytes 196616 | tf_op jit(solution)/shard_map/ppermute | solution.py:435
  34.0 6.2 %collective-permute-start.7 = (f32[128,128]{1,0:T(8,128)S(1)}, f32[128,128]{1,0:T(8,128)S(1)}, u32[]{:S(2)}, u32[]{:S(2)}) collective-permute-start(f32[128,128]{1,0:T(8,128)S(1)} %get-tuple-element.64.refs_0_), channel_id=1, source_target_pairs={{8,16},{24,0}} | collective-permute-start | bytes 196616 | tf_op jit(solution)/shard_map/ppermute | solution.py:435
  35.5 4.7 %copy-start = (s32[8,8]{1,0:T(8,128)S(1)}, s32[8,8]{1,0:T(8,128)}, u32[]{:S(2)}) copy-start(s32[8,8]{1,0:T(8,128)} %refs_3_.1) | copy-start | bytes 772

commit v5 on v4

--- a/solution.py
+++ b/solution.py
@@ -234,9 +234,35 @@
             copy.wait()
 
 
-def work_kernel(*refs, names, steps, final):
+def near_tiles(ref, near, copies):
+    ids, columns, tiles, wide = ref["ids"], ref["columns"], ref["tiles"], ref["wide"]
+    leaves, fan = ids.shape[1], ids.shape[0]
+    size = ref["own"].shape[0]
+    for n, name in enumerate(("low", "own", "high")):
+        wide[n * size : (n + 1) * size, :] = ref[name][...]
+    offset = (position() - 1) * leaves
+    total = len(near) * fan
+
+    def tile(t):
+        at, n = divmod(t, fan)
+        leaf = near[at]
+        other = wide[pl.ds(3 * (ids[n, leaf] - offset), 3), :]
+        shape = (WIDTH, WIDTH)
+        value = matern(*(columns[leaf, d] - jnp.broadcast_to(other[d : d + 1], shape) for d in range(3)))
+        tiles[at, n] = value.astype(bf16)
+        if n == fan - 1:
+            copies.start(tiles.at[at], ref["near_out"].at[leaf])
+
+    return tile, total
+
+
+def work_kernel(*refs, names, steps, near, final):
     ref = dict(zip(names, refs))
     held = ({}, {})
+    copies = Copies(ref["sems"]) if "sems" in ref else None
+    tile, total = near_tiles(ref, near, copies) if near else (None, 0)
+    done = 0
+    share = -(-total // max(1, len(steps) - 1)) if steps else total
     for s in steps:
         for side, name in enumerate(("leaf", "node")):
             source, values = ref[name + "_in"], held[side]
@@ -257,15 +283,23 @@
                 return put_row
 
             eliminate(s, get, put, store(name + "_r"), store("leaf_s") if name == "leaf" else None)
+            if side == 0:
+                for t in range(done, min(done + share, total)):
+                    tile(t)
+                done += share
     for side, name in enumerate(("leaf", "node")):
         if name + "_out" in ref:
             for i in range(STEP * (steps[-1] + 1), WIDTH):
                 ref[name + "_out"][GROUP * i : GROUP * (i + 1), :] = held[side][i]
-    if "own" in ref:
+    if "message" in ref:
         ref["own"][...] = ref["message"][...]
     if not final:
+        if copies:
+            copies.wait()
         return
-    copies = Copies(ref["sems"])
+    if not steps:
+        for t in range(total):
+            tile(t)
     parts = {kind: [ref[f"{kind}{n}"] for n in range(final)] for kind in ("leaf_r", "leaf_s", "node_r")}
     upper = iota((WIDTH, WIDTH), 1) >= iota((WIDTH, WIDTH), 0)
     lower = iota((WIDTH, WIDTH), 1) <= iota((WIDTH, WIDTH), 0)
@@ -287,25 +321,10 @@
     copies.wait()
 
 
-def top_kernel(*refs, names, half):
+def top_kernel(*refs, names, near, half):
     ref = dict(zip(names, refs))
     copies = Copies(ref["sems"])
-    ids, columns, tiles, wide = ref["ids"], ref["columns"], ref["tiles"], ref["wide"]
-    leaves, fan = ids.shape[1], ids.shape[0]
-    size = ref["own"].shape[0]
-    for n, name in enumerate(("low", "own", "high")):
-        wide[n * size : (n + 1) * size, :] = ref[name][...]
-    offset = (position() - 1) * leaves
-
-    def tile(t):
-        leaf, n = divmod(t, fan)
-        other = wide[pl.ds(3 * (ids[n, leaf] - offset), 3), :]
-        shape = (WIDTH, WIDTH)
-        value = matern(*(columns[leaf, d] - jnp.broadcast_to(other[d : d + 1], shape) for d in range(3)))
-        tiles[leaf, n] = value.astype(bf16)
-        if n == fan - 1:
-            copies.start(tiles.at[leaf], ref["near_out"].at[leaf])
-
+    tile, total = near_tiles(ref, near, copies)
     left, right, chosen = ref["left"], ref["right"], ref["chosen"]
     top = jnp.where(position() % half == 0, left[...] + right[...] + unit(ridge), chosen[...])
     values = {}
@@ -322,8 +341,7 @@
     def put_r(i, value):
         target[i : i + 1, :] = jnp.where(lane >= i, value[0:1, :], 0.0)
 
-    total = leaves * fan
-    share = -(-total // (STEPS - 2))
+    share = -(-total // (STEPS - 4))
     for s in range(STEPS):
         eliminate(s, get, put, put_r, None)
         for t in range(s * share, min((s + 1) * share, total)):
@@ -363,7 +381,6 @@
     mats = shape((leaves, WIDTH, WIDTH), f32)
     flat = shape((WIDTH * GROUP, WIDTH), f32)
     coords_shape = shape((3 * leaves, WIDTH), f32)
-    halo_level = 3
 
     basis, gram, heads, weight_own, message, move, columns = pl.pallas_call(
         local_kernel,
@@ -383,12 +400,31 @@
         name="local",
     )(*(pltpu.with_memory_space_constraint(x, pltpu.HBM) for x in (counts, coords, proxies, leaf_transfers, node_transfers)))
 
-    plan = [(0, 1, 2, 3), (4, 5, 6, 7), (8, 9, 10, 11), (12, 13, 14, 15), ()]
-    state = dict(leaf=gram, node=heads)
+    plan = [
+        ((0, 1, 2, 3), ()),
+        ((4, 5, 6, 7), ()),
+        ((8, 9, 10, 11), (0,)),
+        ((12, 13, 14, 15), (1, 2, 3)),
+        ((), (4, 5)),
+    ]
+    last_near = tuple(range(6, leaves))
+    state = dict(leaf=gram, node=heads, near=None)
+    near_shape = shape((leaves, fan, slots, slots), bf16)
+
+    def near_extras(near, operands, outs, scratch, aliases):
+        operands += [("ids", neighbours, smem), ("own", own, vmem), ("low", low, vmem)]
+        operands += [("high", high, vmem), ("columns", columns, vmem)]
+        outs.append(("near_out", near_shape, anywhere))
+        scratch.append(("tiles", pltpu.VMEM((len(near), fan, slots, slots), bf16)))
+        scratch.append(("wide", pltpu.VMEM((9 * leaves, WIDTH), f32)))
+        if state["near"] is not None:
+            operands.append(("near_in", state["near"], anywhere))
+            aliases["near_in"] = "near_out"
     parts = []
 
     def work(n, after):
-        steps = plan[n]
+        steps, near = plan[n]
+        aliases = {}
         final = n == len(plan) - 1
         operands = [("after", after, anywhere)]
         outs, scratch = [], []
@@ -398,9 +434,11 @@
             outs += [(kind, rows, vmem) for kind in ("leaf_r", "leaf_s", "node_r")]
             if steps[-1] + 1 < STEPS:
                 outs += [("leaf_out", flat, vmem), ("node_out", flat, vmem)]
-        if n == halo_level:
+        if n == 0:
             operands.append(("message", message, vmem))
             outs.append(("own", coords_shape, vmem))
+        if near:
+            near_extras(near, operands, outs, scratch, aliases)
         if final:
             for k, part in enumerate(parts):
                 operands += [(f"{kind}{k}", part[kind], vmem) for kind in ("leaf_r", "leaf_s", "node_r")]
@@ -409,11 +447,13 @@
             outs.append(("leaf_bases", shape((leaves * slots, WIDTH), bf16), anywhere))
             scratch += [("factors", pltpu.VMEM(mats.shape, f32)), ("nodes", pltpu.VMEM(mats.shape, f32))]
             scratch.append(("bases", pltpu.VMEM((leaves * slots, WIDTH), bf16)))
-            scratch.append(("sems", pltpu.SemaphoreType.DMA((3 * GROUP,))))
+        if near or final:
+            scratch.append(("sems", pltpu.SemaphoreType.DMA((3 * GROUP + leaves,))))
         made = call(
-            work_kernel, operands, outs, scratch, {}, 3, f"work{n}",
-            steps=steps, final=len(parts) if final else 0,
+            work_kernel, operands, outs, scratch, aliases, 3, f"work{n}",
+            steps=steps, near=near, final=len(parts) if final else 0,
         )
+        state["near"] = made.get("near_out", state["near"])
         if steps:
             parts.append(made)
             state["leaf"], state["node"] = made.get("leaf_out"), made.get("node_out")
@@ -435,7 +475,7 @@
             left, right = lax.ppermute(weight, both, first), lax.ppermute(weight, both, second)
         if level < len(plan):
             made = work(level, weight)
-        if level == halo_level:
+        if level == 0:
             own = made["own"]
             up = [(i, i + 1) for i in range(count - 1)]
             low = lax.ppermute(own, both, up)
@@ -451,23 +491,15 @@
                 name=f"lift{level}",
             )(left, right, move, chosen, next(iter(made.values())))
 
-    top = call(
-        top_kernel,
-        [
-            ("left", left, vmem), ("right", right, vmem), ("chosen", chosen, vmem), ("ids", neighbours, smem),
-            ("own", own, vmem), ("low", low, vmem), ("high", high, vmem), ("columns", columns, vmem),
-            ("node_in", made["node_factors"], anywhere),
-        ],
-        [("near_out", shape((leaves, fan, slots, slots), bf16), anywhere), ("node_out", mats, anywhere)],
-        [
-            ("factor", pltpu.VMEM((WIDTH, WIDTH), f32)),
-            ("tiles", pltpu.VMEM((leaves, fan, slots, slots), bf16)),
-            ("wide", pltpu.VMEM((9 * leaves, WIDTH), f32)),
-            ("sems", pltpu.SemaphoreType.DMA((leaves + 1,))),
-        ],
-        {"node_in": "node_out"},
-        6, "top", half=half,
-    )
+    operands = [
+        ("left", left, vmem), ("right", right, vmem), ("chosen", chosen, vmem),
+        ("node_in", made["node_factors"], anywhere),
+    ]
+    outs = [("node_out", mats, anywhere)]
+    scratch = [("factor", pltpu.VMEM((WIDTH, WIDTH), f32)), ("sems", pltpu.SemaphoreType.DMA((leaves + 1,)))]
+    aliases = {"node_in": "node_out"}
+    near_extras(last_near, operands, outs, scratch, aliases)
+    top = call(top_kernel, operands, outs, scratch, aliases, 6, "top", near=last_near, half=half)
     return (top["near_out"], made["leaf_bases"], made["leaf_factors"], top["node_out"])
 
 

time: 49.3 us -> 52.9 us (1.073)
  the two profiles are of different devices: /device:TPU:0 before, /device:TPU:1 now
where the time goes in v5:
time: 52.9 us; the launch traced here: 52.1 us
  Pallas kernels  28.2 us (53%)
  starting transfers between devices  18.8 us (36%)
  waiting for transfers between devices  4.11 us (8%)
  between operations  1.03 us (2%)
    pallas_call x6, Pallas kernels, call(): pl.pallas_call(functools.partial(body, names=names, **static), out_shape=...  22 us
    ppermute x1, starting transfers between devices, shards(): high = lax.ppermute(own, both, [(target, source) for source, target in up])  4.89 us
    pallas_call x1, Pallas kernels, shards(): pl.pallas_call(local_kernel, out_shape=(mats, flat, flat, mat, coords_sha...  4.81 us
    ppermute x4, starting transfers between devices, shards(): lax.ppermute(weight, both, first)  4.1 us
    ppermute x1, starting transfers between devices, shards(): lax.ppermute(weight, both, [(i, i + 1) for i in range(0, count, 2)])  3.95 us
    ppermute x4, waiting for transfers between devices, shards(): lax.ppermute(weight, both, first)  3.93 us
    ppermute x4, starting transfers between devices, shards(): lax.ppermute(weight, both, second)  3.91 us
    ppermute x1, starting transfers between devices, shards(): low = lax.ppermute(own, both, up)  1.92 us
  transfers between devices with their start and end apart: 11, of which 2 were waited for; matrix products, arithmetic and copies ran while one was open for 0% of the time, Pallas kernels for 31%

profile of v5, /device:TPU:1, one launch (start us, length us, event | category | flops | bytes accessed | tf_op | source)
XLA Modules:
  0.0 52.1 jit_solution(2114904103048112484)
XLA Ops:
  0.6 4.8 %local.1 = (f32[8,128,128]{2,1,0:T(8,128)S(1)}, f32[1024,128]{1,0:T(8,128)S(1)}, f32[1024,128]{1,0:T(8,128)S(1)}, f32[128,128]{1,0:T(8,128)S(1)}, f32[24,128]{1,...) custom-call(s32[8]{0:T(128)} %counts_in.1, f32[3,1024]{1,0:T(4,128)} %coords_in.1, ...), custom_call_target="tpu_custom_call" | custom-call | flops 4000000000 | bytes 12000000 | tf_op jit(solution)/shard_map/local/pallas_call | solution.py:385
  5.4 4.0 %collective-permute-start = (f32[128,128]{1,0:T(8,128)S(1)}, f32[128,128]{1,0:T(8,128)S(1)}, u32[]{:S(2)}, u32[]{:S(2)}) collective-permute-start(f32[128,128]{1,0:T(8,128)S(1)} %get-tuple-element.46.refs_0_.right.chosen_in), channel_id=1, source_target_pairs={{0,1},{2,3},{4,5},{6,7},{8,9},{10,11},{12,13},{14,15},{16,17},{18,... | collective-permute-start | bytes 196616 | tf_op jit(solution)/shard_map/ppermute | solution.py:468
  9.4 2.6 %work0.1 = (f32[256,128]{1,0:T(8,128)S(1)}, f32[256,128]{1,0:T(8,128)S(1)}, f32[256,128]{1,0:T(8,128)S(1)}, f32[1024,128]{1,0:T(8,128)S(1)}, f32[1024,128]{1,0:T(8,128)S(1)}, /*index=5*/f32[24,128]{1,0:T(8,128)S(1)}) custom-call(f32[128,128]{1,0:T(8,128)S(1)} %get-tuple-element.46.refs_0_.right.chosen_in, f32[1024,128]{1,0:T(8,128)S(1)} %get-tuple-element.48.refs_1_, ...), custom_call_target="tpu_custom_call" | custom-call | flops 3000000000 | bytes 9000000 | tf_op jit(solution)/shard_map/work0/pallas_call | solution.py:357
  12.0 4.9 %collective-permute-start.6 = (f32[24,128]{1,0:T(8,128)S(1)}, f32[24,128]{1,0:T(8,128)S(1)}, u32[]{:S(2)}, u32[]{:S(2)}) collective-permute-start(f32[24,128]{1,0:T(8,128)S(1)} %get-tuple-element.61.refs_4_.refs_2_.refs_5_), channel_id=1, source_target_pairs={{1,0},{2,1},{3,2},{4,3},{5,4},{6,5},{7,6},{8,7},{9,8},{10,9},{11,1... | collective-permute-start | bytes 36872 | tf_op jit(solution)/shard_map/ppermute | solution.py:482
  16.9 1.9 %collective-permute-start.5 = (f32[24,128]{1,0:T(8,128)S(1)}, f32[24,128]{1,0:T(8,128)S(1)}, u32[]{:S(2)}, u32[]{:S(2)}) collective-permute-start(f32[24,128]{1,0:T(8,128)S(1)} %get-tuple-element.61.refs_4_.refs_2_.refs_5_), channel_id=1, source_target_pairs={{0,1},{1,2},{2,3},{3,4},{4,5},{5,6},{6,7},{7,8},{8,9},{9,10},{10,1... | collective-permute-start | bytes 36872 | tf_op jit(solution)/shard_map/ppermute | solution.py:481
  18.8 0.3 lift0.1
  19.2 0.7 %collective-permute-start.2 = (f32[128,128]{1,0:T(8,128)S(1)}, f32[128,128]{1,0:T(8,128)S(1)}, u32[]{:S(2)}, u32[]{:S(2)}) collective-permute-start(f32[128,128]{1,0:T(8,128)S(1)} %get-tuple-element.52.refs_0_), channel_id=1, source_target_pairs={{3,2},{7,6},{11,10},{15,14},{19,18},{23,22},{27,26},{31,30}} | collective-permute-start | bytes 196616 | tf_op jit(solution)/shard_map/ppermute | solution.py:475
  19.9 0.7 %collective-permute-start.1 = (f32[128,128]{1,0:T(8,128)S(1)}, f32[128,128]{1,0:T(8,128)S(1)}, u32[]{:S(2)}, u32[]{:S(2)}) collective-permute-start(f32[128,128]{1,0:T(8,128)S(1)} %get-tuple-element.52.refs_0_), channel_id=1, source_target_pairs={{1,2},{5,6},{9,10},{13,14},{17,18},{21,22},{25,26},{29,30}} | collective-permute-start | bytes 196616 | tf_op jit(solution)/shard_map/ppermute | solution.py:475
  20.5 2.2 %work1.1 = (f32[256,128]{1,0:T(8,128)S(1)}, f32[256,128]{1,0:T(8,128)S(1)}, f32[256,128]{1,0:T(8,128)S(1)}, f32[1024,128]{1,0:T(8,128)S(1)}, f32[1024,128]{1,0:T(8,128)S(1)}) custom-call(f32[128,128]{1,0:T(8,128)S(1)} %get-tuple-element.52.refs_0_, f32[1024,128]{1,0:T(8,128)S(1)} %get-tuple-element.54.refs_1_, f32[1024,128]{1,0:T(8,128)S(1)} %get-tuple-element.55.refs_2_), custom_call_target="tpu_custom_call" | custom-call | flops 3000000000 | bytes 9000000 | tf_op jit(solution)/shard_map/work1/pallas_call | solution.py:357
  22.8 0.3 lift1.1
  23.2 0.7 %collective-permute-start.4 = (f32[128,128]{1,0:T(8,128)S(1)}, f32[128,128]{1,0:T(8,128)S(1)}, u32[]{:S(2)}, u32[]{:S(2)}) collective-permute-start(f32[128,128]{1,0:T(8,128)S(1)} %get-tuple-element.57.refs_0_), channel_id=1, source_target_pairs={{6,4},{14,12},{22,20},{30,28}} | collective-permute-start | bytes 196616 | tf_op jit(solution)/shard_map/ppermute | solution.py:475
  23.8 0.7 %collective-permute-start.3 = (f32[128,128]{1,0:T(8,128)S(1)}, f32[128,128]{1,0:T(8,128)S(1)}, u32[]{:S(2)}, u32[]{:S(2)}) collective-permute-start(f32[128,128]{1,0:T(8,128)S(1)} %get-tuple-element.57.refs_0_), channel_id=1, source_target_pairs={{2,4},{10,12},{18,20},{26,28}} | collective-permute-start | bytes 196616 | tf_op jit(solution)/shard_map/ppermute | solution.py:475
  24.5 0.2 collective-permute-done.5.refs_5_.refs_3_.refs_6_
  24.7 3.8 %work2.1 = (f32[256,128]{1,0:T(8,128)S(1)}, f32[256,128]{1,0:T(8,128)S(1)}, f32[256,128]{1,0:T(8,128)S(1)}, f32[1024,128]{1,0:T(8,128)S(1)}, f32[1024,128]{1,0:T(8,128)S(1)}, /*index=5*/bf16[8,8,128,128]{3,2,1,0:T(8,128)(2,1)}) custom-call(f32[128,128]{1,0:T(8,128)S(1)} %get-tuple-element.57.refs_0_, f32[1024,128]{1,0:T(8,128)S(1)} %get-tuple-element.59.refs_1_, ...), custom_call_target="tpu_custom_call" | custom-call | flops 3000000000 | bytes 9000000 | tf_op jit(solution)/shard_map/work2/pallas_call | solution.py:357
  28.5 0.3 lift2.1
  28.9 1.3 %collective-permute-start.8 = (f32[128,128]{1,0:T(8,128)S(1)}, f32[128,128]{1,0:T(8,128)S(1)}, u32[]{:S(2)}, u32[]{:S(2)}) collective-permute-start(f32[128,128]{1,0:T(8,128)S(1)} %get-tuple-element.64.refs_0_), channel_id=1, source_target_pairs={{12,8},{28,24}} | collective-permute-start | bytes 196616 | tf_op jit(solution)/shard_map/ppermute | solution.py:475
  30.2 1.5 %collective-permute-start.7 = (f32[128,128]{1,0:T(8,128)S(1)}, f32[128,128]{1,0:T(8,128)S(1)}, u32[]{:S(2)}, u32[]{:S(2)}) collective-permute-start(f32[128,128]{1,0:T(8,128)S(1)} %get-tuple-element.64.refs_0_), channel_id=1, source_target_pairs={{4,8},{20,24}} | collective-permute-start | bytes 196616 | tf_op jit(solution)/shard_map/ppermute | solution.py:475
  31.6 3.8 %work3.1 = (f32[256,128]{1,0:T(8,128)S(1)}, f32[256,128]{1,0:T(8,128)S(1)}, f32[256,128]{1,0:T(8,128)S(1)}, bf16[8,8,128,128]{3,2,1,0:T(8,128)(2,1)}) custom-call(f32[128,128]{1,0:T(8,128)S(1)} %get-tuple-element.64.refs_0_, f32[1024,128]{1,0:T(8,128)S(1)} %get-tuple-element.66.refs_1_, ...), custom_call_target="tpu_custom_call", output_to_operand_aliasing={{3}: (8, {})} | custom-call | flops 3000000000 | bytes 9000000 | tf_op jit(solution)/shard_map/work3/pallas_call | solution.py:357
  35.5 3.9 %collective-permute-done.7.left = f32[128,128]{1,0:T(8,128)S(1)} collective-permute-done((f32[128,128]{1,0:T(8,128)S(1)}, f32[128,128]{1,0:T(8,128)S(1)}, u32[]{:S(2)}, u32[]{:S(2)}) %collective-permute-start.7) | collective-permute-done | bytes 65568 | tf_op jit(solution)/shard_map/ppermute | solution.py:475
  39.4 0.3 lift3.1
  39.8 1.3 %collective-permute-start.10 = (f32[128,128]{1,0:T(8,128)S(1)}, f32[128,128]{1,0:T(8,128)S(1)}, u32[]{:S(2)}, u32[]{:S(2)}) collective-permute-start(f32[128,128]{1,0:T(8,128)S(1)} %get-tuple-element.70.refs_0_), channel_id=1, source_target_pairs={{24,16},{8,0}} | collective-permute-start | bytes 196616 | tf_op jit(solution)/shard_map/ppermute | solution.py:475
  41.1 1.3 %collective-permute-start.9 = (f32[128,128]{1,0:T(8,128)S(1)}, f32[128,128]{1,0:T(8,128)S(1)}, u32[]{:S(2)}, u32[]{:S(2)}) collective-permute-start(f32[128,128]{1,0:T(8,128)S(1)} %get-tuple-element.70.refs_0_), channel_id=1, source_target_pairs={{8,16},{24,0}} | collective-permute-start | bytes 196616 | tf_op jit(solution)/shard_map/ppermute | solution.py:475
  42.4 3.0 %work4.1 = (bf16[8,8,128,128]{3,2,1,0:T(8,128)(2,1)}, f32[8,128,128]{2,1,0:T(8,128)}, f32[8,128,128]{2,1,0:T(8,128)}, bf16[1024,128]{1,0:T(8,128)(2,1)}) custom-call(f32[128,128]{1,0:T(8,128)S(1)} %get-tuple-element.70.refs_0_, s32[8,8]{1,0:T(8,128)S(1)} %copy-done, ...), custom_call_target="tpu_custom_call", output_to_operand_aliasing={{0}: (6, {})} | custom-call | flops 3000000000 | bytes 9000000 | tf_op jit(solution)/shard_map/work4/pallas_call | solution.py:357
  45.4 6.5 %top.1 = (f32[8,128,128]{2,1,0:T(8,128)}, bf16[8,8,128,128]{3,2,1,0:T(8,128)(2,1)}) custom-call(f32[128,128]{1,0:T(8,128)S(1)} %collective-permute-done.9.refs_0_, f32[128,128]{1,0:T(8,128)S(1)} %collective-permute-done.10.refs_1_, f32[128,128]{1,0:T(8,128)S(1)} %get-tuple-element.71.refs_2_, ...), custom_call_target="tpu_custom_call", output_to_operand_aliasing={{0}: (3, {}), {1}: (9, {})} | custom-call | flops 6000000000 | bytes 18000000 | tf_op jit(solution)/shard_map/top/pallas_call | solution.py:357
  (11 shorter events, 0.0 us)
Async XLA Ops:
  5.4 13.4 %collective-permute-start = (f32[128,128]{1,0:T(8,128)S(1)}, f32[128,128]{1,0:T(8,128)S(1)}, u32[]{:S(2)}, u32[]{:S(2)}) collective-permute-start(f32[128,128]{1,0:T(8,128)S(1)} %get-tuple-element.46.refs_0_.right.chosen_in), channel_id=1, source_target_pairs={{0,1},{2,3},{4,5},{6,7},{8,9},{10,11},{12,13},{14,15},{16,17},{18,... | collective-permute-start | bytes 196616 | tf_op jit(solution)/shard_map/ppermute | solution.py:468
  12.0 12.5 %collective-permute-start.6 = (f32[24,128]{1,0:T(8,128)S(1)}, f32[24,128]{1,0:T(8,128)S(1)}, u32[]{:S(2)}, u32[]{:S(2)}) collective-permute-start(f32[24,128]{1,0:T(8,128)S(1)} %get-tuple-element.61.refs_4_.refs_2_.refs_5_), channel_id=1, source_target_pairs={{1,0},{2,1},{3,2},{4,3},{5,4},{6,5},{7,6},{8,7},{9,8},{10,9},{11,1... | collective-permute-start | bytes 36872 | tf_op jit(solution)/shard_map/ppermute | solution.py:482
  16.9 7.8 %collective-permute-start.5 = (f32[24,128]{1,0:T(8,128)S(1)}, f32[24,128]{1,0:T(8,128)S(1)}, u32[]{:S(2)}, u32[]{:S(2)}) collective-permute-start(f32[24,128]{1,0:T(8,128)S(1)} %get-tuple-element.61.refs_4_.refs_2_.refs_5_), channel_id=1, source_target_pairs={{0,1},{1,2},{2,3},{3,4},{4,5},{5,6},{6,7},{7,8},{8,9},{9,10},{10,1... | collective-permute-start | bytes 36872 | tf_op jit(solution)/shard_map/ppermute | solution.py:481
  19.2 3.6 %collective-permute-start.2 = (f32[128,128]{1,0:T(8,128)S(1)}, f32[128,128]{1,0:T(8,128)S(1)}, u32[]{:S(2)}, u32[]{:S(2)}) collective-permute-start(f32[128,128]{1,0:T(8,128)S(1)} %get-tuple-element.52.refs_0_), channel_id=1, source_target_pairs={{3,2},{7,6},{11,10},{15,14},{19,18},{23,22},{27,26},{31,30}} | collective-permute-start | bytes 196616 | tf_op jit(solution)/shard_map/ppermute | solution.py:475
  19.9 3.0 %collective-permute-start.1 = (f32[128,128]{1,0:T(8,128)S(1)}, f32[128,128]{1,0:T(8,128)S(1)}, u32[]{:S(2)}, u32[]{:S(2)}) collective-permute-start(f32[128,128]{1,0:T(8,128)S(1)} %get-tuple-element.52.refs_0_), channel_id=1, source_target_pairs={{1,2},{5,6},{9,10},{13,14},{17,18},{21,22},{25,26},{29,30}} | collective-permute-start | bytes 196616 | tf_op jit(solution)/shard_map/ppermute | solution.py:475
  20.5 4.2 %copy-start = (s32[8,8]{1,0:T(8,128)S(1)}, s32[8,8]{1,0:T(8,128)}, u32[]{:S(2)}) copy-start(s32[8,8]{1,0:T(8,128)} %refs_4_.1) | copy-start | bytes 772
  23.2 5.3 %collective-permute-start.4 = (f32[128,128]{1,0:T(8,128)S(1)}, f32[128,128]{1,0:T(8,128)S(1)}, u32[]{:S(2)}, u32[]{:S(2)}) collective-permute-start(f32[128,128]{1,0:T(8,128)S(1)} %get-tuple-element.57.refs_0_), channel_id=1, source_target_pairs={{6,4},{14,12},{22,20},{30,28}} | collective-permute-start | bytes 196616 | tf_op jit(solution)/shard_map/ppermute | solution.py:475
  23.8 4.7 %collective-permute-start.3 = (f32[128,128]{1,0:T(8,128)S(1)}, f32[128,128]{1,0:T(8,128)S(1)}, u32[]{:S(2)}, u32[]{:S(2)}) collective-permute-start(f32[128,128]{1,0:T(8,128)S(1)} %get-tuple-element.57.refs_0_), channel_id=1, source_target_pairs={{2,4},{10,12},{18,20},{26,28}} | collective-permute-start | bytes 196616 | tf_op jit(solution)/shard_map/ppermute | solution.py:475
  28.9 6.6 %collective-permute-start.8 = (f32[128,128]{1,0:T(8,128)S(1)}, f32[128,128]{1,0:T(8,128)S(1)}, u32[]{:S(2)}, u32[]{:S(2)}) collective-permute-start(f32[128,128]{1,0:T(8,128)S(1)} %get-tuple-element.64.refs_0_), channel_id=1, source_target_pairs={{12,8},{28,24}} | collective-permute-start | bytes 196616 | tf_op jit(solution)/shard_map/ppermute | solution.py:475
  30.2 9.3 %collective-permute-start.7 = (f32[128,128]{1,0:T(8,128)S(1)}, f32[128,128]{1,0:T(8,128)S(1)}, u32[]{:S(2)}, u32[]{:S(2)}) collective-permute-start(f32[128,128]{1,0:T(8,128)S(1)} %get-tuple-element.64.refs_0_), channel_id=1, source_target_pairs={{4,8},{20,24}} | collective-permute-start | bytes 196616 | tf_op jit(solution)/shard_map/ppermute | solution.py:475
  39.8 5.6 %collective-permute-start.10 = (f32[128,128]{1,0:T(8,128)S(1)}, f32[128,128]{1,0:T(8,128)S(1)}, u32[]{:S(2)}, u32[]{:S(2)}) collective-permute-start(f32[128,128]{1,0:T(8,128)S(1)} %get-tuple-element.70.refs_0_), channel_id=1, source_target_pairs={{24,16},{8,0}} | collective-permute-start | bytes 196616 | tf_op jit(solution)/shard_map/ppermute | solution.py:475
  41.1 4.3 %collective-permute-start.9 = (f32[128,128]{1,0:T(8,128)S(1)}, f32[128,128]{1,0:T(8,128)S(1)}, u32[]{:S(2)}, u32[]{:S(2)}) collective-permute-start(f32[128,128]{1,0:T(8,128)S(1)} %get-tuple-element.70.refs_0_), channel_id=1, source_target_pairs={{8,16},{24,0}} | collective-permute-start | bytes 196616 | tf_op jit(solution)/shard_map/ppermute | solution.py:475

commit v6 on v5

--- a/solution.py
+++ b/solution.py
@@ -154,7 +154,7 @@
 
 def local_kernel(
     counts_in, coords_in, proxies_in, leaf_in, node_in,
-    basis_ref, gram_ref, heads_ref, weight_ref, message_ref, move_ref, columns_ref,
+    basis_ref, gram_ref, heads_ref, message_ref, move_ref, columns_ref,
     counts, coords, proxies, leaf_t, node_t, sems,
 ):
     pairs = ((counts_in, counts), (coords_in, coords), (proxies_in, proxies), (leaf_in, leaf_t), (node_in, node_t))
@@ -172,7 +172,7 @@
         span = slice(leaf * WIDTH, leaf * WIDTH + WIDTH)
         own = coords[:, span]
         valid = lane < counts[leaf]
-        at = 3 * leaf
+        at = WIDTH + 3 * leaf
         message_ref[at : at + 1, :] = jnp.where(valid, own[0:1], -far)
         message_ref[at + 1 : at + 3, :] = own[1:3]
         turned = jnp.concatenate([jnp.where(valid, own[0:1], far), own[1:3], jnp.zeros((5, WIDTH), f32)], axis=0).T
@@ -200,14 +200,15 @@
             following.append(lift(node_t[k * 2**level + 2 ** (level - 1)], head))
         weights = following
         level += 1
-    weight_ref[...] = weights[0]
+    message_ref[0:WIDTH, :] = weights[0]
 
 
 def lift_kernel(left, right, move, chosen_in, token, weight_ref, chosen_ref, *, level):
     del token
-    head = left[...] + right[...] + unit(ridge)
+    span = slice(0, WIDTH)
+    head = left[span, :] + right[span, :] + unit(ridge)
     mine = position() % (2 ** (level + 1)) == 2**level
-    chosen_ref[...] = jnp.where(mine, head, chosen_in[...])
+    chosen_ref[...] = jnp.where(mine, head, chosen_in[span, :])
     weight_ref[...] = lift(move[...], head)
 
 
@@ -234,14 +235,23 @@
             copy.wait()
 
 
-def near_tiles(ref, near, copies):
-    ids, columns, tiles, wide = ref["ids"], ref["columns"], ref["tiles"], ref["wide"]
+def near_tiles(ref, near, flush, copies):
+    for n, leaf in enumerate(flush):
+        copies.start(ref["tiles_in"].at[n], ref["near_out"].at[leaf])
+    if not near:
+        return None, 0
+    ids, columns, wide = ref["ids"], ref["columns"], ref["wide"]
     leaves, fan = ids.shape[1], ids.shape[0]
-    size = ref["own"].shape[0]
-    for n, name in enumerate(("low", "own", "high")):
-        wide[n * size : (n + 1) * size, :] = ref[name][...]
+    size = ref["swapped"].shape[0]
+    odd = position() % 2 == 1
+    first, own, second = (ref[n][-size:, :] for n in ("pair", "own", "swapped"))
+    wide[0:size, :] = jnp.where(odd, first, second)
+    wide[size : 2 * size, :] = own
+    wide[2 * size : 3 * size, :] = jnp.where(odd, second, first)
     offset = (position() - 1) * leaves
     total = len(near) * fan
+    later = "tiles_out" in ref
+    tiles = ref["tiles_out" if later else "tiles"]
 
     def tile(t):
         at, n = divmod(t, fan)
@@ -250,17 +260,17 @@
         shape = (WIDTH, WIDTH)
         value = matern(*(columns[leaf, d] - jnp.broadcast_to(other[d : d + 1], shape) for d in range(3)))
         tiles[at, n] = value.astype(bf16)
-        if n == fan - 1:
+        if n == fan - 1 and not later:
             copies.start(tiles.at[at], ref["near_out"].at[leaf])
 
     return tile, total
 
 
-def work_kernel(*refs, names, steps, near, final):
+def work_kernel(*refs, names, steps, near, flush, final):
     ref = dict(zip(names, refs))
     held = ({}, {})
     copies = Copies(ref["sems"]) if "sems" in ref else None
-    tile, total = near_tiles(ref, near, copies) if near else (None, 0)
+    tile, total = near_tiles(ref, near, flush, copies)
     done = 0
     share = -(-total // max(1, len(steps) - 1)) if steps else total
     for s in steps:
@@ -291,8 +301,8 @@
         if name + "_out" in ref:
             for i in range(STEP * (steps[-1] + 1), WIDTH):
                 ref[name + "_out"][GROUP * i : GROUP * (i + 1), :] = held[side][i]
-    if "message" in ref:
-        ref["own"][...] = ref["message"][...]
+    if "coords_out" in ref:
+        ref["coords_out"][...] = ref["message"][WIDTH:, :]
     if not final:
         if copies:
             copies.wait()
@@ -321,10 +331,10 @@
     copies.wait()
 
 
-def top_kernel(*refs, names, near, half):
+def top_kernel(*refs, names, near, flush, half):
     ref = dict(zip(names, refs))
     copies = Copies(ref["sems"])
-    tile, total = near_tiles(ref, near, copies)
+    tile, total = near_tiles(ref, near, flush, copies)
     left, right, chosen = ref["left"], ref["right"], ref["chosen"]
     top = jnp.where(position() % half == 0, left[...] + right[...] + unit(ridge), chosen[...])
     values = {}
@@ -381,12 +391,13 @@
     mats = shape((leaves, WIDTH, WIDTH), f32)
     flat = shape((WIDTH * GROUP, WIDTH), f32)
     coords_shape = shape((3 * leaves, WIDTH), f32)
-
-    basis, gram, heads, weight_own, message, move, columns = pl.pallas_call(
+    long = shape((WIDTH + 3 * leaves, WIDTH), f32)
+
+    basis, gram, heads, message, move, columns = pl.pallas_call(
         local_kernel,
-        out_shape=(mats, flat, flat, mat, coords_shape, mat, shape((leaves, 3, slots, WIDTH), f32)),
+        out_shape=(mats, flat, flat, long, mat, shape((leaves, 3, slots, WIDTH), f32)),
         in_specs=[anywhere] * 5,
-        out_specs=(vmem,) * 7,
+        out_specs=(vmem,) * 6,
         scratch_shapes=[
             pltpu.SMEM(counts.shape, jnp.int32),
             pltpu.VMEM(coords.shape, f32),
@@ -403,24 +414,31 @@
     plan = [
         ((0, 1, 2, 3), ()),
         ((4, 5, 6, 7), ()),
-        ((8, 9, 10, 11), (0,)),
-        ((12, 13, 14, 15), (1, 2, 3)),
-        ((), (4, 5)),
+        ((8, 9, 10, 11), ()),
+        ((12, 13, 14, 15), (0, 1, 2)),
+        ((), (3, 4, 5)),
     ]
+    parts = []
     last_near = tuple(range(6, leaves))
-    state = dict(leaf=gram, node=heads, near=None)
-    near_shape = shape((leaves, fan, slots, slots), bf16)
-
-    def near_extras(near, operands, outs, scratch, aliases):
-        operands += [("ids", neighbours, smem), ("own", own, vmem), ("low", low, vmem)]
-        operands += [("high", high, vmem), ("columns", columns, vmem)]
-        outs.append(("near_out", near_shape, anywhere))
-        scratch.append(("tiles", pltpu.VMEM((len(near), fan, slots, slots), bf16)))
-        scratch.append(("wide", pltpu.VMEM((9 * leaves, WIDTH), f32)))
-        if state["near"] is not None:
-            operands.append(("near_in", state["near"], anywhere))
-            aliases["near_in"] = "near_out"
-    parts = []
+    state = dict(leaf=gram, node=heads, near=None, tiles=None, flush=())
+
+    def near_extras(near, flush, later, operands, outs, scratch, aliases):
+        if near:
+            operands += [("ids", neighbours, smem), ("own", message, vmem), ("pair", pair, vmem)]
+            operands += [("swapped", swapped, vmem), ("columns", columns, vmem)]
+            scratch.append(("wide", pltpu.VMEM((9 * leaves, WIDTH), f32)))
+            tiles = (len(near), fan, slots, slots)
+            if later:
+                outs.append(("tiles_out", shape(tiles, bf16), vmem))
+            else:
+                scratch.append(("tiles", pltpu.VMEM(tiles, bf16)))
+        if flush:
+            operands.append(("tiles_in", state["tiles"], vmem))
+        if flush or (near and not later):
+            outs.append(("near_out", shape((leaves, fan, slots, slots), bf16), anywhere))
+            if state["near"] is not None:
+                operands.append(("near_in", state["near"], anywhere))
+                aliases["near_in"] = "near_out"
 
     def work(n, after):
         steps, near = plan[n]
@@ -434,11 +452,11 @@
             outs += [(kind, rows, vmem) for kind in ("leaf_r", "leaf_s", "node_r")]
             if steps[-1] + 1 < STEPS:
                 outs += [("leaf_out", flat, vmem), ("node_out", flat, vmem)]
-        if n == 0:
+        if n == 1:
             operands.append(("message", message, vmem))
-            outs.append(("own", coords_shape, vmem))
-        if near:
-            near_extras(near, operands, outs, scratch, aliases)
+            outs.append(("coords_out", coords_shape, vmem))
+        flush = state["flush"]
+        near_extras(near, flush, True, operands, outs, scratch, aliases)
         if final:
             for k, part in enumerate(parts):
                 operands += [(f"{kind}{k}", part[kind], vmem) for kind in ("leaf_r", "leaf_s", "node_r")]
@@ -447,25 +465,27 @@
             outs.append(("leaf_bases", shape((leaves * slots, WIDTH), bf16), anywhere))
             scratch += [("factors", pltpu.VMEM(mats.shape, f32)), ("nodes", pltpu.VMEM(mats.shape, f32))]
             scratch.append(("bases", pltpu.VMEM((leaves * slots, WIDTH), bf16)))
-        if near or final:
+        if flush or final:
             scratch.append(("sems", pltpu.SemaphoreType.DMA((3 * GROUP + leaves,))))
         made = call(
             work_kernel, operands, outs, scratch, aliases, 3, f"work{n}",
-            steps=steps, near=near, final=len(parts) if final else 0,
+            steps=steps, near=near, flush=flush, final=len(parts) if final else 0,
         )
         state["near"] = made.get("near_out", state["near"])
+        state["tiles"], state["flush"] = made.get("tiles_out"), near
         if steps:
             parts.append(made)
             state["leaf"], state["node"] = made.get("leaf_out"), made.get("node_out")
         return made
 
-    weight = chosen = weight_own
-    made = low = high = own = None
+    weight = chosen = message
+    made = pair = swapped = None
     for level in range(levels):
         span = 2 ** (level + 1)
         quarter = span // 4
         if level == 0:
-            left, right = lax.ppermute(weight, both, [(i, i + 1) for i in range(0, count, 2)]), weight
+            pair = lax.ppermute(weight, both, [(i, i ^ 1) for i in range(count)])
+            left, right = pair, weight
         else:
             first = [(i + quarter, i + 2 * quarter) for i in range(0, count, span)]
             second = [(i + 3 * quarter, i + 2 * quarter) for i in range(0, count, span)]
@@ -475,11 +495,10 @@
             left, right = lax.ppermute(weight, both, first), lax.ppermute(weight, both, second)
         if level < len(plan):
             made = work(level, weight)
-        if level == 0:
-            own = made["own"]
-            up = [(i, i + 1) for i in range(count - 1)]
-            low = lax.ppermute(own, both, up)
-            high = lax.ppermute(own, both, [(target, source) for source, target in up])
+        if level == 1:
+            others = [(i, i + 1) for i in range(1, count - 1, 2)]
+            others += [(target, source) for source, target in others]
+            swapped = lax.ppermute(made["coords_out"], both, others)
         if level + 1 < levels:
             weight, chosen = pl.pallas_call(
                 functools.partial(lift_kernel, level=level),
@@ -498,8 +517,10 @@
     outs = [("node_out", mats, anywhere)]
     scratch = [("factor", pltpu.VMEM((WIDTH, WIDTH), f32)), ("sems", pltpu.SemaphoreType.DMA((leaves + 1,)))]
     aliases = {"node_in": "node_out"}
-    near_extras(last_near, operands, outs, scratch, aliases)
-    top = call(top_kernel, operands, outs, scratch, aliases, 6, "top", near=last_near, half=half)
+    near_extras(last_near, state["flush"], False, operands, outs, scratch, aliases)
+    top = call(
+        top_kernel, operands, outs, scratch, aliases, 6, "top", near=last_near, flush=state["flush"], half=half
+    )
     return (top["near_out"], made["leaf_bases"], made["leaf_factors"], top["node_out"])
 
 

time: 52.9 us -> 48.7 us (0.921)
  Pallas kernels: 28.2 us -> 25.6 us
  waiting for transfers between devices: 4.11 us -> 1.95 us
  starting transfers between devices: 18.8 us -> 19.8 us
    pallas_call x6, Pallas kernels: 22 us -> 19.4 us  [call(): pl.pallas_call(functools.partial(body, names=names, **static), out_shape=...]
    ppermute x4, waiting for transfers between devices: 3.93 us -> 1.58 us  [shards(): lax.ppermute(weight, both, first)]
    ppermute x3 -> x2, starting transfers between devices: 10.8 us -> 11.8 us  [the longest x1 9.72 us: shards(): swapped = lax.ppermute(made['coords_out'], both, others)]
  transfers between devices with their start and end apart: 11 -> 10, of which waited for: 2 -> 2; matrix products, arithmetic and copies ran while one was open for 0% -> 0% of each run, Pallas kernels for 31% -> 28%
where the time goes in v6:
time: 48.7 us; the launch traced here: 48.4 us
  Pallas kernels  25.6 us (53%)
  starting transfers between devices  19.8 us (41%)
  waiting for transfers between devices  1.95 us (4%)
  between operations  1.02 us (2%)
    pallas_call x6, Pallas kernels, call(): pl.pallas_call(functools.partial(body, names=names, **static), out_shape=...  19.4 us
    ppermute x1, starting transfers between devices, shards(): swapped = lax.ppermute(made['coords_out'], both, others)  9.72 us
    pallas_call x1, Pallas kernels, shards(): pl.pallas_call(local_kernel, out_shape=(mats, flat, flat, long, mat, shap...  4.81 us
    ppermute x4, starting transfers between devices, shards(): lax.ppermute(weight, both, second)  4.1 us
    ppermute x4, starting transfers between devices, shards(): lax.ppermute(weight, both, first)  3.91 us
    ppermute x1, starting transfers between devices, shards(): pair = lax.ppermute(weight, both, [(i, i ^ 1) for i in range(count)])  2.11 us
    ppermute x4, waiting for transfers between devices, shards(): lax.ppermute(weight, both, first)  1.58 us
    pallas_call x4, Pallas kernels, shards(): pl.pallas_call(functools.partial(lift_kernel, level=level), out_shape=[ma...  1.39 us
  transfers between devices with their start and end apart: 10, of which 2 were waited for; matrix products, arithmetic and copies ran while one was open for 0% of the time, Pallas kernels for 28%

profile of v6, /device:TPU:1, one launch (start us, length us, event | category | flops | bytes accessed | tf_op | source)
XLA Modules:
  0.0 48.4 jit_solution(11757216228808113352)
XLA Ops:
  0.6 4.8 %local.1 = (f32[8,128,128]{2,1,0:T(8,128)S(1)}, f32[1024,128]{1,0:T(8,128)S(1)}, f32[1024,128]{1,0:T(8,128)S(1)}, f32[152,128]{1,0:T(8,128)S(1)}, f32[128,128]{1...) custom-call(s32[8]{0:T(128)} %counts_in.1, f32[3,1024]{1,0:T(4,128)} %coords_in.1, f32[3,1024]{1,0:T(4,128)} %proxies_in.1, ...), custom_call_target="tpu_custom_call" | custom-call | flops 4000000000 | bytes 12000000 | tf_op jit(solution)/shard_map/local/pallas_call | solution.py:396
  5.4 2.1 %collective-permute-start = (f32[152,128]{1,0:T(8,128)S(1)}, f32[152,128]{1,0:T(8,128)S(1)}, u32[]{:S(2)}, u32[]{:S(2)}) collective-permute-start(f32[152,128]{1,0:T(8,128)S(1)} %get-tuple-element.45.refs_0_.right.chosen_in.refs_3_.refs_4_.refs_2_.refs_5_), channel_id=1, source_target_pairs={{0,1},{1,0},{2,3},{3,2},{4,5},{5,4},{6,7},{7,6},{8,9},{9,8},{10,11... | collective-permute-start | bytes 233480 | tf_op jit(solution)/shard_map/ppermute | solution.py:487
  7.6 2.6 %work0.1 = (f32[256,128]{1,0:T(8,128)S(1)}, f32[256,128]{1,0:T(8,128)S(1)}, f32[256,128]{1,0:T(8,128)S(1)}, f32[1024,128]{1,0:T(8,128)S(1)}, f32[1024,128]{1,0:T(8,128)S(1)}) custom-call(f32[152,128]{1,0:T(8,128)S(1)} %get-tuple-element.45.refs_0_.right.chosen_in.refs_3_.refs_4_.refs_2_.refs_5_, f32[1024,128]{1,0:T(8,128)S(1)} %get-tuple-element.47.refs_1_, ...), custom_call_target="tpu_custom_call" | custom-call | flops 3000000000 | bytes 9000000 | tf_op jit(solution)/shard_map/work0/pallas_call | solution.py:367
  10.1 0.3 lift0.1
  10.5 0.7 %collective-permute-start.1 = (f32[128,128]{1,0:T(8,128)S(1)}, f32[128,128]{1,0:T(8,128)S(1)}, u32[]{:S(2)}, u32[]{:S(2)}) collective-permute-start(f32[128,128]{1,0:T(8,128)S(1)} %get-tuple-element.50.refs_0_), channel_id=1, source_target_pairs={{1,2},{5,6},{9,10},{13,14},{17,18},{21,22},{25,26},{29,30}} | collective-permute-start | bytes 196616 | tf_op jit(solution)/shard_map/ppermute | solution.py:495
  11.2 0.7 %collective-permute-start.2 = (f32[128,128]{1,0:T(8,128)S(1)}, f32[128,128]{1,0:T(8,128)S(1)}, u32[]{:S(2)}, u32[]{:S(2)}) collective-permute-start(f32[128,128]{1,0:T(8,128)S(1)} %get-tuple-element.50.refs_0_), channel_id=1, source_target_pairs={{3,2},{7,6},{11,10},{15,14},{19,18},{23,22},{27,26},{31,30}} | collective-permute-start | bytes 196616 | tf_op jit(solution)/shard_map/ppermute | solution.py:495
  11.8 2.3 %work1.1 = (f32[256,128]{1,0:T(8,128)S(1)}, f32[256,128]{1,0:T(8,128)S(1)}, f32[256,128]{1,0:T(8,128)S(1)}, f32[1024,128]{1,0:T(8,128)S(1)}, f32[1024,128]{1,0:T(8,128)S(1)}, /*index=5*/f32[24,128]{1,0:T(8,128)S(1)}) custom-call(f32[128,128]{1,0:T(8,128)S(1)} %get-tuple-element.50.refs_0_, f32[1024,128]{1,0:T(8,128)S(1)} %get-tuple-element.52.refs_1_, ...), custom_call_target="tpu_custom_call" | custom-call | flops 3000000000 | bytes 9000000 | tf_op jit(solution)/shard_map/work1/pallas_call | solution.py:367
  14.1 9.7 %collective-permute-start.7 = (f32[24,128]{1,0:T(8,128)S(1)}, f32[24,128]{1,0:T(8,128)S(1)}, u32[]{:S(2)}, u32[]{:S(2)}) collective-permute-start(f32[24,128]{1,0:T(8,128)S(1)} %get-tuple-element.64), channel_id=1, source_target_pairs={{1,2},{3,4},{5,6},{7,8},{9,10},{11,12},{13,14},{15,16},{17,18},{19... | collective-permute-start | bytes 36872 | tf_op jit(solution)/shard_map/ppermute | solution.py:501
  23.9 0.4 lift1.1
  24.2 0.7 %collective-permute-start.3 = (f32[128,128]{1,0:T(8,128)S(1)}, f32[128,128]{1,0:T(8,128)S(1)}, u32[]{:S(2)}, u32[]{:S(2)}) collective-permute-start(f32[128,128]{1,0:T(8,128)S(1)} %get-tuple-element.55.refs_0_), channel_id=1, source_target_pairs={{2,4},{10,12},{18,20},{26,28}} | collective-permute-start | bytes 196616 | tf_op jit(solution)/shard_map/ppermute | solution.py:495
  24.9 0.7 %collective-permute-start.4 = (f32[128,128]{1,0:T(8,128)S(1)}, f32[128,128]{1,0:T(8,128)S(1)}, u32[]{:S(2)}, u32[]{:S(2)}) collective-permute-start(f32[128,128]{1,0:T(8,128)S(1)} %get-tuple-element.55.refs_0_), channel_id=1, source_target_pairs={{6,4},{14,12},{22,20},{30,28}} | collective-permute-start | bytes 196616 | tf_op jit(solution)/shard_map/ppermute | solution.py:495
  25.6 0.0 copy-start
  25.6 2.0 %work2.1 = (f32[256,128]{1,0:T(8,128)S(1)}, f32[256,128]{1,0:T(8,128)S(1)}, f32[256,128]{1,0:T(8,128)S(1)}, f32[1024,128]{1,0:T(8,128)S(1)}, f32[1024,128]{1,0:T(8,128)S(1)}) custom-call(f32[128,128]{1,0:T(8,128)S(1)} %get-tuple-element.55.refs_0_, f32[1024,128]{1,0:T(8,128)S(1)} %get-tuple-element.57.refs_1_, f32[1024,128]{1,0:T(8,128)S(1)} %get-tuple-element.58.refs_2_), custom_call_target="tpu_custom_call" | custom-call | flops 3000000000 | bytes 9000000 | tf_op jit(solution)/shard_map/work2/pallas_call | solution.py:367
  27.6 0.3 lift2.1
  27.9 1.3 %collective-permute-start.5 = (f32[128,128]{1,0:T(8,128)S(1)}, f32[128,128]{1,0:T(8,128)S(1)}, u32[]{:S(2)}, u32[]{:S(2)}) collective-permute-start(f32[128,128]{1,0:T(8,128)S(1)} %get-tuple-element.60.refs_0_), channel_id=1, source_target_pairs={{4,8},{20,24}} | collective-permute-start | bytes 196616 | tf_op jit(solution)/shard_map/ppermute | solution.py:495
  29.2 1.5 %collective-permute-start.6 = (f32[128,128]{1,0:T(8,128)S(1)}, f32[128,128]{1,0:T(8,128)S(1)}, u32[]{:S(2)}, u32[]{:S(2)}) collective-permute-start(f32[128,128]{1,0:T(8,128)S(1)} %get-tuple-element.60.refs_0_), channel_id=1, source_target_pairs={{12,8},{28,24}} | collective-permute-start | bytes 196616 | tf_op jit(solution)/shard_map/ppermute | solution.py:495
  30.7 2.7 %work3.1 = (f32[256,128]{1,0:T(8,128)S(1)}, f32[256,128]{1,0:T(8,128)S(1)}, f32[256,128]{1,0:T(8,128)S(1)}, bf16[3,8,128,128]{3,2,1,0:T(8,128)(2,1)S(1)}) custom-call(f32[128,128]{1,0:T(8,128)S(1)} %get-tuple-element.60.refs_0_, f32[1024,128]{1,0:T(8,128)S(1)} %get-tuple-element.62.refs_1_, f32[1024,128]{1,0:T(8,128)S(1)} %get-tuple-element.63.refs_2_, ...), custom_call_target="tpu_custom_call" | custom-call | flops 3000000000 | bytes 9000000 | tf_op jit(solution)/shard_map/work3/pallas_call | solution.py:367
  33.5 1.6 %collective-permute-done.5.left = f32[128,128]{1,0:T(8,128)S(1)} collective-permute-done((f32[128,128]{1,0:T(8,128)S(1)}, f32[128,128]{1,0:T(8,128)S(1)}, u32[]{:S(2)}, u32[]{:S(2)}) %collective-permute-start.5) | collective-permute-done | bytes 65568 | tf_op jit(solution)/shard_map/ppermute | solution.py:495
  35.0 0.4 collective-permute-done.6.right
  35.4 0.3 lift3.1
  35.7 1.3 %collective-permute-start.8 = (f32[128,128]{1,0:T(8,128)S(1)}, f32[128,128]{1,0:T(8,128)S(1)}, u32[]{:S(2)}, u32[]{:S(2)}) collective-permute-start(f32[128,128]{1,0:T(8,128)S(1)} %get-tuple-element.67.refs_0_), channel_id=1, source_target_pairs={{8,16},{24,0}} | collective-permute-start | bytes 196616 | tf_op jit(solution)/shard_map/ppermute | solution.py:495
  37.0 1.3 %collective-permute-start.9 = (f32[128,128]{1,0:T(8,128)S(1)}, f32[128,128]{1,0:T(8,128)S(1)}, u32[]{:S(2)}, u32[]{:S(2)}) collective-permute-start(f32[128,128]{1,0:T(8,128)S(1)} %get-tuple-element.67.refs_0_), channel_id=1, source_target_pairs={{24,16},{8,0}} | collective-permute-start | bytes 196616 | tf_op jit(solution)/shard_map/ppermute | solution.py:495
  38.3 3.3 %work4.1 = (bf16[3,8,128,128]{3,2,1,0:T(8,128)(2,1)S(1)}, bf16[8,8,128,128]{3,2,1,0:T(8,128)(2,1)}, f32[8,128,128]{2,1,0:T(8,128)}, f32[8,128,128]{2,1,0:T(8,128)}, bf16[1024,128]{1,0:T(8,128)(2,1)}) custom-call(f32[128,128]{1,0:T(8,128)S(1)} %get-tuple-element.67.refs_0_, s32[8,8]{1,0:T(8,128)S(1)} %copy-done, ...), custom_call_target="tpu_custom_call" | custom-call | flops 3000000000 | bytes 9000000 | tf_op jit(solution)/shard_map/work4/pallas_call | solution.py:367
  41.7 6.6 %top.1 = (f32[8,128,128]{2,1,0:T(8,128)}, bf16[8,8,128,128]{3,2,1,0:T(8,128)(2,1)}) custom-call(f32[128,128]{1,0:T(8,128)S(1)} %collective-permute-done.8.refs_0_, f32[128,128]{1,0:T(8,128)S(1)} %collective-permute-done.9.refs_1_, f32[128,128]{1,0:T(8,128)S(1)} %get-tuple-element.68.refs_2_, ...), custom_call_target="tpu_custom_call", output_to_operand_aliasing={{0}: (3, {}), {1}: (10, {})} | custom-call | flops 6000000000 | bytes 18000000 | tf_op jit(solution)/shard_map/top/pallas_call | solution.py:367
  (9 shorter events, 0.0 us)
Async XLA Ops:
  5.4 4.7 %collective-permute-start = (f32[152,128]{1,0:T(8,128)S(1)}, f32[152,128]{1,0:T(8,128)S(1)}, u32[]{:S(2)}, u32[]{:S(2)}) collective-permute-start(f32[152,128]{1,0:T(8,128)S(1)} %get-tuple-element.45.refs_0_.right.chosen_in.refs_3_.refs_4_.refs_2_.refs_5_), channel_id=1, source_target_pairs={{0,1},{1,0},{2,3},{3,2},{4,5},{5,4},{6,7},{7,6},{8,9},{9,8},{10,11... | collective-permute-start | bytes 233480 | tf_op jit(solution)/shard_map/ppermute | solution.py:487
  10.5 13.3 %collective-permute-start.1 = (f32[128,128]{1,0:T(8,128)S(1)}, f32[128,128]{1,0:T(8,128)S(1)}, u32[]{:S(2)}, u32[]{:S(2)}) collective-permute-start(f32[128,128]{1,0:T(8,128)S(1)} %get-tuple-element.50.refs_0_), channel_id=1, source_target_pairs={{1,2},{5,6},{9,10},{13,14},{17,18},{21,22},{25,26},{29,30}} | collective-permute-start | bytes 196616 | tf_op jit(solution)/shard_map/ppermute | solution.py:495
  11.2 12.7 %collective-permute-start.2 = (f32[128,128]{1,0:T(8,128)S(1)}, f32[128,128]{1,0:T(8,128)S(1)}, u32[]{:S(2)}, u32[]{:S(2)}) collective-permute-start(f32[128,128]{1,0:T(8,128)S(1)} %get-tuple-element.50.refs_0_), channel_id=1, source_target_pairs={{3,2},{7,6},{11,10},{15,14},{19,18},{23,22},{27,26},{31,30}} | collective-permute-start | bytes 196616 | tf_op jit(solution)/shard_map/ppermute | solution.py:495
  14.1 16.6 %collective-permute-start.7 = (f32[24,128]{1,0:T(8,128)S(1)}, f32[24,128]{1,0:T(8,128)S(1)}, u32[]{:S(2)}, u32[]{:S(2)}) collective-permute-start(f32[24,128]{1,0:T(8,128)S(1)} %get-tuple-element.64), channel_id=1, source_target_pairs={{1,2},{3,4},{5,6},{7,8},{9,10},{11,12},{13,14},{15,16},{17,18},{19... | collective-permute-start | bytes 36872 | tf_op jit(solution)/shard_map/ppermute | solution.py:501
  24.2 3.3 %collective-permute-start.3 = (f32[128,128]{1,0:T(8,128)S(1)}, f32[128,128]{1,0:T(8,128)S(1)}, u32[]{:S(2)}, u32[]{:S(2)}) collective-permute-start(f32[128,128]{1,0:T(8,128)S(1)} %get-tuple-element.55.refs_0_), channel_id=1, source_target_pairs={{2,4},{10,12},{18,20},{26,28}} | collective-permute-start | bytes 196616 | tf_op jit(solution)/shard_map/ppermute | solution.py:495
  24.9 2.7 %collective-permute-start.4 = (f32[128,128]{1,0:T(8,128)S(1)}, f32[128,128]{1,0:T(8,128)S(1)}, u32[]{:S(2)}, u32[]{:S(2)}) collective-permute-start(f32[128,128]{1,0:T(8,128)S(1)} %get-tuple-element.55.refs_0_), channel_id=1, source_target_pairs={{6,4},{14,12},{22,20},{30,28}} | collective-permute-start | bytes 196616 | tf_op jit(solution)/shard_map/ppermute | solution.py:495
  25.6 5.1 %copy-start = (s32[8,8]{1,0:T(8,128)S(1)}, s32[8,8]{1,0:T(8,128)}, u32[]{:S(2)}) copy-start(s32[8,8]{1,0:T(8,128)} %refs_4_.1) | copy-start | bytes 772
  27.9 7.1 %collective-permute-start.5 = (f32[128,128]{1,0:T(8,128)S(1)}, f32[128,128]{1,0:T(8,128)S(1)}, u32[]{:S(2)}, u32[]{:S(2)}) collective-permute-start(f32[128,128]{1,0:T(8,128)S(1)} %get-tuple-element.60.refs_0_), channel_id=1, source_target_pairs={{4,8},{20,24}} | collective-permute-start | bytes 196616 | tf_op jit(solution)/shard_map/ppermute | solution.py:495
  29.2 6.2 %collective-permute-start.6 = (f32[128,128]{1,0:T(8,128)S(1)}, f32[128,128]{1,0:T(8,128)S(1)}, u32[]{:S(2)}, u32[]{:S(2)}) collective-permute-start(f32[128,128]{1,0:T(8,128)S(1)} %get-tuple-element.60.refs_0_), channel_id=1, source_target_pairs={{12,8},{28,24}} | collective-permute-start | bytes 196616 | tf_op jit(solution)/shard_map/ppermute | solution.py:495
  35.7 5.9 %collective-permute-start.8 = (f32[128,128]{1,0:T(8,128)S(1)}, f32[128,128]{1,0:T(8,128)S(1)}, u32[]{:S(2)}, u32[]{:S(2)}) collective-permute-start(f32[128,128]{1,0:T(8,128)S(1)} %get-tuple-element.67.refs_0_), channel_id=1, source_target_pairs={{8,16},{24,0}} | collective-permute-start | bytes 196616 | tf_op jit(solution)/shard_map/ppermute | solution.py:495
  37.0 4.6 %collective-permute-start.9 = (f32[128,128]{1,0:T(8,128)S(1)}, f32[128,128]{1,0:T(8,128)S(1)}, u32[]{:S(2)}, u32[]{:S(2)}) collective-permute-start(f32[128,128]{1,0:T(8,128)S(1)} %get-tuple-element.67.refs_0_), channel_id=1, source_target_pairs={{24,16},{8,0}} | collective-permute-start | bytes 196616 | tf_op jit(solution)/shard_map/ppermute | solution.py:495

commit v7 on v6

--- a/solution.py
+++ b/solution.py
@@ -154,7 +154,7 @@
 
 def local_kernel(
     counts_in, coords_in, proxies_in, leaf_in, node_in,
-    basis_ref, gram_ref, heads_ref, message_ref, move_ref, columns_ref,
+    basis_ref, gram_ref, heads_ref, message_ref, move_ref, columns_ref, coords_ref,
     counts, coords, proxies, leaf_t, node_t, sems,
 ):
     pairs = ((counts_in, counts), (coords_in, coords), (proxies_in, proxies), (leaf_in, leaf_t), (node_in, node_t))
@@ -201,6 +201,7 @@
         weights = following
         level += 1
     message_ref[0:WIDTH, :] = weights[0]
+    coords_ref[...] = message_ref[WIDTH:, :]
 
 
 def lift_kernel(left, right, move, chosen_in, token, weight_ref, chosen_ref, *, level):
@@ -393,11 +394,11 @@
     coords_shape = shape((3 * leaves, WIDTH), f32)
     long = shape((WIDTH + 3 * leaves, WIDTH), f32)
 
-    basis, gram, heads, message, move, columns = pl.pallas_call(
+    basis, gram, heads, message, move, columns, coords_own = pl.pallas_call(
         local_kernel,
-        out_shape=(mats, flat, flat, long, mat, shape((leaves, 3, slots, WIDTH), f32)),
+        out_shape=(mats, flat, flat, long, mat, shape((leaves, 3, slots, WIDTH), f32), coords_shape),
         in_specs=[anywhere] * 5,
-        out_specs=(vmem,) * 6,
+        out_specs=(vmem,) * 7,
         scratch_shapes=[
             pltpu.SMEM(counts.shape, jnp.int32),
             pltpu.VMEM(coords.shape, f32),
@@ -452,9 +453,6 @@
             outs += [(kind, rows, vmem) for kind in ("leaf_r", "leaf_s", "node_r")]
             if steps[-1] + 1 < STEPS:
                 outs += [("leaf_out", flat, vmem), ("node_out", flat, vmem)]
-        if n == 1:
-            operands.append(("message", message, vmem))
-            outs.append(("coords_out", coords_shape, vmem))
         flush = state["flush"]
         near_extras(near, flush, True, operands, outs, scratch, aliases)
         if final:
@@ -479,7 +477,10 @@
         return made
 
     weight = chosen = message
-    made = pair = swapped = None
+    made = pair = None
+    others = [(i, i + 1) for i in range(1, count - 1, 2)]
+    others += [(target, source) for source, target in others]
+    swapped = lax.ppermute(coords_own, both, others)
     for level in range(levels):
         span = 2 ** (level + 1)
         quarter = span // 4
@@ -495,10 +496,6 @@
             left, right = lax.ppermute(weight, both, first), lax.ppermute(weight, both, second)
         if level < len(plan):
             made = work(level, weight)
-        if level == 1:
-            others = [(i, i + 1) for i in range(1, count - 1, 2)]
-            others += [(target, source) for source, target in others]
-            swapped = lax.ppermute(made["coords_out"], both, others)
         if level + 1 < levels:
             weight, chosen = pl.pallas_call(
                 functools.partial(lift_kernel, level=level),

time: 48.7 us -> 46.7 us (0.959)
  starting transfers between devices: 19.8 us -> 16.1 us
  waiting for transfers between devices: 1.95 us -> 3.7 us
    ppermute x1, starting transfers between devices: 9.72 us -> 6.02 us  [shards(): swapped = lax.ppermute(coords_own, both, others)]
    ppermute x4, waiting for transfers between devices: 1.58 us -> 3.69 us  [shards(): lax.ppermute(weight, both, first)]
  transfers between devices with their start and end apart: 10 -> 10, of which waited for: 2 -> 1; matrix products, arithmetic and copies ran while one was open for 0% -> 0% of each run, Pallas kernels for 28% -> 30%
where the time goes in v7:
time: 46.7 us; the launch traced here: 46.5 us
  Pallas kernels  25.6 us (55%)
  starting transfers between devices  16.1 us (34%)
  waiting for transfers between devices  3.7 us (8%)
  between operations  1.02 us (2%)
    pallas_call x6, Pallas kernels, call(): pl.pallas_call(functools.partial(body, names=names, **static), out_shape=...  19.4 us
    ppermute x1, starting transfers between devices, shards(): swapped = lax.ppermute(coords_own, both, others)  6.02 us
    pallas_call x1, Pallas kernels, shards(): pl.pallas_call(local_kernel, out_shape=(mats, flat, flat, long, mat, shap...  4.81 us
    ppermute x4, starting transfers between devices, shards(): lax.ppermute(weight, both, second)  4.1 us
    ppermute x4, starting transfers between devices, shards(): lax.ppermute(weight, both, first)  3.91 us
    ppermute x4, waiting for transfers between devices, shards(): lax.ppermute(weight, both, first)  3.69 us
    ppermute x1, starting transfers between devices, shards(): pair = lax.ppermute(weight, both, [(i, i ^ 1) for i in range(count)])  2.11 us
    pallas_call x4, Pallas kernels, shards(): pl.pallas_call(functools.partial(lift_kernel, level=level), out_shape=[ma...  1.39 us
  transfers between devices with their start and end apart: 10, of which 1 were waited for; matrix products, arithmetic and copies ran while one was open for 0% of the time, Pallas kernels for 30%

profile of v7, /device:TPU:1, one launch (start us, length us, event | category | flops | bytes accessed | tf_op | source)
XLA Modules:
  0.0 46.5 jit_solution(4152131779957699908)
XLA Ops:
  0.6 4.8 %local.1 = (f32[8,128,128]{2,1,0:T(8,128)S(1)}, f32[1024,128]{1,0:T(8,128)S(1)}, f32[1024,128]{1,0:T(8,128)S(1)}, f32[152,128]{1,0:T(8,128)S(1)}, f32[128,128]{1...) custom-call(s32[8]{0:T(128)} %counts_in.1, f32[3,1024]{1,0:T(4,128)} %coords_in.1, ...), custom_call_target="tpu_custom_call" | custom-call | flops 4000000000 | bytes 12000000 | tf_op jit(solution)/shard_map/local/pallas_call | solution.py:397
  5.4 2.1 %collective-permute-start = (f32[152,128]{1,0:T(8,128)S(1)}, f32[152,128]{1,0:T(8,128)S(1)}, u32[]{:S(2)}, u32[]{:S(2)}) collective-permute-start(f32[152,128]{1,0:T(8,128)S(1)} %get-tuple-element.45.refs_0_.right.chosen_in.refs_4_.refs_2_.refs_5_), channel_id=1, source_target_pairs={{0,1},{1,0},{2,3},{3,2},{4,5},{5,4},{6,7},{7,6},{8,9},{9,8},{10,11... | collective-permute-start | bytes 233480 | tf_op jit(solution)/shard_map/ppermute | solution.py:488
  7.6 6.0 %collective-permute-start.7 = (f32[24,128]{1,0:T(8,128)S(1)}, f32[24,128]{1,0:T(8,128)S(1)}, u32[]{:S(2)}, u32[]{:S(2)}) collective-permute-start(f32[24,128]{1,0:T(8,128)S(1)} %get-tuple-element.64), channel_id=1, source_target_pairs={{1,2},{3,4},{5,6},{7,8},{9,10},{11,12},{13,14},{15,16},{17,18},{19... | collective-permute-start | bytes 36872 | tf_op jit(solution)/shard_map/ppermute | solution.py:483
  13.6 2.6 %work0.1 = (f32[256,128]{1,0:T(8,128)S(1)}, f32[256,128]{1,0:T(8,128)S(1)}, f32[256,128]{1,0:T(8,128)S(1)}, f32[1024,128]{1,0:T(8,128)S(1)}, f32[1024,128]{1,0:T(8,128)S(1)}) custom-call(f32[152,128]{1,0:T(8,128)S(1)} %get-tuple-element.45.refs_0_.right.chosen_in.refs_4_.refs_2_.refs_5_, f32[1024,128]{1,0:T(8,128)S(1)} %get-tuple-element.47.refs_1_, ...), custom_call_target="tpu_custom_call" | custom-call | flops 3000000000 | bytes 9000000 | tf_op jit(solution)/shard_map/work0/pallas_call | solution.py:368
  16.2 0.4 lift0.1
  16.5 0.7 %collective-permute-start.1 = (f32[128,128]{1,0:T(8,128)S(1)}, f32[128,128]{1,0:T(8,128)S(1)}, u32[]{:S(2)}, u32[]{:S(2)}) collective-permute-start(f32[128,128]{1,0:T(8,128)S(1)} %get-tuple-element.50.refs_0_), channel_id=1, source_target_pairs={{1,2},{5,6},{9,10},{13,14},{17,18},{21,22},{25,26},{29,30}} | collective-permute-start | bytes 196616 | tf_op jit(solution)/shard_map/ppermute | solution.py:496
  17.2 0.7 %collective-permute-start.2 = (f32[128,128]{1,0:T(8,128)S(1)}, f32[128,128]{1,0:T(8,128)S(1)}, u32[]{:S(2)}, u32[]{:S(2)}) collective-permute-start(f32[128,128]{1,0:T(8,128)S(1)} %get-tuple-element.50.refs_0_), channel_id=1, source_target_pairs={{3,2},{7,6},{11,10},{15,14},{19,18},{23,22},{27,26},{31,30}} | collective-permute-start | bytes 196616 | tf_op jit(solution)/shard_map/ppermute | solution.py:496
  17.9 2.3 %work1.1 = (f32[256,128]{1,0:T(8,128)S(1)}, f32[256,128]{1,0:T(8,128)S(1)}, f32[256,128]{1,0:T(8,128)S(1)}, f32[1024,128]{1,0:T(8,128)S(1)}, f32[1024,128]{1,0:T(8,128)S(1)}) custom-call(f32[128,128]{1,0:T(8,128)S(1)} %get-tuple-element.50.refs_0_, f32[1024,128]{1,0:T(8,128)S(1)} %get-tuple-element.52.refs_1_, f32[1024,128]{1,0:T(8,128)S(1)} %get-tuple-element.53.refs_2_), custom_call_target="tpu_custom_call" | custom-call | flops 3000000000 | bytes 9000000 | tf_op jit(solution)/shard_map/work1/pallas_call | solution.py:368
  20.2 0.3 lift1.1
  20.5 0.7 %collective-permute-start.3 = (f32[128,128]{1,0:T(8,128)S(1)}, f32[128,128]{1,0:T(8,128)S(1)}, u32[]{:S(2)}, u32[]{:S(2)}) collective-permute-start(f32[128,128]{1,0:T(8,128)S(1)} %get-tuple-element.55.refs_0_), channel_id=1, source_target_pairs={{2,4},{10,12},{18,20},{26,28}} | collective-permute-start | bytes 196616 | tf_op jit(solution)/shard_map/ppermute | solution.py:496
  21.2 0.7 %collective-permute-start.4 = (f32[128,128]{1,0:T(8,128)S(1)}, f32[128,128]{1,0:T(8,128)S(1)}, u32[]{:S(2)}, u32[]{:S(2)}) collective-permute-start(f32[128,128]{1,0:T(8,128)S(1)} %get-tuple-element.55.refs_0_), channel_id=1, source_target_pairs={{6,4},{14,12},{22,20},{30,28}} | collective-permute-start | bytes 196616 | tf_op jit(solution)/shard_map/ppermute | solution.py:496
  21.9 0.0 copy-start
  21.9 1.9 %work2.1 = (f32[256,128]{1,0:T(8,128)S(1)}, f32[256,128]{1,0:T(8,128)S(1)}, f32[256,128]{1,0:T(8,128)S(1)}, f32[1024,128]{1,0:T(8,128)S(1)}, f32[1024,128]{1,0:T(8,128)S(1)}) custom-call(f32[128,128]{1,0:T(8,128)S(1)} %get-tuple-element.55.refs_0_, f32[1024,128]{1,0:T(8,128)S(1)} %get-tuple-element.57.refs_1_, f32[1024,128]{1,0:T(8,128)S(1)} %get-tuple-element.58.refs_2_), custom_call_target="tpu_custom_call" | custom-call | flops 3000000000 | bytes 9000000 | tf_op jit(solution)/shard_map/work2/pallas_call | solution.py:368
  23.8 0.0 collective-permute-done.3.left
  23.8 0.3 lift2.1
  24.2 1.3 %collective-permute-start.5 = (f32[128,128]{1,0:T(8,128)S(1)}, f32[128,128]{1,0:T(8,128)S(1)}, u32[]{:S(2)}, u32[]{:S(2)}) collective-permute-start(f32[128,128]{1,0:T(8,128)S(1)} %get-tuple-element.60.refs_0_), channel_id=1, source_target_pairs={{4,8},{20,24}} | collective-permute-start | bytes 196616 | tf_op jit(solution)/shard_map/ppermute | solution.py:496
  25.5 1.5 %collective-permute-start.6 = (f32[128,128]{1,0:T(8,128)S(1)}, f32[128,128]{1,0:T(8,128)S(1)}, u32[]{:S(2)}, u32[]{:S(2)}) collective-permute-start(f32[128,128]{1,0:T(8,128)S(1)} %get-tuple-element.60.refs_0_), channel_id=1, source_target_pairs={{12,8},{28,24}} | collective-permute-start | bytes 196616 | tf_op jit(solution)/shard_map/ppermute | solution.py:496
  27.0 2.7 %work3.1 = (f32[256,128]{1,0:T(8,128)S(1)}, f32[256,128]{1,0:T(8,128)S(1)}, f32[256,128]{1,0:T(8,128)S(1)}, bf16[3,8,128,128]{3,2,1,0:T(8,128)(2,1)S(1)}) custom-call(f32[128,128]{1,0:T(8,128)S(1)} %get-tuple-element.60.refs_0_, f32[1024,128]{1,0:T(8,128)S(1)} %get-tuple-element.62.refs_1_, f32[1024,128]{1,0:T(8,128)S(1)} %get-tuple-element.63.refs_2_, ...), custom_call_target="tpu_custom_call" | custom-call | flops 3000000000 | bytes 9000000 | tf_op jit(solution)/shard_map/work3/pallas_call | solution.py:368
  29.8 3.7 %collective-permute-done.5.left = f32[128,128]{1,0:T(8,128)S(1)} collective-permute-done((f32[128,128]{1,0:T(8,128)S(1)}, f32[128,128]{1,0:T(8,128)S(1)}, u32[]{:S(2)}, u32[]{:S(2)}) %collective-permute-start.5) | collective-permute-done | bytes 65568 | tf_op jit(solution)/shard_map/ppermute | solution.py:496
  33.4 0.3 lift3.1
  33.8 1.3 %collective-permute-start.8 = (f32[128,128]{1,0:T(8,128)S(1)}, f32[128,128]{1,0:T(8,128)S(1)}, u32[]{:S(2)}, u32[]{:S(2)}) collective-permute-start(f32[128,128]{1,0:T(8,128)S(1)} %get-tuple-element.67.refs_0_), channel_id=1, source_target_pairs={{8,16},{24,0}} | collective-permute-start | bytes 196616 | tf_op jit(solution)/shard_map/ppermute | solution.py:496
  35.1 1.3 %collective-permute-start.9 = (f32[128,128]{1,0:T(8,128)S(1)}, f32[128,128]{1,0:T(8,128)S(1)}, u32[]{:S(2)}, u32[]{:S(2)}) collective-permute-start(f32[128,128]{1,0:T(8,128)S(1)} %get-tuple-element.67.refs_0_), channel_id=1, source_target_pairs={{24,16},{8,0}} | collective-permute-start | bytes 196616 | tf_op jit(solution)/shard_map/ppermute | solution.py:496
  36.4 3.3 %work4.1 = (bf16[3,8,128,128]{3,2,1,0:T(8,128)(2,1)S(1)}, bf16[8,8,128,128]{3,2,1,0:T(8,128)(2,1)}, f32[8,128,128]{2,1,0:T(8,128)}, f32[8,128,128]{2,1,0:T(8,128)}, bf16[1024,128]{1,0:T(8,128)(2,1)}) custom-call(f32[128,128]{1,0:T(8,128)S(1)} %get-tuple-element.67.refs_0_, s32[8,8]{1,0:T(8,128)S(1)} %copy-done, ...), custom_call_target="tpu_custom_call" | custom-call | flops 3000000000 | bytes 9000000 | tf_op jit(solution)/shard_map/work4/pallas_call | solution.py:368
  39.7 6.6 %top.1 = (f32[8,128,128]{2,1,0:T(8,128)}, bf16[8,8,128,128]{3,2,1,0:T(8,128)(2,1)}) custom-call(f32[128,128]{1,0:T(8,128)S(1)} %collective-permute-done.8.refs_0_, f32[128,128]{1,0:T(8,128)S(1)} %collective-permute-done.9.refs_1_, f32[128,128]{1,0:T(8,128)S(1)} %get-tuple-element.68.refs_2_, ...), custom_call_target="tpu_custom_call", output_to_operand_aliasing={{0}: (3, {}), {1}: (10, {})} | custom-call | flops 6000000000 | bytes 18000000 | tf_op jit(solution)/shard_map/top/pallas_call | solution.py:368
  (9 shorter events, 0.0 us)
Async XLA Ops:
  5.4 10.7 %collective-permute-start = (f32[152,128]{1,0:T(8,128)S(1)}, f32[152,128]{1,0:T(8,128)S(1)}, u32[]{:S(2)}, u32[]{:S(2)}) collective-permute-start(f32[152,128]{1,0:T(8,128)S(1)} %get-tuple-element.45.refs_0_.right.chosen_in.refs_4_.refs_2_.refs_5_), channel_id=1, source_target_pairs={{0,1},{1,0},{2,3},{3,2},{4,5},{5,4},{6,7},{7,6},{8,9},{9,8},{10,11... | collective-permute-start | bytes 233480 | tf_op jit(solution)/shard_map/ppermute | solution.py:488
  7.6 19.4 %collective-permute-start.7 = (f32[24,128]{1,0:T(8,128)S(1)}, f32[24,128]{1,0:T(8,128)S(1)}, u32[]{:S(2)}, u32[]{:S(2)}) collective-permute-start(f32[24,128]{1,0:T(8,128)S(1)} %get-tuple-element.64), channel_id=1, source_target_pairs={{1,2},{3,4},{5,6},{7,8},{9,10},{11,12},{13,14},{15,16},{17,18},{19... | collective-permute-start | bytes 36872 | tf_op jit(solution)/shard_map/ppermute | solution.py:483
  16.5 3.6 %collective-permute-start.1 = (f32[128,128]{1,0:T(8,128)S(1)}, f32[128,128]{1,0:T(8,128)S(1)}, u32[]{:S(2)}, u32[]{:S(2)}) collective-permute-start(f32[128,128]{1,0:T(8,128)S(1)} %get-tuple-element.50.refs_0_), channel_id=1, source_target_pairs={{1,2},{5,6},{9,10},{13,14},{17,18},{21,22},{25,26},{29,30}} | collective-permute-start | bytes 196616 | tf_op jit(solution)/shard_map/ppermute | solution.py:496
  17.2 2.9 %collective-permute-start.2 = (f32[128,128]{1,0:T(8,128)S(1)}, f32[128,128]{1,0:T(8,128)S(1)}, u32[]{:S(2)}, u32[]{:S(2)}) collective-permute-start(f32[128,128]{1,0:T(8,128)S(1)} %get-tuple-element.50.refs_0_), channel_id=1, source_target_pairs={{3,2},{7,6},{11,10},{15,14},{19,18},{23,22},{27,26},{31,30}} | collective-permute-start | bytes 196616 | tf_op jit(solution)/shard_map/ppermute | solution.py:496
  20.5 3.3 %collective-permute-start.3 = (f32[128,128]{1,0:T(8,128)S(1)}, f32[128,128]{1,0:T(8,128)S(1)}, u32[]{:S(2)}, u32[]{:S(2)}) collective-permute-start(f32[128,128]{1,0:T(8,128)S(1)} %get-tuple-element.55.refs_0_), channel_id=1, source_target_pairs={{2,4},{10,12},{18,20},{26,28}} | collective-permute-start | bytes 196616 | tf_op jit(solution)/shard_map/ppermute | solution.py:496
  21.2 2.7 %collective-permute-start.4 = (f32[128,128]{1,0:T(8,128)S(1)}, f32[128,128]{1,0:T(8,128)S(1)}, u32[]{:S(2)}, u32[]{:S(2)}) collective-permute-start(f32[128,128]{1,0:T(8,128)S(1)} %get-tuple-element.55.refs_0_), channel_id=1, source_target_pairs={{6,4},{14,12},{22,20},{30,28}} | collective-permute-start | bytes 196616 | tf_op jit(solution)/shard_map/ppermute | solution.py:496
  21.9 5.1 %copy-start = (s32[8,8]{1,0:T(8,128)S(1)}, s32[8,8]{1,0:T(8,128)}, u32[]{:S(2)}) copy-start(s32[8,8]{1,0:T(8,128)} %refs_4_.1) | copy-start | bytes 772
  24.2 9.2 %collective-permute-start.5 = (f32[128,128]{1,0:T(8,128)S(1)}, f32[128,128]{1,0:T(8,128)S(1)}, u32[]{:S(2)}, u32[]{:S(2)}) collective-permute-start(f32[128,128]{1,0:T(8,128)S(1)} %get-tuple-element.60.refs_0_), channel_id=1, source_target_pairs={{4,8},{20,24}} | collective-permute-start | bytes 196616 | tf_op jit(solution)/shard_map/ppermute | solution.py:496
  25.5 7.9 %collective-permute-start.6 = (f32[128,128]{1,0:T(8,128)S(1)}, f32[128,128]{1,0:T(8,128)S(1)}, u32[]{:S(2)}, u32[]{:S(2)}) collective-permute-start(f32[128,128]{1,0:T(8,128)S(1)} %get-tuple-element.60.refs_0_), channel_id=1, source_target_pairs={{12,8},{28,24}} | collective-permute-start | bytes 196616 | tf_op jit(solution)/shard_map/ppermute | solution.py:496
  33.8 5.9 %collective-permute-start.8 = (f32[128,128]{1,0:T(8,128)S(1)}, f32[128,128]{1,0:T(8,128)S(1)}, u32[]{:S(2)}, u32[]{:S(2)}) collective-permute-start(f32[128,128]{1,0:T(8,128)S(1)} %get-tuple-element.67.refs_0_), channel_id=1, source_target_pairs={{8,16},{24,0}} | collective-permute-start | bytes 196616 | tf_op jit(solution)/shard_map/ppermute | solution.py:496
  35.1 4.6 %collective-permute-start.9 = (f32[128,128]{1,0:T(8,128)S(1)}, f32[128,128]{1,0:T(8,128)S(1)}, u32[]{:S(2)}, u32[]{:S(2)}) collective-permute-start(f32[128,128]{1,0:T(8,128)S(1)} %get-tuple-element.67.refs_0_), channel_id=1, source_target_pairs={{24,16},{8,0}} | collective-permute-start | bytes 196616 | tf_op jit(solution)/shard_map/ppermute | solution.py:496

commit v8 on v7

--- a/solution.py
+++ b/solution.py
@@ -413,10 +413,10 @@
     )(*(pltpu.with_memory_space_constraint(x, pltpu.HBM) for x in (counts, coords, proxies, leaf_transfers, node_transfers)))
 
     plan = [
-        ((0, 1, 2, 3), ()),
-        ((4, 5, 6, 7), ()),
-        ((8, 9, 10, 11), ()),
-        ((12, 13, 14, 15), (0, 1, 2)),
+        ((0, 1, 2, 3, 4), ()),
+        ((5, 6, 7), ()),
+        ((8, 9, 10), ()),
+        ((11, 12, 13, 14, 15), (0, 1, 2)),
         ((), (3, 4, 5)),
     ]
     parts = []

time: 46.7 us -> 47.3 us (1.013)
  waiting for transfers between devices: 3.7 us -> 4.18 us
    ppermute x4, waiting for transfers between devices: 3.69 us -> 4.17 us  [shards(): lax.ppermute(weight, both, first)]
where the time goes in v8:
time: 47.3 us; the launch traced here: 47 us
  Pallas kernels  25.7 us (54%)
  starting transfers between devices  16.1 us (34%)
  waiting for transfers between devices  4.18 us (9%)
  between operations  1.01 us (2%)
    pallas_call x6, Pallas kernels, call(): pl.pallas_call(functools.partial(body, names=names, **static), out_shape=...  19.5 us
    ppermute x1, starting transfers between devices, shards(): swapped = lax.ppermute(coords_own, both, others)  6.02 us
    pallas_call x1, Pallas kernels, shards(): pl.pallas_call(local_kernel, out_shape=(mats, flat, flat, long, mat, shap...  4.81 us
    ppermute x4, waiting for transfers between devices, shards(): lax.ppermute(weight, both, first)  4.17 us
    ppermute x4, starting transfers between devices, shards(): lax.ppermute(weight, both, second)  4.1 us
    ppermute x4, starting transfers between devices, shards(): lax.ppermute(weight, both, first)  3.91 us
    ppermute x1, starting transfers between devices, shards(): pair = lax.ppermute(weight, both, [(i, i ^ 1) for i in range(count)])  2.11 us
    pallas_call x4, Pallas kernels, shards(): pl.pallas_call(functools.partial(lift_kernel, level=level), out_shape=[ma...  1.39 us
  transfers between devices with their start and end apart: 10, of which 1 were waited for; matrix products, arithmetic and copies ran while one was open for 0% of the time, Pallas kernels for 30%

profile of v8, /device:TPU:1, one launch (start us, length us, event | category | flops | bytes accessed | tf_op | source)
XLA Modules:
  0.0 47.0 jit_solution(15884991617505820381)
XLA Ops:
  0.6 4.8 %local.1 = (f32[8,128,128]{2,1,0:T(8,128)S(1)}, f32[1024,128]{1,0:T(8,128)S(1)}, f32[1024,128]{1,0:T(8,128)S(1)}, f32[152,128]{1,0:T(8,128)S(1)}, f32[128,128]{1...) custom-call(s32[8]{0:T(128)} %counts_in.1, f32[3,1024]{1,0:T(4,128)} %coords_in.1, ...), custom_call_target="tpu_custom_call" | custom-call | flops 4000000000 | bytes 12000000 | tf_op jit(solution)/shard_map/local/pallas_call | solution.py:397
  5.4 2.1 %collective-permute-start = (f32[152,128]{1,0:T(8,128)S(1)}, f32[152,128]{1,0:T(8,128)S(1)}, u32[]{:S(2)}, u32[]{:S(2)}) collective-permute-start(f32[152,128]{1,0:T(8,128)S(1)} %get-tuple-element.45.refs_0_.right.chosen_in.refs_4_.refs_2_.refs_5_), channel_id=1, source_target_pairs={{0,1},{1,0},{2,3},{3,2},{4,5},{5,4},{6,7},{7,6},{8,9},{9,8},{10,11... | collective-permute-start | bytes 233480 | tf_op jit(solution)/shard_map/ppermute | solution.py:488
  7.6 6.0 %collective-permute-start.7 = (f32[24,128]{1,0:T(8,128)S(1)}, f32[24,128]{1,0:T(8,128)S(1)}, u32[]{:S(2)}, u32[]{:S(2)}) collective-permute-start(f32[24,128]{1,0:T(8,128)S(1)} %get-tuple-element.64), channel_id=1, source_target_pairs={{1,2},{3,4},{5,6},{7,8},{9,10},{11,12},{13,14},{15,16},{17,18},{19... | collective-permute-start | bytes 36872 | tf_op jit(solution)/shard_map/ppermute | solution.py:483
  13.6 3.1 %work0.1 = (f32[320,128]{1,0:T(8,128)S(1)}, f32[320,128]{1,0:T(8,128)S(1)}, f32[320,128]{1,0:T(8,128)S(1)}, f32[1024,128]{1,0:T(8,128)S(1)}, f32[1024,128]{1,0:T(8,128)S(1)}) custom-call(f32[152,128]{1,0:T(8,128)S(1)} %get-tuple-element.45.refs_0_.right.chosen_in.refs_4_.refs_2_.refs_5_, f32[1024,128]{1,0:T(8,128)S(1)} %get-tuple-element.47.refs_1_, ...), custom_call_target="tpu_custom_call" | custom-call | flops 3000000000 | bytes 9000000 | tf_op jit(solution)/shard_map/work0/pallas_call | solution.py:368
  16.7 0.0 collective-permute-done.left.refs_5_.refs_3_.refs_6_
  16.7 0.4 lift0.1
  17.1 0.7 %collective-permute-start.1 = (f32[128,128]{1,0:T(8,128)S(1)}, f32[128,128]{1,0:T(8,128)S(1)}, u32[]{:S(2)}, u32[]{:S(2)}) collective-permute-start(f32[128,128]{1,0:T(8,128)S(1)} %get-tuple-element.50.refs_0_), channel_id=1, source_target_pairs={{1,2},{5,6},{9,10},{13,14},{17,18},{21,22},{25,26},{29,30}} | collective-permute-start | bytes 196616 | tf_op jit(solution)/shard_map/ppermute | solution.py:496
  17.8 0.7 %collective-permute-start.2 = (f32[128,128]{1,0:T(8,128)S(1)}, f32[128,128]{1,0:T(8,128)S(1)}, u32[]{:S(2)}, u32[]{:S(2)}) collective-permute-start(f32[128,128]{1,0:T(8,128)S(1)} %get-tuple-element.50.refs_0_), channel_id=1, source_target_pairs={{3,2},{7,6},{11,10},{15,14},{19,18},{23,22},{27,26},{31,30}} | collective-permute-start | bytes 196616 | tf_op jit(solution)/shard_map/ppermute | solution.py:496
  18.4 1.7 %work1.1 = (f32[192,128]{1,0:T(8,128)S(1)}, f32[192,128]{1,0:T(8,128)S(1)}, f32[192,128]{1,0:T(8,128)S(1)}, f32[1024,128]{1,0:T(8,128)S(1)}, f32[1024,128]{1,0:T(8,128)S(1)}) custom-call(f32[128,128]{1,0:T(8,128)S(1)} %get-tuple-element.50.refs_0_, f32[1024,128]{1,0:T(8,128)S(1)} %get-tuple-element.52.refs_1_, f32[1024,128]{1,0:T(8,128)S(1)} %get-tuple-element.53.refs_2_), custom_call_target="tpu_custom_call" | custom-call | flops 3000000000 | bytes 9000000 | tf_op jit(solution)/shard_map/work1/pallas_call | solution.py:368
  20.2 0.3 lift1.1
  20.5 0.7 %collective-permute-start.3 = (f32[128,128]{1,0:T(8,128)S(1)}, f32[128,128]{1,0:T(8,128)S(1)}, u32[]{:S(2)}, u32[]{:S(2)}) collective-permute-start(f32[128,128]{1,0:T(8,128)S(1)} %get-tuple-element.55.refs_0_), channel_id=1, source_target_pairs={{2,4},{10,12},{18,20},{26,28}} | collective-permute-start | bytes 196616 | tf_op jit(solution)/shard_map/ppermute | solution.py:496
  21.2 0.7 %collective-permute-start.4 = (f32[128,128]{1,0:T(8,128)S(1)}, f32[128,128]{1,0:T(8,128)S(1)}, u32[]{:S(2)}, u32[]{:S(2)}) collective-permute-start(f32[128,128]{1,0:T(8,128)S(1)} %get-tuple-element.55.refs_0_), channel_id=1, source_target_pairs={{6,4},{14,12},{22,20},{30,28}} | collective-permute-start | bytes 196616 | tf_op jit(solution)/shard_map/ppermute | solution.py:496
  21.9 0.0 copy-start
  21.9 1.5 %work2.1 = (f32[192,128]{1,0:T(8,128)S(1)}, f32[192,128]{1,0:T(8,128)S(1)}, f32[192,128]{1,0:T(8,128)S(1)}, f32[1024,128]{1,0:T(8,128)S(1)}, f32[1024,128]{1,0:T(8,128)S(1)}) custom-call(f32[128,128]{1,0:T(8,128)S(1)} %get-tuple-element.55.refs_0_, f32[1024,128]{1,0:T(8,128)S(1)} %get-tuple-element.57.refs_1_, f32[1024,128]{1,0:T(8,128)S(1)} %get-tuple-element.58.refs_2_), custom_call_target="tpu_custom_call" | custom-call | flops 3000000000 | bytes 9000000 | tf_op jit(solution)/shard_map/work2/pallas_call | solution.py:368
  23.4 0.3 lift2.1
  23.8 1.3 %collective-permute-start.5 = (f32[128,128]{1,0:T(8,128)S(1)}, f32[128,128]{1,0:T(8,128)S(1)}, u32[]{:S(2)}, u32[]{:S(2)}) collective-permute-start(f32[128,128]{1,0:T(8,128)S(1)} %get-tuple-element.60.refs_0_), channel_id=1, source_target_pairs={{4,8},{20,24}} | collective-permute-start | bytes 196616 | tf_op jit(solution)/shard_map/ppermute | solution.py:496
  25.1 1.5 %collective-permute-start.6 = (f32[128,128]{1,0:T(8,128)S(1)}, f32[128,128]{1,0:T(8,128)S(1)}, u32[]{:S(2)}, u32[]{:S(2)}) collective-permute-start(f32[128,128]{1,0:T(8,128)S(1)} %get-tuple-element.60.refs_0_), channel_id=1, source_target_pairs={{12,8},{28,24}} | collective-permute-start | bytes 196616 | tf_op jit(solution)/shard_map/ppermute | solution.py:496
  26.6 3.2 %work3.1 = (f32[320,128]{1,0:T(8,128)S(1)}, f32[320,128]{1,0:T(8,128)S(1)}, f32[320,128]{1,0:T(8,128)S(1)}, bf16[3,8,128,128]{3,2,1,0:T(8,128)(2,1)S(1)}) custom-call(f32[128,128]{1,0:T(8,128)S(1)} %get-tuple-element.60.refs_0_, f32[1024,128]{1,0:T(8,128)S(1)} %get-tuple-element.62.refs_1_, f32[1024,128]{1,0:T(8,128)S(1)} %get-tuple-element.63.refs_2_, ...), custom_call_target="tpu_custom_call" | custom-call | flops 3000000000 | bytes 9000000 | tf_op jit(solution)/shard_map/work3/pallas_call | solution.py:368
  29.8 4.2 %collective-permute-done.5.left = f32[128,128]{1,0:T(8,128)S(1)} collective-permute-done((f32[128,128]{1,0:T(8,128)S(1)}, f32[128,128]{1,0:T(8,128)S(1)}, u32[]{:S(2)}, u32[]{:S(2)}) %collective-permute-start.5) | collective-permute-done | bytes 65568 | tf_op jit(solution)/shard_map/ppermute | solution.py:496
  34.0 0.3 lift3.1
  34.3 1.3 %collective-permute-start.8 = (f32[128,128]{1,0:T(8,128)S(1)}, f32[128,128]{1,0:T(8,128)S(1)}, u32[]{:S(2)}, u32[]{:S(2)}) collective-permute-start(f32[128,128]{1,0:T(8,128)S(1)} %get-tuple-element.67.refs_0_), channel_id=1, source_target_pairs={{8,16},{24,0}} | collective-permute-start | bytes 196616 | tf_op jit(solution)/shard_map/ppermute | solution.py:496
  35.6 1.3 %collective-permute-start.9 = (f32[128,128]{1,0:T(8,128)S(1)}, f32[128,128]{1,0:T(8,128)S(1)}, u32[]{:S(2)}, u32[]{:S(2)}) collective-permute-start(f32[128,128]{1,0:T(8,128)S(1)} %get-tuple-element.67.refs_0_), channel_id=1, source_target_pairs={{24,16},{8,0}} | collective-permute-start | bytes 196616 | tf_op jit(solution)/shard_map/ppermute | solution.py:496
  36.9 3.3 %work4.1 = (bf16[3,8,128,128]{3,2,1,0:T(8,128)(2,1)S(1)}, bf16[8,8,128,128]{3,2,1,0:T(8,128)(2,1)}, f32[8,128,128]{2,1,0:T(8,128)}, f32[8,128,128]{2,1,0:T(8,128)}, bf16[1024,128]{1,0:T(8,128)(2,1)}) custom-call(f32[128,128]{1,0:T(8,128)S(1)} %get-tuple-element.67.refs_0_, s32[8,8]{1,0:T(8,128)S(1)} %copy-done, ...), custom_call_target="tpu_custom_call" | custom-call | flops 3000000000 | bytes 9000000 | tf_op jit(solution)/shard_map/work4/pallas_call | solution.py:368
  40.3 6.6 %top.1 = (f32[8,128,128]{2,1,0:T(8,128)}, bf16[8,8,128,128]{3,2,1,0:T(8,128)(2,1)}) custom-call(f32[128,128]{1,0:T(8,128)S(1)} %collective-permute-done.8.refs_0_, f32[128,128]{1,0:T(8,128)S(1)} %collective-permute-done.9.refs_1_, f32[128,128]{1,0:T(8,128)S(1)} %get-tuple-element.68.refs_2_, ...), custom_call_target="tpu_custom_call", output_to_operand_aliasing={{0}: (3, {}), {1}: (10, {})} | custom-call | flops 6000000000 | bytes 18000000 | tf_op jit(solution)/shard_map/top/pallas_call | solution.py:368
  (9 shorter events, 0.0 us)
Async XLA Ops:
  5.4 11.3 %collective-permute-start = (f32[152,128]{1,0:T(8,128)S(1)}, f32[152,128]{1,0:T(8,128)S(1)}, u32[]{:S(2)}, u32[]{:S(2)}) collective-permute-start(f32[152,128]{1,0:T(8,128)S(1)} %get-tuple-element.45.refs_0_.right.chosen_in.refs_4_.refs_2_.refs_5_), channel_id=1, source_target_pairs={{0,1},{1,0},{2,3},{3,2},{4,5},{5,4},{6,7},{7,6},{8,9},{9,8},{10,11... | collective-permute-start | bytes 233480 | tf_op jit(solution)/shard_map/ppermute | solution.py:488
  7.6 19.0 %collective-permute-start.7 = (f32[24,128]{1,0:T(8,128)S(1)}, f32[24,128]{1,0:T(8,128)S(1)}, u32[]{:S(2)}, u32[]{:S(2)}) collective-permute-start(f32[24,128]{1,0:T(8,128)S(1)} %get-tuple-element.64), channel_id=1, source_target_pairs={{1,2},{3,4},{5,6},{7,8},{9,10},{11,12},{13,14},{15,16},{17,18},{19... | collective-permute-start | bytes 36872 | tf_op jit(solution)/shard_map/ppermute | solution.py:483
  17.1 3.1 %collective-permute-start.1 = (f32[128,128]{1,0:T(8,128)S(1)}, f32[128,128]{1,0:T(8,128)S(1)}, u32[]{:S(2)}, u32[]{:S(2)}) collective-permute-start(f32[128,128]{1,0:T(8,128)S(1)} %get-tuple-element.50.refs_0_), channel_id=1, source_target_pairs={{1,2},{5,6},{9,10},{13,14},{17,18},{21,22},{25,26},{29,30}} | collective-permute-start | bytes 196616 | tf_op jit(solution)/shard_map/ppermute | solution.py:496
  17.8 2.4 %collective-permute-start.2 = (f32[128,128]{1,0:T(8,128)S(1)}, f32[128,128]{1,0:T(8,128)S(1)}, u32[]{:S(2)}, u32[]{:S(2)}) collective-permute-start(f32[128,128]{1,0:T(8,128)S(1)} %get-tuple-element.50.refs_0_), channel_id=1, source_target_pairs={{3,2},{7,6},{11,10},{15,14},{19,18},{23,22},{27,26},{31,30}} | collective-permute-start | bytes 196616 | tf_op jit(solution)/shard_map/ppermute | solution.py:496
  20.5 2.9 %collective-permute-start.3 = (f32[128,128]{1,0:T(8,128)S(1)}, f32[128,128]{1,0:T(8,128)S(1)}, u32[]{:S(2)}, u32[]{:S(2)}) collective-permute-start(f32[128,128]{1,0:T(8,128)S(1)} %get-tuple-element.55.refs_0_), channel_id=1, source_target_pairs={{2,4},{10,12},{18,20},{26,28}} | collective-permute-start | bytes 196616 | tf_op jit(solution)/shard_map/ppermute | solution.py:496
  21.2 2.2 %collective-permute-start.4 = (f32[128,128]{1,0:T(8,128)S(1)}, f32[128,128]{1,0:T(8,128)S(1)}, u32[]{:S(2)}, u32[]{:S(2)}) collective-permute-start(f32[128,128]{1,0:T(8,128)S(1)} %get-tuple-element.55.refs_0_), channel_id=1, source_target_pairs={{6,4},{14,12},{22,20},{30,28}} | collective-permute-start | bytes 196616 | tf_op jit(solution)/shard_map/ppermute | solution.py:496
  21.9 4.7 %copy-start = (s32[8,8]{1,0:T(8,128)S(1)}, s32[8,8]{1,0:T(8,128)}, u32[]{:S(2)}) copy-start(s32[8,8]{1,0:T(8,128)} %refs_4_.1) | copy-start | bytes 772
  23.8 10.2 %collective-permute-start.5 = (f32[128,128]{1,0:T(8,128)S(1)}, f32[128,128]{1,0:T(8,128)S(1)}, u32[]{:S(2)}, u32[]{:S(2)}) collective-permute-start(f32[128,128]{1,0:T(8,128)S(1)} %get-tuple-element.60.refs_0_), channel_id=1, source_target_pairs={{4,8},{20,24}} | collective-permute-start | bytes 196616 | tf_op jit(solution)/shard_map/ppermute | solution.py:496
  25.1 8.9 %collective-permute-start.6 = (f32[128,128]{1,0:T(8,128)S(1)}, f32[128,128]{1,0:T(8,128)S(1)}, u32[]{:S(2)}, u32[]{:S(2)}) collective-permute-start(f32[128,128]{1,0:T(8,128)S(1)} %get-tuple-element.60.refs_0_), channel_id=1, source_target_pairs={{12,8},{28,24}} | collective-permute-start | bytes 196616 | tf_op jit(solution)/shard_map/ppermute | solution.py:496
  34.3 5.9 %collective-permute-start.8 = (f32[128,128]{1,0:T(8,128)S(1)}, f32[128,128]{1,0:T(8,128)S(1)}, u32[]{:S(2)}, u32[]{:S(2)}) collective-permute-start(f32[128,128]{1,0:T(8,128)S(1)} %get-tuple-element.67.refs_0_), channel_id=1, source_target_pairs={{8,16},{24,0}} | collective-permute-start | bytes 196616 | tf_op jit(solution)/shard_map/ppermute | solution.py:496
  35.6 4.6 %collective-permute-start.9 = (f32[128,128]{1,0:T(8,128)S(1)}, f32[128,128]{1,0:T(8,128)S(1)}, u32[]{:S(2)}, u32[]{:S(2)}) collective-permute-start(f32[128,128]{1,0:T(8,128)S(1)} %get-tuple-element.67.refs_0_), channel_id=1, source_target_pairs={{24,16},{8,0}} | collective-permute-start | bytes 196616 | tf_op jit(solution)/shard_map/ppermute | solution.py:496
